TPU v7x, 128 devices: a whole 4x4x4 slice. The times are simulated.
128 devices in a mesh: pos: 4 (over x), depth: 32 (over z, y, core).
Axes of the slice: x: 4, y: 4, z: 4, core: 2. Of those that a mesh axis runs over, the one named last changes fastest.
Arguments:
- object_field: float32 [64, 2, 512, 512], P('depth', None, 'pos'), may hold values from -1.25 to 1.25, as said below
- offsets: int32 [8, 2], P('pos'), may hold values from 0 to 511, as said below
- probe: float32 [2, 128, 128], replicated, may hold values from -4.2 to 4.2
- intensity: float32 [8, 128, 128], P('pos'), may hold values from 0 to 2
Outputs:
- object_grad: float32 [64, 2, 512, 512], P('depth', None, 'pos')
Inputs may be any that keep to these rules, and one draw needn't show every extreme that they name: `offsets`: the row of position p lies in rows p // 2 * 128 up to that plus 128 - 1; its column is at most 384. Position 0 has row 0 and column 384; the last position has row 511. `object_field`: each pixel's transmission has magnitude between 0.75 and 1.25.
All inputs are finite; a program needn't handle non-finite values.
Results may differ from a plain program's by a relative error of at most 0.0003.
Values sent between devices are 32-bit elements; how exact they have to be, the bound alone decides.
No kernel may reach another device: no remote copies, remote signals or barrier semaphores. Data moves between devices by JAX's collectives and lax.ppermute only.
A program may use at most 64 MiB of HBM per device.

v0:
```python
import math

import jax
import jax.numpy as jnp
from jax import lax
from jax.sharding import PartitionSpec as P


def shifted(value, axis, steps):
    count = lax.axis_size(axis)
    pairs = [(source, (source + steps) % count) for source in range(count)]
    return lax.ppermute(value, axis, pairs)


def from_behind(block, axis, distance):
    devices = range(lax.axis_size(axis))
    route = [(i - distance, i) for i in devices if i - distance in devices]
    return lax.ppermute(block, axis, route)


def dft_tables(window, conjugate):
    indices = jnp.arange(window, dtype=jnp.int32)
    product = indices[:, None] * indices[None, :] % window
    angles = product.astype(jnp.float32) * (2.0 * math.pi / window)
    scaling = 1.0 / math.sqrt(window)
    sign_value = 1.0 if conjugate else -1.0
    real_part = jnp.cos(angles) * scaling
    imag_part = sign_value * jnp.sin(angles) * scaling
    right_table = jnp.stack(
        [jnp.stack([real_part, imag_part], 1), jnp.stack([-imag_part, real_part], 1)], 0
    )
    left_table = jnp.stack(
        [jnp.stack([real_part, -imag_part], 0), jnp.stack([imag_part, real_part], 0)], 0
    )
    return (right_table, left_table)


def make_tables(window):
    right_fwd, left_fwd = dft_tables(window, False)
    right_inv, left_inv = dft_tables(window, True)
    indices = jnp.arange(window, dtype=jnp.int32)
    centred = (indices + window // 2) % window - window // 2
    squares = centred[:, None] * centred[:, None] + centred[None, :] * centred[None, :]
    phase = squares.astype(jnp.float32) * (math.pi / window)
    return (right_fwd, left_fwd, right_inv, left_inv, jnp.cos(phase), jnp.sin(phase))


def right_product(field, table):
    return jnp.einsum("pcik,ckdj->pdij", field, table, precision=lax.Precision.HIGHEST)


def left_product(table, field):
    return jnp.einsum("dcik,pckj->pdij", table, field, precision=lax.Precision.HIGHEST)


def complex_times(first_re, first_im, second_re, second_im):
    return (
        first_re * second_re - first_im * second_im,
        first_re * second_im + first_im * second_re,
    )


def conj_times(first_re, first_im, second_re, second_im):
    return (
        first_re * second_re + first_im * second_im,
        first_im * second_re - first_re * second_im,
    )


def as_wave(real_part, imag_part):
    return jnp.stack([real_part, imag_part], 1)


def propagate(field_in, windows, tables):
    right_fwd, left_fwd, right_inv, left_inv, phase_cos, phase_sin = tables
    mixed = as_wave(*complex_times(field_in[:, 0], field_in[:, 1], windows[:, 0], windows[:, 1]))
    across = right_product(mixed, right_fwd)
    spectrum = left_product(left_fwd, across)
    phased = as_wave(*conj_times(spectrum[:, 0], spectrum[:, 1], phase_cos, phase_sin))
    turned = right_product(phased, right_inv)
    return left_product(left_inv, turned)


def adjoint(field_in, windows, grad_out, tables):
    right_fwd, left_fwd, right_inv, left_inv, phase_cos, phase_sin = tables
    grad_last = left_product(left_fwd, grad_out)
    grad_spec = right_product(grad_last, right_fwd)
    grad_phased = as_wave(*complex_times(grad_spec[:, 0], grad_spec[:, 1], phase_cos, phase_sin))
    grad_across = left_product(left_inv, grad_phased)
    grad_mixed = right_product(grad_across, right_inv)
    grad_windows = jnp.stack(
        conj_times(grad_mixed[:, 0], grad_mixed[:, 1], field_in[:, 0], field_in[:, 1]), 1
    )
    grad_field = as_wave(
        *conj_times(grad_mixed[:, 0], grad_mixed[:, 1], windows[:, 0], windows[:, 1])
    )
    return (grad_field, grad_windows)


def far_field(exit_wave, measured, tables):
    right_fwd, left_fwd, right_inv, left_inv, phase_cos, phase_sin = tables
    across = right_product(exit_wave, right_fwd)
    spectrum = left_product(left_fwd, across)
    power = spectrum[:, 0] * spectrum[:, 0] + spectrum[:, 1] * spectrum[:, 1]
    misfit = power - measured
    weighted = as_wave(misfit * spectrum[:, 0], misfit * spectrum[:, 1])
    grad_across = left_product(left_inv, weighted)
    return right_product(grad_across, right_inv)


def group_forward(field_in, windows, tables):
    entries = []
    for layer_num in range(windows.shape[1]):
        entries.append(field_in)
        field_in = propagate(field_in, windows[:, layer_num], tables)
    return (field_in, entries)


def group_backward(field_in, windows, grad_field, tables):
    unused, entries = group_forward(field_in, windows, tables)
    gradients = [None] * windows.shape[1]
    for layer_num in reversed(range(windows.shape[1])):
        grad_field, gradients[layer_num] = adjoint(
            entries[layer_num], windows[:, layer_num], grad_field, tables
        )
    return (grad_field, jnp.stack(gradients, axis=1))


def body(object_field, offsets, probe, intensity):
    slices_here, components, strip_rows, width_cols = object_field.shape
    window = probe.shape[-1]
    pos_count = offsets.shape[0]
    tables = make_tables(window)
    row_here = offsets[:, 0] % strip_rows
    col_here = offsets[:, 1]
    following = shifted(object_field, "pos", -1)
    extended = jnp.concatenate([object_field, following], axis=2)

    def single_window(row_at, col_at):
        return lax.dynamic_slice(
            extended, (0, 0, row_at, col_at), (slices_here, components, window, window)
        )

    patches = jax.vmap(single_window)(row_here, col_here)
    group_size = 1
    groups = pos_count // group_size
    depth_count = lax.axis_size("depth")
    depth_here = lax.axis_index("depth")
    sections = depth_count + groups - 1
    incident = probe[None]
    wave_shape = (group_size, components, window, window)

    def forward_section(section_num, state_in):
        saved, exits, arrived = state_in
        batch_num = section_num - depth_here
        active = (batch_num >= 0) & (batch_num < groups)
        slot_index = jnp.clip(batch_num, 0, groups - 1)
        entering = jnp.where(depth_here == 0, incident, arrived)
        windows_now = lax.dynamic_slice_in_dim(patches, slot_index * group_size, group_size, 0)
        leaving, unused = group_forward(entering, windows_now, tables)
        saved = jnp.where(
            active, lax.dynamic_update_slice_in_dim(saved, entering[None], slot_index, 0), saved
        )
        finished = active & (depth_here == depth_count - 1)
        exits = jnp.where(
            finished, lax.dynamic_update_slice_in_dim(exits, leaving[None], slot_index, 0), exits
        )
        arrived = from_behind(leaving, "depth", 1)
        return (saved, exits, arrived)

    empty_waves = jnp.zeros((groups,) + wave_shape, jnp.float32)
    saved, exits, unused = lax.fori_loop(
        0, sections, forward_section, (empty_waves, empty_waves, jnp.zeros(wave_shape, jnp.float32))
    )
    grad_exit = far_field(exits.reshape((pos_count, components, window, window)), intensity, tables)
    grad_exit = grad_exit.reshape((groups,) + wave_shape)

    def backward_section(section_num, state_in):
        collected, arrived = state_in
        batch_num = section_num - (depth_count - 1 - depth_here)
        active = (batch_num >= 0) & (batch_num < groups)
        slot_index = jnp.clip(batch_num, 0, groups - 1)
        entering = jnp.where(depth_here == depth_count - 1, grad_exit[slot_index], arrived)
        windows_now = lax.dynamic_slice_in_dim(patches, slot_index * group_size, group_size, 0)
        grad_prev, grad_windows = group_backward(saved[slot_index], windows_now, entering, tables)
        updated = lax.dynamic_update_slice_in_dim(
            collected, grad_windows, slot_index * group_size, 0
        )
        collected = jnp.where(active, updated, collected)
        arrived = from_behind(grad_prev, "depth", -1)
        return (collected, arrived)

    collected, unused = lax.fori_loop(
        0,
        sections,
        backward_section,
        (jnp.zeros(patches.shape, jnp.float32), jnp.zeros(wave_shape, jnp.float32)),
    )
    target = jnp.zeros((slices_here, components, 2 * strip_rows, width_cols), jnp.float32)
    for position in range(collected.shape[0]):
        start_at = (0, 0, row_here[position], col_here[position])
        current = lax.dynamic_slice(target, start_at, (slices_here, components, window, window))
        target = lax.dynamic_update_slice(target, current + collected[position], start_at)
    returned = shifted(target[:, :, strip_rows:], "pos", 1)
    result = target[:, :, :strip_rows] + returned
    return result


def solution(mesh):
    return jax.shard_map(
        body,
        mesh=mesh,
        in_specs=(P("depth", None, "pos", None), P("pos", None), P(), P("pos", None, None)),
        out_specs=P("depth", None, "pos", None),
        check_vma=False,
    )
```

profile of v0, /device:TPU:57, one launch (start us, length us, event | category | flops | bytes accessed | tf_op | source)
XLA Modules:
  0.0 938.6 jit_solution(884844790691231928)
XLA Ops:
  16.6 8.0 collective-permute-done.2
  33.9 405.2 %while.43 = (s32[]{:T(128)}, f32[2,1,2,128,128]{4,3,2,1,0:T(8,128)S(1)}, f32[2,1,2,128,128]{3,4,2,1,0:T(8,128)S(1)}, f32[1,2,128,128]{2,3,1,0:T(8,128)S(1)}, s32...) while((s32[]{:T(128)}, ...), condition=%wide.region_1.2_spmd.clone.clone.clone, body=%wide.region_0.1_spmd.clone.clone.clone.sunk | while | flops 806027264 | bytes 7735592 | solution.py:172
  48.3 6.5 collective-permute-start
  60.7 6.5 collective-permute-start
  73.0 6.5 collective-permute-start
  85.3 6.5 collective-permute-start
  97.7 6.5 collective-permute-start
  122.3 6.5 collective-permute-start
  134.7 6.5 collective-permute-start
  147.0 6.5 collective-permute-start
  171.7 6.5 collective-permute-start
  184.0 6.5 collective-permute-start
  196.3 6.5 collective-permute-start
  208.7 6.5 collective-permute-start
  221.0 6.5 collective-permute-start
  233.4 6.5 collective-permute-start
  245.7 6.5 collective-permute-start
  270.4 6.5 collective-permute-start
  282.7 6.5 collective-permute-start
  295.0 6.5 collective-permute-start
  319.7 6.5 collective-permute-start
  332.0 6.5 collective-permute-start
  344.4 6.5 collective-permute-start
  356.7 6.5 collective-permute-start
  369.0 6.5 collective-permute-start
  381.4 6.5 collective-permute-start
  393.7 6.5 collective-permute-start
  418.4 6.5 collective-permute-start
  430.7 6.5 collective-permute-start
  441.8 461.1 %while.44 = (s32[]{:T(128)}, f32[2,2,2,128,128]{4,3,2,1,0:T(8,128)S(1)}, f32[1,2,128,128]{3,2,1,0:T(8,128)S(1)}, s32[]{:T(128)}, pred[]{:T(512)}, /*index=5*/f32...) while((s32[]{:T(128)}, ...), condition=%wide.region_3.4_spmd.clone.clone.clone, body=%wide.region_2.3_spmd.clone.clone.clone.sunk | while | flops 1209270272 | bytes 12323100 | solution.py:193
  449.4 7.1 collective-permute-done.1
  916.9 20.5 %collective-permute-done.3 = f32[2,2,128,512]{3,2,1,0:T(8,128)S(1)} collective-permute-done((f32[2,2,128,512]{3,2,1,0:T(8,128)S(1)}, f32[2,2,128,512]{3,2,1,0:T(8,128)S(1)}, u32[]{:S(2)}, u32[]{:S(2)}) %collective-permute-start.3) | collective-permute-done | bytes 1048608 | tf_op jit(solution)/shard_map/ppermute | solution.py:12
  (1451 shorter events, 715.6 us)
Async XLA Ops:
  0.0 24.6 %collective-permute-start.2 = (f32[2,2,128,512]{3,2,1,0:T(8,128)}, f32[2,2,128,512]{3,2,1,0:T(8,128)}, u32[]{:S(2)}, u32[]{:S(2)}) collective-permute-start(f32[2,2,128,512]{3,2,1,0:T(8,128)} %param.8), channel_id=1, source_target_pairs={{0,96},{32,0},{64,32},{96,64},{1,97},{33,1},{65,33},{97,65},{2,98}... | collective-permute-start | bytes 3145736 | tf_op jit(solution)/shard_map/ppermute | solution.py:12
  48.3 8.4 collective-permute-start
  73.0 8.4 collective-permute-start
  97.7 8.4 collective-permute-start
  122.3 8.4 collective-permute-start
  147.0 8.4 collective-permute-start
  171.7 8.4 collective-permute-start
  196.3 8.4 collective-permute-start
  221.0 8.4 collective-permute-start
  245.7 8.4 collective-permute-start
  270.4 8.4 collective-permute-start
  295.0 8.4 collective-permute-start
  319.7 8.4 collective-permute-start
  344.4 8.4 collective-permute-start
  369.0 8.4 collective-permute-start
  393.7 8.4 collective-permute-start
  418.4 8.4 collective-permute-start
  447.3 9.1 collective-permute-start.1
  462.0 8.4 collective-permute-start.1
  476.0 8.4 collective-permute-start.1
  489.9 8.4 collective-permute-start.1
  503.9 8.4 collective-permute-start.1
  517.8 8.4 collective-permute-start.1
  545.7 8.4 collective-permute-start.1
  559.6 8.4 collective-permute-start.1
  573.6 8.4 collective-permute-start.1
  587.5 8.4 collective-permute-start.1
  615.4 8.4 collective-permute-start.1
  629.4 8.4 collective-permute-start.1
  643.3 8.4 collective-permute-start.1
  657.3 8.4 collective-permute-start.1
  914.2 23.2 %collective-permute-start.3 = (f32[2,2,128,512]{3,2,1,0:T(8,128)S(1)}, f32[2,2,128,512]{3,2,1,0:T(8,128)S(1)}, u32[]{:S(2)}, u32[]{:S(2)}) collective-permute-start(f32[2,2,128,512]{3,2,1,0:T(8,128)S(1)} %slice.511), channel_id=1, source_target_pairs={{0,32},{32,64},{64,96},{96,0},{1,33},{33,65},{65,97},{97,1},{2,34}... | collective-permute-start | bytes 3145736 | tf_op jit(solution)/shard_map/ppermute | solution.py:12
  (40 other events, 361.6 us)
where the time goes:
time: 941 us; the launch traced here: 939 us
  waiting for transfers between devices  303 us (32%)
  starting transfers between devices  280 us (30%)
  matrix products  248 us (26%)
  other arithmetic  60.6 us (6%)
  local copies, waits for them, and re-layouts  28.1 us (3%)
  loops' own time  11.4 us (1%)
    ppermute x66, starting transfers between devices, from_behind(): return lax.ppermute(block, axis, route)  275 us
    ppermute x66, waiting for transfers between devices, from_behind(): return lax.ppermute(block, axis, route)  274 us
    dot_general x332, matrix products, left_product(): jnp.einsum('dcik,pckj->pdij', table, field, precision=lax.Precision.HIGHEST)  132 us
    dot_general x332, matrix products, right_product(): jnp.einsum('pcik,ckdj->pdij', field, table, precision=lax.Precision.HIGHEST)  116 us
    ppermute x2, waiting for transfers between devices, shifted(): return lax.ppermute(value, axis, pairs)  28.5 us
    sub x165, other arithmetic, complex_times(): first_re * second_re - first_im * second_im  23.8 us
    add x132, other arithmetic, conj_times(): first_re * second_re + first_im * second_im  23.7 us
  transfers between devices with their start and end apart: 68, of which 68 were waited for; matrix products, arithmetic and copies ran while one was open for 1% of the time, Pallas kernels for 0%

commit v1 on v0

v1 whole, which is shorter than its diff:
```python
import math

import jax
import jax.numpy as jnp
import ml_dtypes
import numpy as np
from jax import lax
from jax.experimental import pallas as pl
from jax.experimental.pallas import tpu as pltpu
from jax.sharding import PartitionSpec as P

N = 128
CORES = 2
RING = 4
STAGES = 4
PER_DEVICE = 2
PER_CHIP = CORES * PER_DEVICE
PER_STAGE = RING * PER_CHIP
PLANE = (2, N, N)
F32 = jnp.float32
BF16 = jnp.bfloat16
PARAMS = pltpu.CompilerParams(vmem_limit_bytes=40 << 20)


def halves(table):
    high = table.astype(ml_dtypes.bfloat16)
    low = (table - high.astype(np.float64)).astype(ml_dtypes.bfloat16)
    return high, low


def rounded(table):
    scaled = table
    for _ in range(4):
        high, low = halves(scaled)
        total = high.astype(np.float64) + low.astype(np.float64)
        scaled = scaled * (1.0 + np.sum(table * (table - total)) / np.sum(table * table))
    return halves(scaled)


def operator_tables(matrix):
    real, imag = matrix.real, matrix.imag
    right = np.block([[real, imag], [-imag, real]])
    left = np.block([[real, -imag], [imag, real]])
    return rounded(right) + rounded(left)


def make_tables():
    index = np.arange(N)
    product = np.outer(index, index) % N
    dft = np.exp(-2j * np.pi * product / N) / math.sqrt(N)
    centred = (index + N // 2) % N - N // 2
    phase = np.exp(-1j * np.pi * centred * centred / N)
    step = (np.conj(dft) * phase[None, :]) @ dft
    step = (step + step.T) / 2
    return operator_tables(step), operator_tables(dft)


def split(value):
    high = value.astype(BF16)
    return high, (value - high.astype(F32)).astype(BF16)


def product(first, second):
    return jnp.dot(first, second, preferred_element_type=F32)


def two_sided(real, imag, tables):
    right_high, right_low, left_high, left_low = tables
    high, low = split(jnp.concatenate([real, imag], axis=1))
    turned = product(high, right_high[...]) + product(low, right_high[...])
    turned = turned + product(high, right_low[...])
    high, low = split(jnp.concatenate([turned[:, :N], turned[:, N:]], axis=0))
    result = product(left_high[...], high) + product(left_high[...], low)
    result = result + product(left_low[...], high)
    return result[:N], result[N:]


def times(first_re, first_im, second_re, second_im):
    return (
        first_re * second_re - first_im * second_im,
        first_re * second_im + first_im * second_re,
    )


def cut_kernel(where, field, probe, fore_same, fore_other, own_same, own_other, wave):
    lane = lax.broadcasted_iota(jnp.int32, (N, N), 1)

    def cut(target, base):
        tile = pl.multiple_of(where[base + 1] * N, N)
        after = pl.multiple_of(where[base + 2] * N, N)
        wrapped = lane < where[base + 3]
        for layer in range(PER_DEVICE):
            for part in range(2):
                here = field[layer, part, :, pl.ds(tile, N)]
                there = field[layer, part, :, pl.ds(after, N)]
                target[layer, part] = jnp.where(wrapped, there, here)

    cut(own_same, 0)
    cut(own_other, 4)
    cut(fore_same, 8)
    cut(fore_other, 12)
    for part in range(2):
        rolled = pltpu.roll(probe[part], where[0], 0)
        wave[part] = pltpu.roll(rolled, where[3], 1)


def cut_windows(where, field, probe):
    piece = jax.ShapeDtypeStruct((PER_DEVICE,) + PLANE, F32)
    return pl.pallas_call(
        cut_kernel,
        out_shape=(piece,) * 4 + (jax.ShapeDtypeStruct(PLANE, F32),),
        in_specs=[
            pl.BlockSpec(memory_space=pltpu.SMEM),
            pl.BlockSpec(memory_space=pltpu.VMEM),
            pl.BlockSpec(memory_space=pltpu.VMEM),
        ],
        name="cut_windows",
        compiler_params=PARAMS,
    )(where, field, probe)


def paste_kernel(where, own_same, own_other, prev_same, prev_other, out):
    row = lax.broadcasted_iota(jnp.int32, (N, N), 0)
    lane = lax.broadcasted_iota(jnp.int32, (N, N), 1)
    out[...] = jnp.zeros(out.shape, F32)

    def paste(source, base, ahead):
        tile = pl.multiple_of(where[base + 1] * N, N)
        after = pl.multiple_of(where[base + 2] * N, N)
        rows = row < where[base] if ahead else row >= where[base]
        first = rows & (lane >= where[base + 3])
        second = rows & (lane < where[base + 3])
        for layer in range(PER_DEVICE):
            for part in range(2):
                value = source[layer, part]
                out[layer, part, :, pl.ds(tile, N)] += jnp.where(first, value, 0.0)
                out[layer, part, :, pl.ds(after, N)] += jnp.where(second, value, 0.0)

    paste(own_same, 0, False)
    paste(own_other, 4, False)
    paste(prev_same, 8, True)
    paste(prev_other, 12, True)


def paste_windows(where, pieces, shape):
    vmem = pl.BlockSpec(memory_space=pltpu.VMEM)
    return pl.pallas_call(
        paste_kernel,
        out_shape=jax.ShapeDtypeStruct(shape, F32),
        in_specs=[pl.BlockSpec(memory_space=pltpu.SMEM)] + [vmem] * 4,
        name="paste_windows",
        compiler_params=PARAMS,
    )(where, *pieces)


def fetch(place, sources, windows, sems):
    near, up, far_up, far_down, down = sources
    for distance in range(RING):
        chip = (place[1] + distance) % RING
        for slot in range(PER_CHIP):
            if distance == 2:
                source = (far_up if slot < PER_DEVICE else far_down).at[slot % PER_DEVICE]
            else:
                source = (near, up, None, down)[distance].at[slot]
            core = place[2] if slot < PER_DEVICE else 1 - place[2]
            layer = chip * PER_CHIP + core * PER_DEVICE + slot % PER_DEVICE
            pltpu.make_async_copy(source, windows.at[layer], sems.at[layer]).start()


def arrive(source, windows, sems, layer):
    pltpu.make_async_copy(source, windows.at[layer], sems.at[layer]).wait()


def forward_steps(count, real, imag, windows, history, sems, source, tables):
    def one(layer, state):
        real, imag = state
        arrive(source, windows, sems, layer)
        history[layer, 0] = real
        history[layer, 1] = imag
        mixed = times(real, imag, windows[layer, 0], windows[layer, 1])
        return two_sided(*mixed, tables)

    return lax.fori_loop(0, count, one, (real, imag), unroll=count // 5 if count % 5 == 0 else 4)


def forward_kernel(place, near, up, far_up, far_down, down, wave, *rest):
    tables, (leaving, saved, windows, history, sems, out_sem) = rest[:4], rest[4:]

    @pl.when(place[0] == 1)
    def _():
        fetch(place, (near, up, far_up, far_down, down), windows, sems)
        real, imag = forward_steps(
            PER_STAGE, wave[0], wave[1], windows, history, sems, near.at[0], tables
        )
        leaving[0] = real
        leaving[1] = imag
        kept = history.at[pl.ds(place[1] * PER_CHIP, PER_CHIP)]
        copy = pltpu.make_async_copy(kept, saved, out_sem)
        copy.start()
        copy.wait()


def gradients(place, trail, psi_of, piece, same, other, sems):
    for slot in range(PER_CHIP):
        core = place[2] if slot < PER_DEVICE else 1 - place[2]
        local = core * PER_DEVICE + slot % PER_DEVICE
        layer = place[1] * PER_CHIP + local
        psi_re, psi_im = psi_of(layer, local)
        real, imag = times(trail[layer, 0], trail[layer, 1], psi_re, psi_im)
        piece[slot, 0] = real
        piece[slot, 1] = -imag
    copies = (
        pltpu.make_async_copy(piece.at[pl.ds(0, PER_DEVICE)], same, sems.at[0]),
        pltpu.make_async_copy(piece.at[pl.ds(PER_DEVICE, PER_DEVICE)], other, sems.at[1]),
    )
    for copy in copies:
        copy.start()
    for copy in copies:
        copy.wait()


def backward_kernel(place, near, up, far_up, far_down, down, wave, saved, *rest):
    tables, rest = rest[:4], rest[4:]
    unused_same, unused_other, leaving, same, other, windows, trail, psi, piece, sems, more = rest

    @pl.when(place[0] == 1)
    def _():
        fetch(place, (near, up, far_up, far_down, down), windows, sems)
        load = pltpu.make_async_copy(saved, psi, more.at[2])
        load.start()

        def one(step, state):
            layer = PER_STAGE - 1 - step
            real, imag = state
            arrive(near.at[0], windows, sems, layer)
            trail[layer, 0] = real
            trail[layer, 1] = imag
            mixed = times(real, imag, windows[layer, 0], windows[layer, 1])
            return two_sided(*mixed, tables)

        real, imag = lax.fori_loop(0, PER_STAGE, one, (wave[0], wave[1]), unroll=4)
        leaving[0] = real
        leaving[1] = imag
        load.wait()
        gradients(
            place,
            trail,
            lambda layer, local: (psi[local, 0], psi[local, 1]),
            piece,
            same,
            other,
            more,
        )


def turn_kernel(place, near, up, far_up, far_down, down, wave, measured, *rest):
    tables, far_tables, rest = rest[:4], rest[4:8], rest[8:]
    leaving, same, other, windows, history, trail, piece, sems, more = rest

    @pl.when(place[0] == 1)
    def _():
        fetch(place, (near, up, far_up, far_down, down), windows, sems)
        last = PER_STAGE - 1
        real, imag = forward_steps(
            last, wave[0], wave[1], windows, history, sems, near.at[0], tables
        )
        arrive(near.at[0], windows, sems, last)
        history[last, 0] = real
        history[last, 1] = imag
        mixed = times(real, imag, windows[last, 0], windows[last, 1])
        real, imag = two_sided(*mixed, far_tables)
        misfit = real * real + imag * imag - measured[...]
        real, imag = two_sided(misfit * real, -(misfit * imag), far_tables)

        def one(step, state):
            layer = last - step
            real, imag = state
            trail[layer, 0] = real
            trail[layer, 1] = imag
            mixed = times(real, imag, windows[layer, 0], windows[layer, 1])
            return two_sided(*mixed, tables)

        real, imag = lax.fori_loop(0, PER_STAGE, one, (real, imag), unroll=4)
        leaving[0] = real
        leaving[1] = imag
        gradients(
            place,
            trail,
            lambda layer, local: (history[layer, 0], history[layer, 1]),
            piece,
            same,
            other,
            more,
        )


STACK = pltpu.VMEM((PER_STAGE,) + PLANE, F32)
CHIP_STACK = pltpu.VMEM((PER_CHIP,) + PLANE, F32)
WAVE = jax.ShapeDtypeStruct(PLANE, F32)
PIECE = jax.ShapeDtypeStruct((PER_DEVICE,) + PLANE, F32)
SAVED = jax.ShapeDtypeStruct((PER_CHIP,) + PLANE, F32)
SMEM_SPEC = pl.BlockSpec(memory_space=pltpu.SMEM)
VMEM_SPEC = pl.BlockSpec(memory_space=pltpu.VMEM)
ANY_SPEC = pl.BlockSpec(memory_space=pl.ANY)


def forward_stage(place, sources, wave, tables):
    return pl.pallas_call(
        forward_kernel,
        out_shape=(WAVE, SAVED),
        in_specs=[SMEM_SPEC] + [ANY_SPEC] * 5 + [VMEM_SPEC] * 5,
        out_specs=(VMEM_SPEC, ANY_SPEC),
        scratch_shapes=[
            STACK,
            STACK,
            pltpu.SemaphoreType.DMA((PER_STAGE,)),
            pltpu.SemaphoreType.DMA(()),
        ],
        name="forward_stage",
        compiler_params=PARAMS,
    )(place, *sources, wave, *tables)


def backward_stage(place, sources, wave, saved, tables, same, other):
    return pl.pallas_call(
        backward_kernel,
        out_shape=(WAVE, PIECE, PIECE),
        in_specs=[SMEM_SPEC] + [ANY_SPEC] * 5 + [VMEM_SPEC, ANY_SPEC] + [VMEM_SPEC] * 4
        + [ANY_SPEC] * 2,
        out_specs=(VMEM_SPEC, ANY_SPEC, ANY_SPEC),
        scratch_shapes=[
            STACK,
            STACK,
            CHIP_STACK,
            CHIP_STACK,
            pltpu.SemaphoreType.DMA((PER_STAGE,)),
            pltpu.SemaphoreType.DMA((3,)),
        ],
        input_output_aliases={12: 1, 13: 2},
        name="backward_stage",
        compiler_params=PARAMS,
    )(place, *sources, wave, saved, *tables, same, other)


def turn_stage(place, sources, wave, measured, tables, far_tables):
    return pl.pallas_call(
        turn_kernel,
        out_shape=(WAVE, PIECE, PIECE),
        in_specs=[SMEM_SPEC] + [ANY_SPEC] * 5 + [VMEM_SPEC] * 10,
        out_specs=(VMEM_SPEC, ANY_SPEC, ANY_SPEC),
        scratch_shapes=[
            STACK,
            STACK,
            STACK,
            CHIP_STACK,
            pltpu.SemaphoreType.DMA((PER_STAGE,)),
            pltpu.SemaphoreType.DMA((2,)),
        ],
        name="turn_stage",
        compiler_params=PARAMS,
    )(place, *sources, wave, measured, *tables, *far_tables)


def along_ring(value, steps):
    def target(device):
        stage, rest = divmod(device, RING * CORES)
        chip, core = divmod(rest, CORES)
        return (stage * RING + (chip + steps) % RING) * CORES + core

    pairs = [(device, target(device)) for device in range(STAGES * RING * CORES)]
    return lax.ppermute(value, "depth", pairs)


def along_stages(value, steps):
    count = STAGES * RING * CORES
    pairs = [(device, (device + steps * RING * CORES) % count) for device in range(count)]
    return lax.ppermute(value, "depth", pairs)


def across(value, strips, swap):
    rows, depth = lax.axis_size("pos"), lax.axis_size("depth")
    pairs = []
    for strip in range(rows):
        for device in range(depth):
            other = device ^ 1 if swap else device
            pairs.append((strip * depth + device, (strip + strips) % rows * depth + other))
    return lax.ppermute(value, ("pos", "depth"), pairs)


def corner(offsets, strip_rows):
    tile = offsets[:, 1] // N
    after = jnp.minimum(tile + 1, 3)
    return jnp.stack([offsets[:, 0] % strip_rows, tile, after, offsets[:, 1] % N], axis=1)


def body(object_field, offsets, probe, intensity, tables, far_tables):
    strip_rows = object_field.shape[2]
    depth_here = lax.axis_index("depth")
    core = depth_here % CORES
    chip = depth_here // CORES % RING
    stage = depth_here // (CORES * RING)

    rows, depth = lax.axis_size("pos"), lax.axis_size("depth")
    before = lax.ppermute(offsets, "pos", [(i, (i + 1) % rows) for i in range(rows)])
    own = corner(offsets, strip_rows)
    prev = corner(before, strip_rows)
    flip = core == 1
    own = jnp.where(flip, own[::-1], own)
    prev = jnp.where(flip, prev[::-1], prev)
    where = jnp.concatenate([own.reshape(-1), prev.reshape(-1)])

    fore_same, fore_other, own_same, own_other, wave = cut_windows(where, object_field, probe)
    fore_same = across(fore_same, -1, False)
    fore_other = across(fore_other, -1, True)
    own_other = across(own_other, 0, True)
    below = jnp.arange(strip_rows, dtype=jnp.int32)[:, None] >= where[0]
    near = jnp.concatenate(
        [jnp.where(below, own_same, fore_same), jnp.where(below, own_other, fore_other)], axis=0
    )
    up = along_ring(near, -1)
    down = along_ring(near, 1)
    far_up = along_ring(up[:PER_DEVICE], -1)
    far_down = along_ring(down[PER_DEVICE:], 1)
    sources = (near, up, far_up, far_down, down)

    def place(section):
        return jnp.stack([(stage == section).astype(jnp.int32), chip, core])

    kept = []
    for section in range(STAGES - 1):
        wave, saved = forward_stage(place(section), sources, wave, tables)
        kept.append(saved)
        wave = along_stages(wave, 1)
    measured = lax.dynamic_index_in_dim(intensity, core, 0, keepdims=False)
    wave, same, other = turn_stage(
        place(STAGES - 1), sources, wave, measured, tables, far_tables
    )
    for section in reversed(range(STAGES - 1)):
        wave = along_stages(wave, -1)
        wave, same, other = backward_stage(
            place(section), sources, wave, kept[section], tables, same, other
        )
    prev_same = across(same, 1, False)
    prev_other = across(other, 1, True)
    own_other = across(other, 0, True)
    return paste_windows(where, (same, own_other, prev_same, prev_other), object_field.shape)


def solution(mesh):
    step, far = make_tables()
    mapped = jax.shard_map(
        body,
        mesh=mesh,
        in_specs=(
            P("depth", None, "pos", None),
            P("pos", None),
            P(),
            P("pos", None, None),
            P(),
            P(),
        ),
        out_specs=P("depth", None, "pos", None),
        check_vma=False,
    )

    def run(object_field, offsets, probe, intensity):
        return mapped(
            object_field,
            offsets,
            probe,
            intensity,
            tuple(jnp.asarray(table) for table in step),
            tuple(jnp.asarray(table) for table in far),
        )

    return run
```

time: 941 us -> 184 us (0.20)
  the two profiles are of different devices: /device:TPU:57 before, /device:TPU:1 now
where the time goes in v1:
time: 184 us
  starting transfers between devices  75.7 us (41%)
  waiting for transfers between devices  67.4 us (37%)
  Pallas kernels  32.3 us (18%)
  local copies, waits for them, and re-layouts  6.54 us (4%)
    ppermute x6, starting transfers between devices, along_stages(): return lax.ppermute(value, 'depth', pairs)  56.1 us
    ppermute x6, waiting for transfers between devices, along_stages(): return lax.ppermute(value, 'depth', pairs)  27 us
    ppermute x6, waiting for transfers between devices, across(): return lax.ppermute(value, ('pos', 'depth'), pairs)  20.9 us
    ppermute x4, waiting for transfers between devices, along_ring(): return lax.ppermute(value, 'depth', pairs)  17.9 us
    pallas_call x3, Pallas kernels, backward_stage(): pl.pallas_call(backward_kernel, out_shape=(WAVE, PIECE, PIECE), in_specs=...  14.2 us
    pallas_call x3, Pallas kernels, forward_stage(): pl.pallas_call(forward_kernel, out_shape=(WAVE, SAVED), in_specs=[SMEM_SP...  14 us
    ppermute x6, starting transfers between devices, across(): return lax.ppermute(value, ('pos', 'depth'), pairs)  11.6 us
    unnamed x34, local copies, waits for them, and re-layouts  6.27 us
  transfers between devices with their start and end apart: 17, of which 12 were waited for; matrix products, arithmetic and copies ran while one was open for 1% of the time, Pallas kernels for 0%

profile of v1, /device:TPU:1, one launch (start us, length us, event | category | flops | bytes accessed | tf_op | source)
XLA Modules:
  0.0 183.7 jit_solution(6155231716516507269)
XLA Ops:
  0.0 2.0 %collective-permute-start = (s32[2,2]{1,0:T(2,128)}, s32[2,2]{1,0:T(2,128)S(1)}, u32[]{:S(2)}, u32[]{:S(2)}) collective-permute-start(s32[2,2]{1,0:T(2,128)} %param.13), channel_id=1, source_target_pairs={{0,32},{32,64},{64,96},{96,0},{1,33},{33,65},{65,97},{97,1},{2,34}... | collective-permute-start | bytes 56 | tf_op jit(solution)/shard_map/ppermute | solution.py:404
  2.9 1.5 collective-permute-done
  5.0 1.2 copy-done.5
  6.2 0.9 copy-done.10
  8.0 1.5 collective-permute-start.1
  9.5 2.1 %collective-permute-start.2 = (f32[2,2,128,128]{3,2,1,0:T(8,128)S(1)}, f32[2,2,128,128]{3,2,1,0:T(8,128)S(1)}, u32[]{:S(2)}, u32[]{:S(2)}) collective-permute-start(f32[2,2,128,128]{3,2,1,0:T(8,128)S(1)} %get-tuple-element.29), channel_id=1, source_target_pairs={{0,1},{1,0},{2,3},{3,2},{4,5},{5,4},{6,7},{7,6},{8,9},{9,8},{10,11... | collective-permute-start | bytes 786440 | tf_op jit(solution)/shard_map/ppermute | solution.py:387
  12.1 1.8 collective-permute-done.1
  13.9 7.8 %collective-permute-done.3 = f32[2,2,128,128]{3,2,1,0:T(8,128)S(1)} collective-permute-done((f32[2,2,128,128]{3,2,1,0:T(8,128)S(1)}, f32[2,2,128,128]{3,2,1,0:T(8,128)S(1)}, u32[]{:S(2)}, u32[]{:S(2)}) %collective-permute-start.3) | collective-permute-done | bytes 262176 | tf_op jit(solution)/shard_map/ppermute | solution.py:387
  21.9 1.6 collective-permute-start.6
  23.5 1.5 collective-permute-start.4
  25.0 12.2 %collective-permute-done.6.down = f32[4,2,128,128]{3,2,1,0:T(8,128)S(1)} collective-permute-done((f32[4,2,128,128]{3,2,1,0:T(8,128)S(1)}, f32[4,2,128,128]{3,2,1,0:T(8,128)S(1)}, u32[]{:S(2)}, u32[]{:S(2)}) %collective-permute-start.6) | collective-permute-done | bytes 524320 | tf_op jit(solution)/shard_map/ppermute | solution.py:371
  37.4 2.7 %collective-permute-start.5 = (f32[2,2,128,128]{3,2,1,0:T(8,128)S(1)}, f32[2,2,128,128]{3,2,1,0:T(8,128)S(1)}, u32[]{:S(2)}, u32[]{:S(2)}) collective-permute-start(f32[2,2,128,128]{3,2,1,0:T(8,128)S(1)} %slice.30), channel_id=1, source_target_pairs={{0,6},{1,7},{2,0},{3,1},{4,2},{5,3},{6,4},{7,5},{8,14},{9,15},{10,... | collective-permute-start | bytes 786440 | tf_op jit(solution)/shard_map/ppermute | solution.py:371
  40.2 5.7 %collective-permute-done.7.far_down = f32[2,2,128,128]{3,2,1,0:T(8,128)S(1)} collective-permute-done((f32[2,2,128,128]{3,2,1,0:T(8,128)S(1)}, f32[2,2,128,128]{3,2,1,0:T(8,128)S(1)}, u32[]{:S(2)}, u32[]{:S(2)}) %collective-permute-start.7) | collective-permute-done | bytes 262176 | tf_op jit(solution)/shard_map/ppermute | solution.py:371
  45.9 11.9 %forward_stage.3 = (f32[2,128,128]{2,1,0:T(8,128)S(1)}, f32[4,2,128,128]{3,2,1,0:T(8,128)S(1)}) custom-call(s32[3]{0:T(128)S(1)} %add_add_fusion.place, f32[4,2,128,128]{3,2,1,0:T(8,128)S(1)} %pad_maximum_fusion.near, f32[4,2,128,128]{3,2,1,0:T(8,128)S(1)} %collective-permute-done.4.up, f32[2,2,128,128]{3,2,1,0:T(8,128)S(1)} %collective-permute-done.5.far_up, ...), custom_call_target="tpu_custom_call" | custom-call | tf_op jit(solution)/shard_map/forward_stage/pallas_call | solution.py:308
  58.0 4.9 %collective-permute-done.8.wave = f32[2,128,128]{2,1,0:T(8,128)S(1)} collective-permute-done((f32[2,128,128]{2,1,0:T(8,128)S(1)}, f32[2,128,128]{2,1,0:T(8,128)S(1)}, u32[]{:S(2)}, u32[]{:S(2)}) %collective-permute-start.8) | collective-permute-done | bytes 131104 | tf_op jit(solution)/shard_map/ppermute | solution.py:377
  64.4 10.0 %collective-permute-start.9 = (f32[2,128,128]{2,1,0:T(8,128)S(1)}, f32[2,128,128]{2,1,0:T(8,128)S(1)}, u32[]{:S(2)}, u32[]{:S(2)}) collective-permute-start(f32[2,128,128]{2,1,0:T(8,128)S(1)} %get-tuple-element.33), channel_id=1, source_target_pairs={{0,8},{1,9},{2,10},{3,11},{4,12},{5,13},{6,14},{7,15},{8,16},{9,17... | collective-permute-start | bytes 393224 | tf_op jit(solution)/shard_map/ppermute | solution.py:377
  74.5 1.9 %collective-permute-done.9.wave = f32[2,128,128]{2,1,0:T(8,128)S(1)} collective-permute-done((f32[2,128,128]{2,1,0:T(8,128)S(1)}, f32[2,128,128]{2,1,0:T(8,128)S(1)}, u32[]{:S(2)}, u32[]{:S(2)}) %collective-permute-start.9) | collective-permute-done | bytes 131104 | tf_op jit(solution)/shard_map/ppermute | solution.py:377
  76.4 1.4 forward_stage.5
  78.5 1.9 %collective-permute-start.10 = (f32[2,128,128]{2,1,0:T(8,128)}, f32[2,128,128]{2,1,0:T(8,128)}, u32[]{:S(2)}, u32[]{:S(2)}) collective-permute-start(f32[2,128,128]{2,1,0:T(8,128)} %get-tuple-element.34), channel_id=1, source_target_pairs={{0,8},{1,9},{2,10},{3,11},{4,12},{5,13},{6,14},{7,15},{8,16},{9,17... | collective-permute-start | bytes 393224 | tf_op jit(solution)/shard_map/ppermute | solution.py:377
  81.1 2.8 %collective-permute-done.10.wave = f32[2,128,128]{2,1,0:T(8,128)} collective-permute-done((f32[2,128,128]{2,1,0:T(8,128)}, f32[2,128,128]{2,1,0:T(8,128)}, u32[]{:S(2)}, u32[]{:S(2)}) %collective-permute-start.10) | collective-permute-done | bytes 131104 | tf_op jit(solution)/shard_map/ppermute | solution.py:377
  84.8 0.9 copy-done.14
  85.7 1.3 turn_stage.1
  87.0 30.8 %collective-permute-start.11 = (f32[2,128,128]{2,1,0:T(8,128)S(1)}, f32[2,128,128]{2,1,0:T(8,128)S(1)}, u32[]{:S(2)}, u32[]{:S(2)}) collective-permute-start(f32[2,128,128]{2,1,0:T(8,128)S(1)} %get-tuple-element.35), channel_id=1, source_target_pairs={{0,24},{1,25},{2,26},{3,27},{4,28},{5,29},{6,30},{7,31},{8,0},{9,1... | collective-permute-start | bytes 393224 | tf_op jit(solution)/shard_map/ppermute | solution.py:377
  117.8 1.9 %collective-permute-done.11.wave = f32[2,128,128]{2,1,0:T(8,128)S(1)} collective-permute-done((f32[2,128,128]{2,1,0:T(8,128)S(1)}, f32[2,128,128]{2,1,0:T(8,128)S(1)}, u32[]{:S(2)}, u32[]{:S(2)}) %collective-permute-start.11) | collective-permute-done | bytes 131104 | tf_op jit(solution)/shard_map/ppermute | solution.py:377
  120.5 3.1 %collective-permute-start.12 = (f32[2,128,128]{2,1,0:T(8,128)S(1)}, f32[2,128,128]{2,1,0:T(8,128)S(1)}, u32[]{:S(2)}, u32[]{:S(2)}) collective-permute-start(f32[2,128,128]{2,1,0:T(8,128)S(1)} %get-tuple-element.39), channel_id=1, source_target_pairs={{0,24},{1,25},{2,26},{3,27},{4,28},{5,29},{6,30},{7,31},{8,0},{9,1... | collective-permute-start | bytes 393224 | tf_op jit(solution)/shard_map/ppermute | solution.py:377
  123.7 2.0 %collective-permute-done.12.wave = f32[2,128,128]{2,1,0:T(8,128)S(1)} collective-permute-done((f32[2,128,128]{2,1,0:T(8,128)S(1)}, f32[2,128,128]{2,1,0:T(8,128)S(1)}, u32[]{:S(2)}, u32[]{:S(2)}) %collective-permute-start.12) | collective-permute-done | bytes 131104 | tf_op jit(solution)/shard_map/ppermute | solution.py:377
  126.3 10.2 %collective-permute-start.13 = (f32[2,128,128]{2,1,0:T(8,128)S(1)}, f32[2,128,128]{2,1,0:T(8,128)S(1)}, u32[]{:S(2)}, u32[]{:S(2)}) collective-permute-start(f32[2,128,128]{2,1,0:T(8,128)S(1)} %get-tuple-element.43), channel_id=1, source_target_pairs={{0,24},{1,25},{2,26},{3,27},{4,28},{5,29},{6,30},{7,31},{8,0},{9,1... | collective-permute-start | bytes 393224 | tf_op jit(solution)/shard_map/ppermute | solution.py:377
  136.5 13.5 %collective-permute-done.13.wave = f32[2,128,128]{2,1,0:T(8,128)S(1)} collective-permute-done((f32[2,128,128]{2,1,0:T(8,128)S(1)}, f32[2,128,128]{2,1,0:T(8,128)S(1)}, u32[]{:S(2)}, u32[]{:S(2)}) %collective-permute-start.13) | collective-permute-done | bytes 131104 | tf_op jit(solution)/shard_map/ppermute | solution.py:377
  150.1 12.7 %backward_stage.5 = (f32[2,128,128]{2,1,0:T(8,128)}, f32[2,2,128,128]{3,2,1,0:T(8,128)S(1)}, f32[2,2,128,128]{3,2,1,0:T(8,128)S(1)}) custom-call(s32[3]{0:T(128)S(1)} %add_add_fusion.place, f32[4,2,128,128]{3,2,1,0:T(8,128)S(1)} %pad_maximum_fusion.near, ...), custom_call_target="tpu_custom_call", output_to_operand_aliasing={{1}: (12, {}), {2}: (13, {})} | custom-call | tf_op jit(solution)/shard_map/backward_stage/pallas_call | solution.py:325
  162.9 7.5 %collective-permute-start.16 = (f32[2,2,128,128]{3,2,1,0:T(8,128)S(1)}, f32[2,2,128,128]{3,2,1,0:T(8,128)S(1)}, u32[]{:S(2)}, u32[]{:S(2)}) collective-permute-start(f32[2,2,128,128]{3,2,1,0:T(8,128)S(1)} %get-tuple-element.48), channel_id=1, source_target_pairs={{0,33},{1,32},{2,35},{3,34},{4,37},{5,36},{6,39},{7,38},{8,41},{9,... | collective-permute-start | bytes 786440 | tf_op jit(solution)/shard_map/ppermute | solution.py:387
  170.4 11.3 %collective-permute-done.16.prev_other = f32[2,2,128,128]{3,2,1,0:T(8,128)S(1)} collective-permute-done((f32[2,2,128,128]{3,2,1,0:T(8,128)S(1)}, f32[2,2,128,128]{3,2,1,0:T(8,128)S(1)}, u32[]{:S(2)}, u32[]{:S(2)}) %collective-permute-start.16) | collective-permute-done | bytes 262176 | tf_op jit(solution)/shard_map/ppermute | solution.py:387
  181.7 2.0 %paste_windows.1 = f32[2,2,128,512]{3,2,1,0:T(8,128)} custom-call(s32[16]{0:T(128)S(1)} %pad_add_fusion.2.where, f32[2,2,128,128]{3,2,1,0:T(8,128)S(1)} %get-tuple-element.47.own_same, f32[2,2,128,128]{3,2,1,0:T(8,128)S(1)} %collective-permute-done.14.own_other, f32[2,2,128,128]{3,2,1,0:T(8,128)S(1)} %collective-permute-done.15.prev_same, ...), custom_call_target="tpu_custom_call" | custom-call | tf_op jit(solution)/shard_map/paste_windows/pallas_call | solution.py:147
  (65 shorter events, 8.8 us)
Async XLA Ops:
  0.0 81.1 %copy-start = (f32[2,128,128]{2,1,0:T(8,128)S(1)}, f32[2,128,128]{2,1,0:T(8,128)}, u32[]{:S(2)}) copy-start(f32[2,128,128]{2,1,0:T(8,128)} %param.15) | copy-start | bytes 393220
  0.0 4.5 %collective-permute-start = (s32[2,2]{1,0:T(2,128)}, s32[2,2]{1,0:T(2,128)S(1)}, u32[]{:S(2)}, u32[]{:S(2)}) collective-permute-start(s32[2,2]{1,0:T(2,128)} %param.13), channel_id=1, source_target_pairs={{0,32},{32,64},{64,96},{96,0},{1,33},{33,65},{65,97},{97,1},{2,34}... | collective-permute-start | bytes 56 | tf_op jit(solution)/shard_map/ppermute | solution.py:404
  5.0 1.2 copy-start.5
  6.2 0.9 copy-start.10
  8.0 5.9 %collective-permute-start.1 = (f32[2,2,128,128]{3,2,1,0:T(8,128)S(1)}, f32[2,2,128,128]{3,2,1,0:T(8,128)S(1)}, u32[]{:S(2)}, u32[]{:S(2)}) collective-permute-start(f32[2,2,128,128]{3,2,1,0:T(8,128)S(1)} %get-tuple-element.28), channel_id=1, source_target_pairs={{0,96},{1,97},{2,98},{3,99},{4,100},{5,101},{6,102},{7,103},{8,104... | collective-permute-start | bytes 786440 | tf_op jit(solution)/shard_map/ppermute | solution.py:387
  9.5 4.4 %collective-permute-start.2 = (f32[2,2,128,128]{3,2,1,0:T(8,128)S(1)}, f32[2,2,128,128]{3,2,1,0:T(8,128)S(1)}, u32[]{:S(2)}, u32[]{:S(2)}) collective-permute-start(f32[2,2,128,128]{3,2,1,0:T(8,128)S(1)} %get-tuple-element.29), channel_id=1, source_target_pairs={{0,1},{1,0},{2,3},{3,2},{4,5},{5,4},{6,7},{7,6},{8,9},{9,8},{10,11... | collective-permute-start | bytes 786440 | tf_op jit(solution)/shard_map/ppermute | solution.py:387
  11.6 10.1 %collective-permute-start.3 = (f32[2,2,128,128]{3,2,1,0:T(8,128)S(1)}, f32[2,2,128,128]{3,2,1,0:T(8,128)S(1)}, u32[]{:S(2)}, u32[]{:S(2)}) collective-permute-start(f32[2,2,128,128]{3,2,1,0:T(8,128)S(1)} %get-tuple-element.30), channel_id=1, source_target_pairs={{0,97},{1,96},{2,99},{3,98},{4,101},{5,100},{6,103},{7,102},{8,105... | collective-permute-start | bytes 786440 | tf_op jit(solution)/shard_map/ppermute | solution.py:387
  21.9 15.3 %collective-permute-start.6 = (f32[4,2,128,128]{3,2,1,0:T(8,128)S(1)}, f32[4,2,128,128]{3,2,1,0:T(8,128)S(1)}, u32[]{:S(2)}, u32[]{:S(2)}) collective-permute-start(f32[4,2,128,128]{3,2,1,0:T(8,128)S(1)} %pad_maximum_fusion.near), channel_id=1, source_target_pairs={{0,2},{1,3},{2,4},{3,5},{4,6},{5,7},{6,0},{7,1},{8,10},{9,11},{10,... | collective-permute-start | bytes 1572872 | tf_op jit(solution)/shard_map/ppermute | solution.py:371
  23.5 13.9 %collective-permute-start.4 = (f32[4,2,128,128]{3,2,1,0:T(8,128)S(1)}, f32[4,2,128,128]{3,2,1,0:T(8,128)S(1)}, u32[]{:S(2)}, u32[]{:S(2)}) collective-permute-start(f32[4,2,128,128]{3,2,1,0:T(8,128)S(1)} %pad_maximum_fusion.near), channel_id=1, source_target_pairs={{0,6},{1,7},{2,0},{3,1},{4,2},{5,3},{6,4},{7,5},{8,14},{9,15},{10,... | collective-permute-start | bytes 1572872 | tf_op jit(solution)/shard_map/ppermute | solution.py:371
  37.3 8.6 %collective-permute-start.7 = (f32[2,2,128,128]{3,2,1,0:T(8,128)S(1)}, f32[2,2,128,128]{3,2,1,0:T(8,128)S(1)}, u32[]{:S(2)}, u32[]{:S(2)}) collective-permute-start(f32[2,2,128,128]{3,2,1,0:T(8,128)S(1)} %slice.31), channel_id=1, source_target_pairs={{0,2},{1,3},{2,4},{3,5},{4,6},{5,7},{6,0},{7,1},{8,10},{9,11},{10,... | collective-permute-start | bytes 786440 | tf_op jit(solution)/shard_map/ppermute | solution.py:371
  37.3 8.5 %copy-start.1 = (bf16[256,256]{1,0:T(8,128)(2,1)S(1)}, bf16[256,256]{1,0:T(8,128)(2,1)}, u32[]{:S(2)}) copy-start(bf16[256,256]{1,0:T(8,128)(2,1)} %constant.122.clone.rest_3_) | copy-start | bytes 393220
  37.4 8.5 %copy-start.2 = (bf16[256,256]{1,0:T(8,128)(2,1)S(1)}, bf16[256,256]{1,0:T(8,128)(2,1)}, u32[]{:S(2)}) copy-start(bf16[256,256]{1,0:T(8,128)(2,1)} %constant.121.clone.rest_2_) | copy-start | bytes 393220
  37.4 8.5 %copy-start.3 = (bf16[256,256]{1,0:T(8,128)(2,1)S(1)}, bf16[256,256]{1,0:T(8,128)(2,1)}, u32[]{:S(2)}) copy-start(bf16[256,256]{1,0:T(8,128)(2,1)} %constant.120.clone.rest_1_) | copy-start | bytes 393220
  37.4 8.5 %copy-start.4 = (bf16[256,256]{1,0:T(8,128)(2,1)S(1)}, bf16[256,256]{1,0:T(8,128)(2,1)}, u32[]{:S(2)}) copy-start(bf16[256,256]{1,0:T(8,128)(2,1)} %constant.119.clone.rest_0_) | copy-start | bytes 393220
  37.4 8.4 %collective-permute-start.5 = (f32[2,2,128,128]{3,2,1,0:T(8,128)S(1)}, f32[2,2,128,128]{3,2,1,0:T(8,128)S(1)}, u32[]{:S(2)}, u32[]{:S(2)}) collective-permute-start(f32[2,2,128,128]{3,2,1,0:T(8,128)S(1)} %slice.30), channel_id=1, source_target_pairs={{0,6},{1,7},{2,0},{3,1},{4,2},{5,3},{6,4},{7,5},{8,14},{9,15},{10,... | collective-permute-start | bytes 786440 | tf_op jit(solution)/shard_map/ppermute | solution.py:371
  57.8 5.1 %collective-permute-start.8 = (f32[2,128,128]{2,1,0:T(8,128)S(1)}, f32[2,128,128]{2,1,0:T(8,128)S(1)}, u32[]{:S(2)}, u32[]{:S(2)}) collective-permute-start(f32[2,128,128]{2,1,0:T(8,128)S(1)} %get-tuple-element.32), channel_id=1, source_target_pairs={{0,8},{1,9},{2,10},{3,11},{4,12},{5,13},{6,14},{7,15},{8,16},{9,17... | collective-permute-start | bytes 393224 | tf_op jit(solution)/shard_map/ppermute | solution.py:377
  64.4 12.0 %collective-permute-start.9 = (f32[2,128,128]{2,1,0:T(8,128)S(1)}, f32[2,128,128]{2,1,0:T(8,128)S(1)}, u32[]{:S(2)}, u32[]{:S(2)}) collective-permute-start(f32[2,128,128]{2,1,0:T(8,128)S(1)} %get-tuple-element.33), channel_id=1, source_target_pairs={{0,8},{1,9},{2,10},{3,11},{4,12},{5,13},{6,14},{7,15},{8,16},{9,17... | collective-permute-start | bytes 393224 | tf_op jit(solution)/shard_map/ppermute | solution.py:377
  76.4 7.5 %copy-start.12 = (bf16[256,256]{1,0:T(8,128)(2,1)S(1)}, bf16[256,256]{1,0:T(8,128)(2,1)}, u32[]{:S(2)}) copy-start(bf16[256,256]{1,0:T(8,128)(2,1)} %constant.125.clone.rest_6_) | copy-start | bytes 393220
  77.7 0.8 copy-start.8
  78.5 5.4 %copy-start.11 = (bf16[256,256]{1,0:T(8,128)(2,1)S(1)}, bf16[256,256]{1,0:T(8,128)(2,1)}, u32[]{:S(2)}) copy-start(bf16[256,256]{1,0:T(8,128)(2,1)} %constant.126.clone.rest_7_) | copy-start | bytes 393220
  78.5 5.3 %collective-permute-start.10 = (f32[2,128,128]{2,1,0:T(8,128)}, f32[2,128,128]{2,1,0:T(8,128)}, u32[]{:S(2)}, u32[]{:S(2)}) collective-permute-start(f32[2,128,128]{2,1,0:T(8,128)} %get-tuple-element.34), channel_id=1, source_target_pairs={{0,8},{1,9},{2,10},{3,11},{4,12},{5,13},{6,14},{7,15},{8,16},{9,17... | collective-permute-start | bytes 393224 | tf_op jit(solution)/shard_map/ppermute | solution.py:377
  81.1 2.8 %copy-start.15 = (s32[3]{0:T(128)S(1)}, s32[3]{0:T(128)}, u32[]{:S(2)}) copy-start(s32[3]{0:T(128)} %add_add_fusion.3.place) | copy-start | bytes 40
  81.1 38.7 %copy-start.9 = (f32[4,2,128,128]{3,2,1,0:T(8,128)S(1)}, f32[4,2,128,128]{3,2,1,0:T(8,128)}, u32[]{:S(2)}) copy-start(f32[4,2,128,128]{3,2,1,0:T(8,128)} %copy-done.8) | copy-start | bytes 1572868
  83.9 0.9 copy-start.13
  84.8 0.9 copy-start.14
  87.0 32.8 %collective-permute-start.11 = (f32[2,128,128]{2,1,0:T(8,128)S(1)}, f32[2,128,128]{2,1,0:T(8,128)S(1)}, u32[]{:S(2)}, u32[]{:S(2)}) collective-permute-start(f32[2,128,128]{2,1,0:T(8,128)S(1)} %get-tuple-element.35), channel_id=1, source_target_pairs={{0,24},{1,25},{2,26},{3,27},{4,28},{5,29},{6,30},{7,31},{8,0},{9,1... | collective-permute-start | bytes 393224 | tf_op jit(solution)/shard_map/ppermute | solution.py:377
  119.8 5.8 %copy-start.7 = (f32[4,2,128,128]{3,2,1,0:T(8,128)S(1)}, f32[4,2,128,128]{3,2,1,0:T(8,128)}, u32[]{:S(2)}) copy-start(f32[4,2,128,128]{3,2,1,0:T(8,128)} %copy-done.6) | copy-start | bytes 1572868
  120.5 5.1 %collective-permute-start.12 = (f32[2,128,128]{2,1,0:T(8,128)S(1)}, f32[2,128,128]{2,1,0:T(8,128)S(1)}, u32[]{:S(2)}, u32[]{:S(2)}) collective-permute-start(f32[2,128,128]{2,1,0:T(8,128)S(1)} %get-tuple-element.39), channel_id=1, source_target_pairs={{0,24},{1,25},{2,26},{3,27},{4,28},{5,29},{6,30},{7,31},{8,0},{9,1... | collective-permute-start | bytes 393224 | tf_op jit(solution)/shard_map/ppermute | solution.py:377
  126.3 23.7 %collective-permute-start.13 = (f32[2,128,128]{2,1,0:T(8,128)S(1)}, f32[2,128,128]{2,1,0:T(8,128)S(1)}, u32[]{:S(2)}, u32[]{:S(2)}) collective-permute-start(f32[2,128,128]{2,1,0:T(8,128)S(1)} %get-tuple-element.43), channel_id=1, source_target_pairs={{0,24},{1,25},{2,26},{3,27},{4,28},{5,29},{6,30},{7,31},{8,0},{9,1... | collective-permute-start | bytes 393224 | tf_op jit(solution)/shard_map/ppermute | solution.py:377
  162.8 7.6 %collective-permute-start.15 = (f32[2,2,128,128]{3,2,1,0:T(8,128)S(1)}, f32[2,2,128,128]{3,2,1,0:T(8,128)S(1)}, u32[]{:S(2)}, u32[]{:S(2)}) collective-permute-start(f32[2,2,128,128]{3,2,1,0:T(8,128)S(1)} %get-tuple-element.47.own_same), channel_id=1, source_target_pairs={{0,32},{1,33},{2,34},{3,35},{4,36},{5,37},{6,38},{7,39},{8,40},{9,... | collective-permute-start | bytes 786440 | tf_op jit(solution)/shard_map/ppermute | solution.py:387
  162.9 18.8 %collective-permute-start.16 = (f32[2,2,128,128]{3,2,1,0:T(8,128)S(1)}, f32[2,2,128,128]{3,2,1,0:T(8,128)S(1)}, u32[]{:S(2)}, u32[]{:S(2)}) collective-permute-start(f32[2,2,128,128]{3,2,1,0:T(8,128)S(1)} %get-tuple-element.48), channel_id=1, source_target_pairs={{0,33},{1,32},{2,35},{3,34},{4,37},{5,36},{6,39},{7,38},{8,41},{9,... | collective-permute-start | bytes 786440 | tf_op jit(solution)/shard_map/ppermute | solution.py:387
  170.4 11.3 %collective-permute-start.14 = (f32[2,2,128,128]{3,2,1,0:T(8,128)S(1)}, f32[2,2,128,128]{3,2,1,0:T(8,128)S(1)}, u32[]{:S(2)}, u32[]{:S(2)}) collective-permute-start(f32[2,2,128,128]{3,2,1,0:T(8,128)S(1)} %get-tuple-element.48), channel_id=1, source_target_pairs={{0,1},{1,0},{2,3},{3,2},{4,5},{5,4},{6,7},{7,6},{8,9},{9,8},{10,11... | collective-permute-start | bytes 786440 | tf_op jit(solution)/shard_map/ppermute | solution.py:387
  (2 other events, 1.5 us)

commit v2 on v1

v2 whole, which is shorter than its diff:
```python
import functools
import math

import jax
import jax.numpy as jnp
import numpy as np
from jax import lax
from jax.experimental import pallas as pl
from jax.experimental.pallas import tpu as pltpu
from jax.sharding import PartitionSpec as P

N = 128
CORES = 2
RING = 4
STAGES = 4
PER_DEVICE = 2
PER_CHIP = CORES * PER_DEVICE
PER_STAGE = RING * PER_CHIP
PLANE = (2, N, N)
F32 = jnp.float32
PARAMS = pltpu.CompilerParams(vmem_limit_bytes=40 << 20)
GROUP = 8
STACK = pltpu.VMEM((PER_STAGE,) + PLANE, F32)
CHIP_STACK = pltpu.VMEM((PER_CHIP,) + PLANE, F32)
ROW_STAGES = pltpu.VMEM((2,) + PLANE, F32)
WAVE = jax.ShapeDtypeStruct(PLANE, F32)
PIECE = jax.ShapeDtypeStruct((PER_DEVICE,) + PLANE, F32)
SAVED = jax.ShapeDtypeStruct((PER_CHIP,) + PLANE, F32)
SMEM_SPEC = pl.BlockSpec(memory_space=pltpu.SMEM)
VMEM_SPEC = pl.BlockSpec(memory_space=pltpu.VMEM)
ANY_SPEC = pl.BlockSpec(memory_space=pl.ANY)


def make_tables():
    index = np.arange(N)
    turn = np.exp(1j * np.pi * (index * index % (2 * N)) / N)
    chirp = np.outer(turn, turn)
    first, second = np.divmod(index, GROUP)
    twiddle = np.exp(-2j * np.pi * first * second / N)[:, None] * np.ones((1, N))
    tables = (
        twiddle,
        -1j * chirp * chirp / N,
        1j * np.conj(chirp),
        np.conj(chirp),
        1j * np.conj(chirp) / N,
        -chirp * chirp,
    )
    return tuple(np.stack([t.real, t.imag]).astype(np.float32) for t in tables)


def times(first_re, first_im, second_re, second_im):
    return (
        first_re * second_re - first_im * second_im,
        first_re * second_im + first_im * second_re,
    )


def rotate(value, numerator, count):
    real, imag = value
    if numerator == 0:
        return value
    if numerator * 4 == count:
        return imag, -real
    half = math.sqrt(0.5)
    if numerator * 8 == count:
        return (real + imag) * half, (imag - real) * half
    if numerator * 8 == 3 * count:
        return (imag - real) * half, -(real + imag) * half
    cosine = math.cos(2.0 * math.pi * numerator / count)
    sine = -math.sin(2.0 * math.pi * numerator / count)
    return real * cosine - imag * sine, real * sine + imag * cosine


def transform(values):
    count = len(values)
    if count == 1:
        return values
    even, odd = transform(values[0::2]), transform(values[1::2])
    result = [None] * count
    for k in range(count // 2):
        moved = rotate(odd[k], k, count)
        result[k] = (even[k][0] + moved[0], even[k][1] + moved[1])
        result[k + count // 2] = (even[k][0] - moved[0], even[k][1] - moved[1])
    return result


def transform_rows(real, imag, twiddle, stage):
    groups = [
        (real[GROUP * k : GROUP * (k + 1)], imag[GROUP * k : GROUP * (k + 1)])
        for k in range(N // GROUP)
    ]
    for k, value in enumerate(transform(groups)):
        rows = pl.ds(GROUP * k, GROUP)
        if k:
            value = times(*value, twiddle[0, rows], twiddle[1, rows])
        stage[0, rows], stage[1, rows] = value
    result = [None] * (N // GROUP)
    for part in range(2):
        picked = [pl.ds(GROUP * GROUP * part + k, GROUP, stride=GROUP) for k in range(GROUP)]
        done = transform([(stage[0, rows], stage[1, rows]) for rows in picked])
        for k in range(GROUP):
            result[2 * k + part] = done[k]
    return (
        jnp.concatenate([value[0] for value in result], axis=0),
        jnp.concatenate([value[1] for value in result], axis=0),
    )


def two_sided(real, imag, twiddle, stages):
    real, imag = transform_rows(real, imag, twiddle, stages.at[0])
    return transform_rows(real.T, imag.T, twiddle, stages.at[1])


def cut(where, base, field, factor, target):
    lane = lax.broadcasted_iota(jnp.int32, (N, N), 1)
    tile = pl.multiple_of(where[base + 1] * N, N)
    after = pl.multiple_of(where[base + 2] * N, N)
    wrapped = lane < where[base + 3]
    for layer in range(PER_DEVICE):
        value = [
            jnp.where(
                wrapped,
                field[layer, part, :, pl.ds(after, N)],
                field[layer, part, :, pl.ds(tile, N)],
            )
            for part in range(2)
        ]
        value = times(*value, factor[0], factor[1])
        for part in range(2):
            target[layer, part] = value[part].T if layer % 2 else value[part]


def cut_fore_kernel(where, field, factor, same, other):
    cut(where, 8, field, factor, same)
    cut(where, 12, field, factor, other)


def cut_own_kernel(where, field, factor, probe, start, same, other, wave):
    cut(where, 0, field, factor, same)
    cut(where, 4, field, factor, other)
    rolled = [pltpu.roll(pltpu.roll(probe[k], where[0], 0), where[3], 1) for k in range(2)]
    wave[0], wave[1] = times(*rolled, start[0], start[1])


def cut_fore(where, field, factor):
    return pl.pallas_call(
        cut_fore_kernel,
        out_shape=(PIECE, PIECE),
        in_specs=[SMEM_SPEC] + [VMEM_SPEC] * 2,
        name="cut_fore",
        compiler_params=PARAMS,
    )(where, field, factor)


def cut_own(where, field, factor, probe, start):
    return pl.pallas_call(
        cut_own_kernel,
        out_shape=(PIECE, PIECE, WAVE),
        in_specs=[SMEM_SPEC] + [VMEM_SPEC] * 4,
        name="cut_own",
        compiler_params=PARAMS,
    )(where, field, factor, probe, start)


def paste_kernel(where, own_same, own_other, prev_same, prev_other, out):
    row = lax.broadcasted_iota(jnp.int32, (N, N), 0)
    lane = lax.broadcasted_iota(jnp.int32, (N, N), 1)
    out[...] = jnp.zeros(out.shape, F32)

    def paste(source, base, ahead):
        tile = pl.multiple_of(where[base + 1] * N, N)
        after = pl.multiple_of(where[base + 2] * N, N)
        rows = row < where[base] if ahead else row >= where[base]
        first = rows & (lane >= where[base + 3])
        second = rows & (lane < where[base + 3])
        for layer in range(PER_DEVICE):
            for part in range(2):
                value = source[layer, part]
                out[layer, part, :, pl.ds(tile, N)] += jnp.where(first, value, 0.0)
                out[layer, part, :, pl.ds(after, N)] += jnp.where(second, value, 0.0)

    paste(own_same, 0, False)
    paste(own_other, 4, False)
    paste(prev_same, 8, True)
    paste(prev_other, 12, True)


def paste_windows(where, pieces, shape):
    return pl.pallas_call(
        paste_kernel,
        out_shape=jax.ShapeDtypeStruct(shape, F32),
        in_specs=[SMEM_SPEC] + [VMEM_SPEC] * 4,
        name="paste_windows",
        compiler_params=PARAMS,
    )(where, *pieces)


def fetch(place, sources, windows, sems):
    near, up, far_up, far_down, down = sources
    for distance in range(RING):
        chip = (place[1] + distance) % RING
        for slot in range(PER_CHIP):
            if distance == 2:
                source = (far_up if slot < PER_DEVICE else far_down).at[slot % PER_DEVICE]
            else:
                source = (near, up, None, down)[distance].at[slot]
            core = place[2] if slot < PER_DEVICE else 1 - place[2]
            layer = chip * PER_CHIP + core * PER_DEVICE + slot % PER_DEVICE
            pltpu.make_async_copy(source, windows.at[layer], sems.at[layer]).start()


def arrive(source, windows, sems, layer):
    pltpu.make_async_copy(source, windows.at[layer], sems.at[layer]).wait()


def steps(first, count, change, state, windows, trail, sems, source, twiddle, stages):
    def one(step, state):
        layer = first + change * step
        real, imag = state
        if sems is not None:
            arrive(source, windows, sems, layer)
        trail[layer, 0] = real
        trail[layer, 1] = imag
        mixed = times(real, imag, windows[layer, 0], windows[layer, 1])
        return two_sided(*mixed, twiddle, stages)

    return lax.fori_loop(0, count, one, state)


def forward_kernel(section, place, near, up, far_up, far_down, down, wave, twiddle, *rest):
    leaving, saved, windows, trail, stages, sems, out_sem = rest

    @pl.when(place[0] == section)
    def _():
        fetch(place, (near, up, far_up, far_down, down), windows, sems)
        leaving[0], leaving[1] = steps(
            0, PER_STAGE, 1, (wave[0], wave[1]), windows, trail, sems, near.at[0], twiddle, stages
        )
        kept = trail.at[pl.ds(place[1] * PER_CHIP, PER_CHIP)]
        copy = pltpu.make_async_copy(kept, saved, out_sem)
        copy.start()
        copy.wait()


def gradients(place, trail, psi_of, factor, piece, same, other, sems):
    for slot in range(PER_CHIP):
        core = place[2] if slot < PER_DEVICE else 1 - place[2]
        local = core * PER_DEVICE + slot % PER_DEVICE
        layer = place[1] * PER_CHIP + local
        psi_re, psi_im = psi_of(layer, local)
        value = times(trail[layer, 0], trail[layer, 1], psi_re, psi_im)
        real, imag = times(*value, factor[0], factor[1])
        piece[slot, 0] = real.T if slot % 2 else real
        piece[slot, 1] = (-imag).T if slot % 2 else -imag
    copies = (
        pltpu.make_async_copy(piece.at[pl.ds(0, PER_DEVICE)], same, sems.at[0]),
        pltpu.make_async_copy(piece.at[pl.ds(PER_DEVICE, PER_DEVICE)], other, sems.at[1]),
    )
    for copy in copies:
        copy.start()
    for copy in copies:
        copy.wait()


def backward_kernel(section, place, near, up, far_up, far_down, down, wave, saved, *rest):
    twiddle, factor, unused_same, unused_other, leaving, same, other = rest[:7]
    windows, trail, psi, piece, stages, sems, more = rest[7:]

    @pl.when(place[0] == section)
    def _():
        fetch(place, (near, up, far_up, far_down, down), windows, sems)
        load = pltpu.make_async_copy(saved, psi, more.at[2])
        load.start()
        state = (wave[0], wave[1])
        last = PER_STAGE - 1
        leaving[0], leaving[1] = steps(
            last, PER_STAGE, -1, state, windows, trail, sems, near.at[0], twiddle, stages
        )
        load.wait()
        gradients(
            place,
            trail,
            lambda layer, local: (psi[local, 0], psi[local, 1]),
            factor,
            piece,
            same,
            other,
            more,
        )


def turn_kernel(section, place, near, up, far_up, far_down, down, wave, measured, *rest):
    twiddle, factor, into, back, leaving, same, other = rest[:7]
    windows, history, trail, piece, stages, sems, more = rest[7:]

    @pl.when(place[0] == section)
    def _():
        fetch(place, (near, up, far_up, far_down, down), windows, sems)
        last = PER_STAGE - 1
        source = near.at[0]
        state = (wave[0], wave[1])
        state = steps(0, last, 1, state, windows, history, sems, source, twiddle, stages)
        arrive(source, windows, sems, last)
        history[last, 0], history[last, 1] = state
        mixed = times(*state, windows[last, 0], windows[last, 1])
        real, imag = two_sided(*times(*mixed, into[0], into[1]), twiddle, stages)
        misfit = real * real + imag * imag - measured[...]
        state = two_sided(misfit * real, -(misfit * imag), twiddle, stages)
        state = times(*state, back[0], back[1])
        leaving[0], leaving[1] = steps(
            last, PER_STAGE, -1, state, windows, trail, None, source, twiddle, stages
        )
        gradients(
            place,
            trail,
            lambda layer, local: (history[layer, 0], history[layer, 1]),
            factor,
            piece,
            same,
            other,
            more,
        )


def forward_stage(section, place, sources, wave, twiddle):
    return pl.pallas_call(
        functools.partial(forward_kernel, section),
        out_shape=(WAVE, SAVED),
        in_specs=[SMEM_SPEC] + [ANY_SPEC] * 5 + [VMEM_SPEC] * 2,
        out_specs=(VMEM_SPEC, ANY_SPEC),
        scratch_shapes=[
            STACK,
            STACK,
            ROW_STAGES,
            pltpu.SemaphoreType.DMA((PER_STAGE,)),
            pltpu.SemaphoreType.DMA(()),
        ],
        name="forward_stage",
        compiler_params=PARAMS,
    )(place, *sources, wave, twiddle)


def backward_stage(section, place, sources, wave, saved, twiddle, factor, same, other):
    return pl.pallas_call(
        functools.partial(backward_kernel, section),
        out_shape=(WAVE, PIECE, PIECE),
        in_specs=[SMEM_SPEC] + [ANY_SPEC] * 5 + [VMEM_SPEC, ANY_SPEC] + [VMEM_SPEC] * 2
        + [ANY_SPEC] * 2,
        out_specs=(VMEM_SPEC, ANY_SPEC, ANY_SPEC),
        scratch_shapes=[
            STACK,
            STACK,
            CHIP_STACK,
            CHIP_STACK,
            ROW_STAGES,
            pltpu.SemaphoreType.DMA((PER_STAGE,)),
            pltpu.SemaphoreType.DMA((3,)),
        ],
        input_output_aliases={10: 1, 11: 2},
        name="backward_stage",
        compiler_params=PARAMS,
    )(place, *sources, wave, saved, twiddle, factor, same, other)


def turn_stage(section, place, sources, wave, measured, twiddle, factor, into, back):
    return pl.pallas_call(
        functools.partial(turn_kernel, section),
        out_shape=(WAVE, PIECE, PIECE),
        in_specs=[SMEM_SPEC] + [ANY_SPEC] * 5 + [VMEM_SPEC] * 6,
        out_specs=(VMEM_SPEC, ANY_SPEC, ANY_SPEC),
        scratch_shapes=[
            STACK,
            STACK,
            STACK,
            CHIP_STACK,
            ROW_STAGES,
            pltpu.SemaphoreType.DMA((PER_STAGE,)),
            pltpu.SemaphoreType.DMA((2,)),
        ],
        name="turn_stage",
        compiler_params=PARAMS,
    )(place, *sources, wave, measured, twiddle, factor, into, back)


def along_ring(value, steps):
    def target(device):
        stage, rest = divmod(device, RING * CORES)
        chip, core = divmod(rest, CORES)
        return (stage * RING + (chip + steps) % RING) * CORES + core

    pairs = [(device, target(device)) for device in range(STAGES * RING * CORES)]
    return lax.ppermute(value, "depth", pairs)


def along_stages(value, steps):
    count = STAGES * RING * CORES
    pairs = [(device, (device + steps * RING * CORES) % count) for device in range(count)]
    return lax.ppermute(value, "depth", pairs)


def across(value, strips, swap):
    rows, depth = lax.axis_size("pos"), lax.axis_size("depth")
    pairs = []
    for strip in range(rows):
        for device in range(depth):
            other = device ^ 1 if swap else device
            pairs.append((strip * depth + device, (strip + strips) % rows * depth + other))
    return lax.ppermute(value, ("pos", "depth"), pairs)


def corner(offsets, strip_rows):
    tile = offsets[:, 1] // N
    after = jnp.minimum(tile + 1, 3)
    return jnp.stack([offsets[:, 0] % strip_rows, tile, after, offsets[:, 1] % N], axis=1)


def body(object_field, offsets, probe, intensity, tables):
    twiddle, factor, start, into, back, last_factor = tables
    strip_rows = object_field.shape[2]
    depth_here = lax.axis_index("depth")
    core = depth_here % CORES
    chip = depth_here // CORES % RING
    stage = depth_here // (CORES * RING)
    place = jnp.stack([stage, chip, core])

    rows = lax.axis_size("pos")
    before = lax.ppermute(offsets, "pos", [(i, (i + 1) % rows) for i in range(rows)])
    own = corner(offsets, strip_rows)
    prev = corner(before, strip_rows)
    flip = core == 1
    own = jnp.where(flip, own[::-1], own)
    prev = jnp.where(flip, prev[::-1], prev)
    where = jnp.concatenate([own.reshape(-1), prev.reshape(-1)])

    fore_same, fore_other = cut_fore(where, object_field, factor)
    fore_same = across(fore_same, -1, False)
    fore_other = across(fore_other, -1, True)
    own_same, own_other, wave = cut_own(where, object_field, factor, probe, start)
    own_other = across(own_other, 0, True)
    index = jnp.arange(N, dtype=jnp.int32)
    upright = jnp.broadcast_to(index[:, None] >= where[0], (N, N))
    below = jnp.stack([upright, upright.T])[:, None]
    near = jnp.concatenate(
        [jnp.where(below, own_same, fore_same), jnp.where(below, own_other, fore_other)], axis=0
    )
    up = along_ring(near, -1)
    down = along_ring(near, 1)
    far_up = along_ring(up[:PER_DEVICE], -1)
    far_down = along_ring(down[PER_DEVICE:], 1)
    sources = (near, up, far_up, far_down, down)

    kept = []
    for section in range(STAGES - 1):
        wave, saved = forward_stage(section, place, sources, wave, twiddle)
        kept.append(saved)
        wave = along_stages(wave, 1)
    measured = lax.dynamic_index_in_dim(intensity, core, 0, keepdims=False)
    wave, same, other = turn_stage(
        STAGES - 1, place, sources, wave, measured, twiddle, last_factor, into, back
    )
    for section in reversed(range(STAGES - 1)):
        wave = along_stages(wave, -1)
        wave, same, other = backward_stage(
            section, place, sources, wave, kept[section], twiddle, last_factor, same, other
        )
    prev_same = across(same, 1, False)
    prev_other = across(other, 1, True)
    own_other = across(other, 0, True)
    return paste_windows(where, (same, own_other, prev_same, prev_other), object_field.shape)


def solution(mesh):
    mapped = jax.shard_map(
        body,
        mesh=mesh,
        in_specs=(
            P("depth", None, "pos", None),
            P("pos", None),
            P(),
            P("pos", None, None),
            P(),
        ),
        out_specs=P("depth", None, "pos", None),
        check_vma=False,
    )
    tables = make_tables()

    def run(object_field, offsets, probe, intensity):
        constants = tuple(jnp.asarray(table) for table in tables)
        return mapped(object_field, offsets, probe, intensity, constants)

    return run
```

time: 184 us -> 148 us (0.80)
  starting transfers between devices: 75.7 us -> 54.2 us
  Pallas kernels: 32.3 us -> 24.1 us
  waiting for transfers between devices: 67.4 us -> 62.9 us
    ppermute x6, starting transfers between devices: 56.1 us -> 34.5 us  [along_stages(): return lax.ppermute(value, 'depth', pairs)]
    pallas_call x8 -> x9, Pallas kernels: 30.3 us -> 22 us  [the longest x3 9.86 us: backward_stage(): pl.pallas_call(functools.partial(backward_kernel, section), out_shape=(WA...]
    ppermute x6, waiting for transfers between devices: 27 us -> 23.5 us  [along_stages(): return lax.ppermute(value, 'depth', pairs)]
    unnamed x34 -> x24, local copies, waits for them, and re-layouts: 6.27 us -> 5.47 us
  transfers between devices with their start and end apart: 17 -> 17, of which waited for: 12 -> 12; matrix products, arithmetic and copies ran while one was open for 1% -> 0% of each run, Pallas kernels for 0% -> 1%
where the time goes in v2:
time: 148 us
  waiting for transfers between devices  62.9 us (42%)
  starting transfers between devices  54.2 us (37%)
  Pallas kernels  24.1 us (16%)
  local copies, waits for them, and re-layouts  5.83 us (4%)
    ppermute x6, starting transfers between devices, along_stages(): return lax.ppermute(value, 'depth', pairs)  34.5 us
    ppermute x6, waiting for transfers between devices, along_stages(): return lax.ppermute(value, 'depth', pairs)  23.5 us
    ppermute x6, waiting for transfers between devices, across(): return lax.ppermute(value, ('pos', 'depth'), pairs)  19.9 us
    ppermute x4, waiting for transfers between devices, along_ring(): return lax.ppermute(value, 'depth', pairs)  17.9 us
    ppermute x6, starting transfers between devices, across(): return lax.ppermute(value, ('pos', 'depth'), pairs)  11.7 us
    pallas_call x3, Pallas kernels, backward_stage(): pl.pallas_call(functools.partial(backward_kernel, section), out_shape=(WA...  9.86 us
    pallas_call x3, Pallas kernels, forward_stage(): pl.pallas_call(functools.partial(forward_kernel, section), out_shape=(WAV...  9.55 us
    ppermute x4, starting transfers between devices, along_ring(): return lax.ppermute(value, 'depth', pairs)  5.86 us
  transfers between devices with their start and end apart: 17, of which 12 were waited for; matrix products, arithmetic and copies ran while one was open for 0% of the time, Pallas kernels for 1%

profile of v2, /device:TPU:1, one launch (start us, length us, event | category | flops | bytes accessed | tf_op | source)
XLA Modules:
  0.0 147.9 jit_solution(1527953264862077162)
XLA Ops:
  0.0 2.0 %collective-permute-start = (s32[2,2]{1,0:T(2,128)}, s32[2,2]{1,0:T(2,128)S(1)}, u32[]{:S(2)}, u32[]{:S(2)}) collective-permute-start(s32[2,2]{1,0:T(2,128)} %param.11), channel_id=1, source_target_pairs={{0,32},{32,64},{64,96},{96,0},{1,33},{33,65},{65,97},{97,1},{2,34}... | collective-permute-start | bytes 56 | tf_op jit(solution)/shard_map/ppermute | solution.py:427
  2.9 1.5 %collective-permute-done = s32[2,2]{1,0:T(2,128)S(1)} collective-permute-done((s32[2,2]{1,0:T(2,128)}, s32[2,2]{1,0:T(2,128)S(1)}, u32[]{:S(2)}, u32[]{:S(2)}) %collective-permute-start) | collective-permute-done | bytes 48 | tf_op jit(solution)/shard_map/ppermute | solution.py:427
  5.0 1.2 copy-done.2
  6.2 0.9 copy-done.4
  7.9 1.5 %collective-permute-start.1 = (f32[2,2,128,128]{3,2,1,0:T(8,128)S(1)}, f32[2,2,128,128]{3,2,1,0:T(8,128)S(1)}, u32[]{:S(2)}, u32[]{:S(2)}) collective-permute-start(f32[2,2,128,128]{3,2,1,0:T(8,128)S(1)} %get-tuple-element.28), channel_id=1, source_target_pairs={{0,96},{1,97},{2,98},{3,99},{4,100},{5,101},{6,102},{7,103},{8,104... | collective-permute-start | bytes 786440 | tf_op jit(solution)/shard_map/ppermute | solution.py:408
  9.4 2.5 %collective-permute-start.3 = (f32[2,2,128,128]{3,2,1,0:T(8,128)S(1)}, f32[2,2,128,128]{3,2,1,0:T(8,128)S(1)}, u32[]{:S(2)}, u32[]{:S(2)}) collective-permute-start(f32[2,2,128,128]{3,2,1,0:T(8,128)S(1)} %get-tuple-element.30), channel_id=1, source_target_pairs={{0,97},{1,96},{2,99},{3,98},{4,101},{5,100},{6,103},{7,102},{8,105... | collective-permute-start | bytes 786440 | tf_op jit(solution)/shard_map/ppermute | solution.py:408
  13.8 7.8 %collective-permute-done.3 = f32[2,2,128,128]{3,2,1,0:T(8,128)S(1)} collective-permute-done((f32[2,2,128,128]{3,2,1,0:T(8,128)S(1)}, f32[2,2,128,128]{3,2,1,0:T(8,128)S(1)}, u32[]{:S(2)}, u32[]{:S(2)}) %collective-permute-start.3) | collective-permute-done | bytes 262176 | tf_op jit(solution)/shard_map/ppermute | solution.py:408
  21.7 1.6 %collective-permute-start.6 = (f32[4,2,128,128]{3,2,1,0:T(8,128)S(1)}, f32[4,2,128,128]{3,2,1,0:T(8,128)S(1)}, u32[]{:S(2)}, u32[]{:S(2)}) collective-permute-start(f32[4,2,128,128]{3,2,1,0:T(8,128)S(1)} %pad_maximum_fusion.near), channel_id=1, source_target_pairs={{0,2},{1,3},{2,4},{3,5},{4,6},{5,7},{6,0},{7,1},{8,10},{9,11},{10,... | collective-permute-start | bytes 1572872 | tf_op jit(solution)/shard_map/ppermute | solution.py:392
  23.3 1.5 %collective-permute-start.4 = (f32[4,2,128,128]{3,2,1,0:T(8,128)S(1)}, f32[4,2,128,128]{3,2,1,0:T(8,128)S(1)}, u32[]{:S(2)}, u32[]{:S(2)}) collective-permute-start(f32[4,2,128,128]{3,2,1,0:T(8,128)S(1)} %pad_maximum_fusion.near), channel_id=1, source_target_pairs={{0,6},{1,7},{2,0},{3,1},{4,2},{5,3},{6,4},{7,5},{8,14},{9,15},{10,... | collective-permute-start | bytes 1572872 | tf_op jit(solution)/shard_map/ppermute | solution.py:392
  24.8 12.2 %collective-permute-done.6.down = f32[4,2,128,128]{3,2,1,0:T(8,128)S(1)} collective-permute-done((f32[4,2,128,128]{3,2,1,0:T(8,128)S(1)}, f32[4,2,128,128]{3,2,1,0:T(8,128)S(1)}, u32[]{:S(2)}, u32[]{:S(2)}) %collective-permute-start.6) | collective-permute-done | bytes 524320 | tf_op jit(solution)/shard_map/ppermute | solution.py:392
  37.2 2.7 %collective-permute-start.5 = (f32[2,2,128,128]{3,2,1,0:T(8,128)S(1)}, f32[2,2,128,128]{3,2,1,0:T(8,128)S(1)}, u32[]{:S(2)}, u32[]{:S(2)}) collective-permute-start(f32[2,2,128,128]{3,2,1,0:T(8,128)S(1)} %slice.30), channel_id=1, source_target_pairs={{0,6},{1,7},{2,0},{3,1},{4,2},{5,3},{6,4},{7,5},{8,14},{9,15},{10,... | collective-permute-start | bytes 786440 | tf_op jit(solution)/shard_map/ppermute | solution.py:392
  40.0 5.7 %collective-permute-done.7.far_down = f32[2,2,128,128]{3,2,1,0:T(8,128)S(1)} collective-permute-done((f32[2,2,128,128]{3,2,1,0:T(8,128)S(1)}, f32[2,2,128,128]{3,2,1,0:T(8,128)S(1)}, u32[]{:S(2)}, u32[]{:S(2)}) %collective-permute-start.7) | collective-permute-done | bytes 262176 | tf_op jit(solution)/shard_map/ppermute | solution.py:392
  45.7 7.5 %forward_stage.3 = (f32[2,128,128]{2,1,0:T(8,128)S(1)}, f32[4,2,128,128]{3,2,1,0:T(8,128)S(1)}) custom-call(s32[3]{0:T(128)S(1)} %pad_add_fusion.4.place, f32[4,2,128,128]{3,2,1,0:T(8,128)S(1)} %pad_maximum_fusion.near, f32[4,2,128,128]{3,2,1,0:T(8,128)S(1)} %collective-permute-done.4.up, f32[2,2,128,128]{3,2,1,0:T(8,128)S(1)} %collective-permute-done.5.far_up, ...), custom_call_target="tpu_custom_call" | custom-call | tf_op jit(solution)/shard_map/forward_stage/pallas_call | solution.py:326
  53.3 5.0 %collective-permute-done.8.wave = f32[2,128,128]{2,1,0:T(8,128)S(1)} collective-permute-done((f32[2,128,128]{2,1,0:T(8,128)S(1)}, f32[2,128,128]{2,1,0:T(8,128)S(1)}, u32[]{:S(2)}, u32[]{:S(2)}) %collective-permute-start.8) | collective-permute-done | bytes 131104 | tf_op jit(solution)/shard_map/ppermute | solution.py:398
  59.0 5.7 %collective-permute-start.9 = (f32[2,128,128]{2,1,0:T(8,128)S(1)}, f32[2,128,128]{2,1,0:T(8,128)S(1)}, u32[]{:S(2)}, u32[]{:S(2)}) collective-permute-start(f32[2,128,128]{2,1,0:T(8,128)S(1)} %get-tuple-element.33), channel_id=1, source_target_pairs={{0,8},{1,9},{2,10},{3,11},{4,12},{5,13},{6,14},{7,15},{8,16},{9,17... | collective-permute-start | bytes 393224 | tf_op jit(solution)/shard_map/ppermute | solution.py:398
  64.7 1.9 %collective-permute-done.9.wave = f32[2,128,128]{2,1,0:T(8,128)S(1)} collective-permute-done((f32[2,128,128]{2,1,0:T(8,128)S(1)}, f32[2,128,128]{2,1,0:T(8,128)S(1)}, u32[]{:S(2)}, u32[]{:S(2)}) %collective-permute-start.9) | collective-permute-done | bytes 131104 | tf_op jit(solution)/shard_map/ppermute | solution.py:398
  66.6 1.3 forward_stage.5
  68.8 1.9 %collective-permute-start.10 = (f32[2,128,128]{2,1,0:T(8,128)}, f32[2,128,128]{2,1,0:T(8,128)}, u32[]{:S(2)}, u32[]{:S(2)}) collective-permute-start(f32[2,128,128]{2,1,0:T(8,128)} %get-tuple-element.34), channel_id=1, source_target_pairs={{0,8},{1,9},{2,10},{3,11},{4,12},{5,13},{6,14},{7,15},{8,16},{9,17... | collective-permute-start | bytes 393224 | tf_op jit(solution)/shard_map/ppermute | solution.py:398
  70.7 3.5 %collective-permute-done.10.wave = f32[2,128,128]{2,1,0:T(8,128)} collective-permute-done((f32[2,128,128]{2,1,0:T(8,128)}, f32[2,128,128]{2,1,0:T(8,128)}, u32[]{:S(2)}, u32[]{:S(2)}) %collective-permute-start.10) | collective-permute-done | bytes 131104 | tf_op jit(solution)/shard_map/ppermute | solution.py:398
  74.1 0.9 copy-done.7
  75.0 0.9 copy-done.8
  75.9 1.1 turn_stage.1
  77.0 17.9 %collective-permute-start.11 = (f32[2,128,128]{2,1,0:T(8,128)S(1)}, f32[2,128,128]{2,1,0:T(8,128)S(1)}, u32[]{:S(2)}, u32[]{:S(2)}) collective-permute-start(f32[2,128,128]{2,1,0:T(8,128)S(1)} %get-tuple-element.35), channel_id=1, source_target_pairs={{0,24},{1,25},{2,26},{3,27},{4,28},{5,29},{6,30},{7,31},{8,0},{9,1... | collective-permute-start | bytes 393224 | tf_op jit(solution)/shard_map/ppermute | solution.py:398
  94.9 1.9 %collective-permute-done.11.wave = f32[2,128,128]{2,1,0:T(8,128)S(1)} collective-permute-done((f32[2,128,128]{2,1,0:T(8,128)S(1)}, f32[2,128,128]{2,1,0:T(8,128)S(1)}, u32[]{:S(2)}, u32[]{:S(2)}) %collective-permute-start.11) | collective-permute-done | bytes 131104 | tf_op jit(solution)/shard_map/ppermute | solution.py:398
  97.6 3.1 %collective-permute-start.12 = (f32[2,128,128]{2,1,0:T(8,128)S(1)}, f32[2,128,128]{2,1,0:T(8,128)S(1)}, u32[]{:S(2)}, u32[]{:S(2)}) collective-permute-start(f32[2,128,128]{2,1,0:T(8,128)S(1)} %get-tuple-element.39), channel_id=1, source_target_pairs={{0,24},{1,25},{2,26},{3,27},{4,28},{5,29},{6,30},{7,31},{8,0},{9,1... | collective-permute-start | bytes 393224 | tf_op jit(solution)/shard_map/ppermute | solution.py:398
  100.7 2.0 %collective-permute-done.12.wave = f32[2,128,128]{2,1,0:T(8,128)S(1)} collective-permute-done((f32[2,128,128]{2,1,0:T(8,128)S(1)}, f32[2,128,128]{2,1,0:T(8,128)S(1)}, u32[]{:S(2)}, u32[]{:S(2)}) %collective-permute-start.12) | collective-permute-done | bytes 131104 | tf_op jit(solution)/shard_map/ppermute | solution.py:398
  103.4 5.9 %collective-permute-start.13 = (f32[2,128,128]{2,1,0:T(8,128)S(1)}, f32[2,128,128]{2,1,0:T(8,128)S(1)}, u32[]{:S(2)}, u32[]{:S(2)}) collective-permute-start(f32[2,128,128]{2,1,0:T(8,128)S(1)} %get-tuple-element.43), channel_id=1, source_target_pairs={{0,24},{1,25},{2,26},{3,27},{4,28},{5,29},{6,30},{7,31},{8,0},{9,1... | collective-permute-start | bytes 393224 | tf_op jit(solution)/shard_map/ppermute | solution.py:398
  109.3 9.2 %collective-permute-done.13.wave = f32[2,128,128]{2,1,0:T(8,128)S(1)} collective-permute-done((f32[2,128,128]{2,1,0:T(8,128)S(1)}, f32[2,128,128]{2,1,0:T(8,128)S(1)}, u32[]{:S(2)}, u32[]{:S(2)}) %collective-permute-start.13) | collective-permute-done | bytes 131104 | tf_op jit(solution)/shard_map/ppermute | solution.py:398
  118.5 8.4 %backward_stage.5 = (f32[2,128,128]{2,1,0:T(8,128)}, f32[2,2,128,128]{3,2,1,0:T(8,128)S(1)}, f32[2,2,128,128]{3,2,1,0:T(8,128)S(1)}) custom-call(s32[3]{0:T(128)S(1)} %pad_add_fusion.4.place, f32[4,2,128,128]{3,2,1,0:T(8,128)S(1)} %pad_maximum_fusion.near, ...), custom_call_target="tpu_custom_call", output_to_operand_aliasing={{1}: (10, {}), {2}: (11, {})} | custom-call | tf_op jit(solution)/shard_map/backward_stage/pallas_call | solution.py:344
  127.0 7.5 %collective-permute-start.16 = (f32[2,2,128,128]{3,2,1,0:T(8,128)S(1)}, f32[2,2,128,128]{3,2,1,0:T(8,128)S(1)}, u32[]{:S(2)}, u32[]{:S(2)}) collective-permute-start(f32[2,2,128,128]{3,2,1,0:T(8,128)S(1)} %get-tuple-element.48), channel_id=1, source_target_pairs={{0,33},{1,32},{2,35},{3,34},{4,37},{5,36},{6,39},{7,38},{8,41},{9,... | collective-permute-start | bytes 786440 | tf_op jit(solution)/shard_map/ppermute | solution.py:408
  134.5 11.3 %collective-permute-done.16.prev_other = f32[2,2,128,128]{3,2,1,0:T(8,128)S(1)} collective-permute-done((f32[2,2,128,128]{3,2,1,0:T(8,128)S(1)}, f32[2,2,128,128]{3,2,1,0:T(8,128)S(1)}, u32[]{:S(2)}, u32[]{:S(2)}) %collective-permute-start.16) | collective-permute-done | bytes 262176 | tf_op jit(solution)/shard_map/ppermute | solution.py:408
  145.9 2.0 %paste_windows.1 = f32[2,2,128,512]{3,2,1,0:T(8,128)} custom-call(s32[16]{0:T(128)S(1)} %pad_add_fusion.3.where, f32[2,2,128,128]{3,2,1,0:T(8,128)S(1)} %get-tuple-element.47.own_same, f32[2,2,128,128]{3,2,1,0:T(8,128)S(1)} %collective-permute-done.14.own_other, f32[2,2,128,128]{3,2,1,0:T(8,128)S(1)} %collective-permute-done.15.prev_same, ...), custom_call_target="tpu_custom_call" | custom-call | tf_op jit(solution)/shard_map/paste_windows/pallas_call | solution.py:189
  (56 shorter events, 7.4 us)
Async XLA Ops:
  0.0 70.6 %copy-start = (f32[2,128,128]{2,1,0:T(8,128)S(1)}, f32[2,128,128]{2,1,0:T(8,128)}, u32[]{:S(2)}) copy-start(f32[2,128,128]{2,1,0:T(8,128)} %param.13) | copy-start | bytes 393220
  0.0 4.5 %collective-permute-start = (s32[2,2]{1,0:T(2,128)}, s32[2,2]{1,0:T(2,128)S(1)}, u32[]{:S(2)}, u32[]{:S(2)}) collective-permute-start(s32[2,2]{1,0:T(2,128)} %param.11), channel_id=1, source_target_pairs={{0,32},{32,64},{64,96},{96,0},{1,33},{33,65},{65,97},{97,1},{2,34}... | collective-permute-start | bytes 56 | tf_op jit(solution)/shard_map/ppermute | solution.py:427
  2.0 0.7 copy-start.11
  5.0 1.2 copy-start.2
  6.2 0.9 copy-start.4
  7.1 4.8 %copy-start.9 = (f32[2,128,128]{2,1,0:T(8,128)S(1)}, f32[2,128,128]{2,1,0:T(8,128)}, u32[]{:S(2)}) copy-start(f32[2,128,128]{2,1,0:T(8,128)} %probe.1) | copy-start | bytes 393220
  7.1 4.8 %copy-start.10 = (f32[2,128,128]{2,1,0:T(8,128)S(1)}, f32[2,128,128]{2,1,0:T(8,128)}, u32[]{:S(2)}) copy-start(f32[2,128,128]{2,1,0:T(8,128)} %constant.115.clone.start) | copy-start | bytes 393220
  7.9 5.9 %collective-permute-start.1 = (f32[2,2,128,128]{3,2,1,0:T(8,128)S(1)}, f32[2,2,128,128]{3,2,1,0:T(8,128)S(1)}, u32[]{:S(2)}, u32[]{:S(2)}) collective-permute-start(f32[2,2,128,128]{3,2,1,0:T(8,128)S(1)} %get-tuple-element.28), channel_id=1, source_target_pairs={{0,96},{1,97},{2,98},{3,99},{4,100},{5,101},{6,102},{7,103},{8,104... | collective-permute-start | bytes 786440 | tf_op jit(solution)/shard_map/ppermute | solution.py:408
  9.4 12.2 %collective-permute-start.3 = (f32[2,2,128,128]{3,2,1,0:T(8,128)S(1)}, f32[2,2,128,128]{3,2,1,0:T(8,128)S(1)}, u32[]{:S(2)}, u32[]{:S(2)}) collective-permute-start(f32[2,2,128,128]{3,2,1,0:T(8,128)S(1)} %get-tuple-element.30), channel_id=1, source_target_pairs={{0,97},{1,96},{2,99},{3,98},{4,101},{5,100},{6,103},{7,102},{8,105... | collective-permute-start | bytes 786440 | tf_op jit(solution)/shard_map/ppermute | solution.py:408
  12.8 8.8 %collective-permute-start.2 = (f32[2,2,128,128]{3,2,1,0:T(8,128)S(1)}, f32[2,2,128,128]{3,2,1,0:T(8,128)S(1)}, u32[]{:S(2)}, u32[]{:S(2)}) collective-permute-start(f32[2,2,128,128]{3,2,1,0:T(8,128)S(1)} %get-tuple-element.29), channel_id=1, source_target_pairs={{0,1},{1,0},{2,3},{3,2},{4,5},{5,4},{6,7},{7,6},{8,9},{9,8},{10,11... | collective-permute-start | bytes 786440 | tf_op jit(solution)/shard_map/ppermute | solution.py:408
  21.7 15.3 %collective-permute-start.6 = (f32[4,2,128,128]{3,2,1,0:T(8,128)S(1)}, f32[4,2,128,128]{3,2,1,0:T(8,128)S(1)}, u32[]{:S(2)}, u32[]{:S(2)}) collective-permute-start(f32[4,2,128,128]{3,2,1,0:T(8,128)S(1)} %pad_maximum_fusion.near), channel_id=1, source_target_pairs={{0,2},{1,3},{2,4},{3,5},{4,6},{5,7},{6,0},{7,1},{8,10},{9,11},{10,... | collective-permute-start | bytes 1572872 | tf_op jit(solution)/shard_map/ppermute | solution.py:392
  23.3 13.9 %collective-permute-start.4 = (f32[4,2,128,128]{3,2,1,0:T(8,128)S(1)}, f32[4,2,128,128]{3,2,1,0:T(8,128)S(1)}, u32[]{:S(2)}, u32[]{:S(2)}) collective-permute-start(f32[4,2,128,128]{3,2,1,0:T(8,128)S(1)} %pad_maximum_fusion.near), channel_id=1, source_target_pairs={{0,6},{1,7},{2,0},{3,1},{4,2},{5,3},{6,4},{7,5},{8,14},{9,15},{10,... | collective-permute-start | bytes 1572872 | tf_op jit(solution)/shard_map/ppermute | solution.py:392
  37.1 8.6 %collective-permute-start.7 = (f32[2,2,128,128]{3,2,1,0:T(8,128)S(1)}, f32[2,2,128,128]{3,2,1,0:T(8,128)S(1)}, u32[]{:S(2)}, u32[]{:S(2)}) collective-permute-start(f32[2,2,128,128]{3,2,1,0:T(8,128)S(1)} %slice.31), channel_id=1, source_target_pairs={{0,2},{1,3},{2,4},{3,5},{4,6},{5,7},{6,0},{7,1},{8,10},{9,11},{10,... | collective-permute-start | bytes 786440 | tf_op jit(solution)/shard_map/ppermute | solution.py:392
  37.2 8.5 %copy-start.1 = (f32[2,128,128]{2,1,0:T(8,128)S(1)}, f32[2,128,128]{2,1,0:T(8,128)}, u32[]{:S(2)}) copy-start(f32[2,128,128]{2,1,0:T(8,128)} %constant.113.clone.twiddle.rest_0_) | copy-start | bytes 393220
  37.2 8.5 %collective-permute-start.5 = (f32[2,2,128,128]{3,2,1,0:T(8,128)S(1)}, f32[2,2,128,128]{3,2,1,0:T(8,128)S(1)}, u32[]{:S(2)}, u32[]{:S(2)}) collective-permute-start(f32[2,2,128,128]{3,2,1,0:T(8,128)S(1)} %slice.30), channel_id=1, source_target_pairs={{0,6},{1,7},{2,0},{3,1},{4,2},{5,3},{6,4},{7,5},{8,14},{9,15},{10,... | collective-permute-start | bytes 786440 | tf_op jit(solution)/shard_map/ppermute | solution.py:392
  53.2 5.1 %collective-permute-start.8 = (f32[2,128,128]{2,1,0:T(8,128)S(1)}, f32[2,128,128]{2,1,0:T(8,128)S(1)}, u32[]{:S(2)}, u32[]{:S(2)}) collective-permute-start(f32[2,128,128]{2,1,0:T(8,128)S(1)} %get-tuple-element.32), channel_id=1, source_target_pairs={{0,8},{1,9},{2,10},{3,11},{4,12},{5,13},{6,14},{7,15},{8,16},{9,17... | collective-permute-start | bytes 393224 | tf_op jit(solution)/shard_map/ppermute | solution.py:398
  59.0 7.6 %collective-permute-start.9 = (f32[2,128,128]{2,1,0:T(8,128)S(1)}, f32[2,128,128]{2,1,0:T(8,128)S(1)}, u32[]{:S(2)}, u32[]{:S(2)}) collective-permute-start(f32[2,128,128]{2,1,0:T(8,128)S(1)} %get-tuple-element.33), channel_id=1, source_target_pairs={{0,8},{1,9},{2,10},{3,11},{4,12},{5,13},{6,14},{7,15},{8,16},{9,17... | collective-permute-start | bytes 393224 | tf_op jit(solution)/shard_map/ppermute | solution.py:398
  68.0 0.8 copy-start.5
  68.8 5.3 %copy-start.3 = (f32[2,128,128]{2,1,0:T(8,128)S(1)}, f32[2,128,128]{2,1,0:T(8,128)}, u32[]{:S(2)}) copy-start(f32[2,128,128]{2,1,0:T(8,128)} %constant.118.clone.rest_1_) | copy-start | bytes 393220
  68.8 5.3 %collective-permute-start.10 = (f32[2,128,128]{2,1,0:T(8,128)}, f32[2,128,128]{2,1,0:T(8,128)}, u32[]{:S(2)}, u32[]{:S(2)}) collective-permute-start(f32[2,128,128]{2,1,0:T(8,128)} %get-tuple-element.34), channel_id=1, source_target_pairs={{0,8},{1,9},{2,10},{3,11},{4,12},{5,13},{6,14},{7,15},{8,16},{9,17... | collective-permute-start | bytes 393224 | tf_op jit(solution)/shard_map/ppermute | solution.py:398
  70.6 26.2 %copy-start.6 = (f32[4,2,128,128]{3,2,1,0:T(8,128)S(1)}, f32[4,2,128,128]{3,2,1,0:T(8,128)}, u32[]{:S(2)}) copy-start(f32[4,2,128,128]{3,2,1,0:T(8,128)} %copy-done.5) | copy-start | bytes 1572868
  74.1 0.9 copy-start.7
  75.0 0.9 copy-start.8
  77.0 19.8 %collective-permute-start.11 = (f32[2,128,128]{2,1,0:T(8,128)S(1)}, f32[2,128,128]{2,1,0:T(8,128)S(1)}, u32[]{:S(2)}, u32[]{:S(2)}) collective-permute-start(f32[2,128,128]{2,1,0:T(8,128)S(1)} %get-tuple-element.35), channel_id=1, source_target_pairs={{0,24},{1,25},{2,26},{3,27},{4,28},{5,29},{6,30},{7,31},{8,0},{9,1... | collective-permute-start | bytes 393224 | tf_op jit(solution)/shard_map/ppermute | solution.py:398
  97.6 5.1 %collective-permute-start.12 = (f32[2,128,128]{2,1,0:T(8,128)S(1)}, f32[2,128,128]{2,1,0:T(8,128)S(1)}, u32[]{:S(2)}, u32[]{:S(2)}) collective-permute-start(f32[2,128,128]{2,1,0:T(8,128)S(1)} %get-tuple-element.39), channel_id=1, source_target_pairs={{0,24},{1,25},{2,26},{3,27},{4,28},{5,29},{6,30},{7,31},{8,0},{9,1... | collective-permute-start | bytes 393224 | tf_op jit(solution)/shard_map/ppermute | solution.py:398
  103.4 15.1 %collective-permute-start.13 = (f32[2,128,128]{2,1,0:T(8,128)S(1)}, f32[2,128,128]{2,1,0:T(8,128)S(1)}, u32[]{:S(2)}, u32[]{:S(2)}) collective-permute-start(f32[2,128,128]{2,1,0:T(8,128)S(1)} %get-tuple-element.43), channel_id=1, source_target_pairs={{0,24},{1,25},{2,26},{3,27},{4,28},{5,29},{6,30},{7,31},{8,0},{9,1... | collective-permute-start | bytes 393224 | tf_op jit(solution)/shard_map/ppermute | solution.py:398
  126.9 7.6 %collective-permute-start.15 = (f32[2,2,128,128]{3,2,1,0:T(8,128)S(1)}, f32[2,2,128,128]{3,2,1,0:T(8,128)S(1)}, u32[]{:S(2)}, u32[]{:S(2)}) collective-permute-start(f32[2,2,128,128]{3,2,1,0:T(8,128)S(1)} %get-tuple-element.47.own_same), channel_id=1, source_target_pairs={{0,32},{1,33},{2,34},{3,35},{4,36},{5,37},{6,38},{7,39},{8,40},{9,... | collective-permute-start | bytes 786440 | tf_op jit(solution)/shard_map/ppermute | solution.py:408
  127.0 18.8 %collective-permute-start.16 = (f32[2,2,128,128]{3,2,1,0:T(8,128)S(1)}, f32[2,2,128,128]{3,2,1,0:T(8,128)S(1)}, u32[]{:S(2)}, u32[]{:S(2)}) collective-permute-start(f32[2,2,128,128]{3,2,1,0:T(8,128)S(1)} %get-tuple-element.48), channel_id=1, source_target_pairs={{0,33},{1,32},{2,35},{3,34},{4,37},{5,36},{6,39},{7,38},{8,41},{9,... | collective-permute-start | bytes 786440 | tf_op jit(solution)/shard_map/ppermute | solution.py:408
  134.5 11.3 %collective-permute-start.14 = (f32[2,2,128,128]{3,2,1,0:T(8,128)S(1)}, f32[2,2,128,128]{3,2,1,0:T(8,128)S(1)}, u32[]{:S(2)}, u32[]{:S(2)}) collective-permute-start(f32[2,2,128,128]{3,2,1,0:T(8,128)S(1)} %get-tuple-element.48), channel_id=1, source_target_pairs={{0,1},{1,0},{2,3},{3,2},{4,5},{5,4},{6,7},{7,6},{8,9},{9,8},{10,11... | collective-permute-start | bytes 786440 | tf_op jit(solution)/shard_map/ppermute | solution.py:408

commit v3 on v2

v3 whole, which is shorter than its diff:
```python
import functools
import math

import jax
import jax.numpy as jnp
import numpy as np
from jax import lax
from jax.experimental import pallas as pl
from jax.experimental.pallas import tpu as pltpu
from jax.sharding import PartitionSpec as P

N = 128
CORES = 2
RING = 4
STAGES = 4
PER_DEVICE = 2
PER_CHIP = CORES * PER_DEVICE
PER_STAGE = RING * PER_CHIP
PLANE = (2, N, N)
F32 = jnp.float32
PARAMS = pltpu.CompilerParams(vmem_limit_bytes=20 << 20)
GROUP = 8
PAD_ROWS = 128
PITCH = GROUP + 1
TRAIL = pltpu.VMEM((PER_STAGE + 1,) + PLANE, F32)
ROW_STAGES = pltpu.VMEM((2, 2, 160, N), F32)
WAVE = jax.ShapeDtypeStruct(PLANE, F32)
PIECE = jax.ShapeDtypeStruct((PER_DEVICE,) + PLANE, F32)
SAVED = jax.ShapeDtypeStruct((PER_CHIP,) + PLANE, F32)
STACK = jax.ShapeDtypeStruct((PER_STAGE,) + PLANE, F32)
SMEM_SPEC = pl.BlockSpec(memory_space=pltpu.SMEM)
VMEM_SPEC = pl.BlockSpec(memory_space=pltpu.VMEM)
ANY_SPEC = pl.BlockSpec(memory_space=pl.ANY)


def make_tables():
    index = np.arange(N)
    turn = np.exp(1j * np.pi * (index * index % (2 * N)) / N)
    chirp = np.outer(turn, turn)
    first, second = np.divmod(index, GROUP)
    twiddle = np.exp(-2j * np.pi * first * second / N)[:, None] * np.ones((1, N))
    tables = (twiddle, np.conj(chirp))
    return tuple(np.stack([t.real, t.imag]).astype(np.float32) for t in tables)


def times(first_re, first_im, second_re, second_im):
    return (
        first_re * second_re - first_im * second_im,
        first_re * second_im + first_im * second_re,
    )


def rotate(value, numerator, count):
    real, imag = value
    if numerator == 0:
        return value
    if numerator * 4 == count:
        return imag, -real
    half = math.sqrt(0.5)
    if numerator * 8 == count:
        return (real + imag) * half, (imag - real) * half
    if numerator * 8 == 3 * count:
        return (imag - real) * half, -(real + imag) * half
    cosine = math.cos(2.0 * math.pi * numerator / count)
    sine = -math.sin(2.0 * math.pi * numerator / count)
    return real * cosine - imag * sine, real * sine + imag * cosine


def transform(values):
    count = len(values)
    if count == 1:
        return values
    even, odd = transform(values[0::2]), transform(values[1::2])
    result = [None] * count
    for k in range(count // 2):
        moved = rotate(odd[k], k, count)
        result[k] = (even[k][0] + moved[0], even[k][1] + moved[1])
        result[k + count // 2] = (even[k][0] - moved[0], even[k][1] - moved[1])
    return result


def transform_rows(real, imag, twiddle, stage, put):
    groups = [
        (real[GROUP * k : GROUP * (k + 1)], imag[GROUP * k : GROUP * (k + 1)])
        for k in range(N // GROUP)
    ]
    for k, value in enumerate(transform(groups)):
        rows = pl.ds(GROUP * k, GROUP)
        if k:
            value = times(*value, twiddle[0, rows], twiddle[1, rows])
        rows = pl.ds(PITCH * k, GROUP)
        stage[0, rows], stage[1, rows] = value
    for part in range(2):
        picked = [pl.ds(PITCH * GROUP * part + k, GROUP, stride=PITCH) for k in range(GROUP)]
        done = transform([(stage[0, rows], stage[1, rows]) for rows in picked])
        for k in range(GROUP):
            put(2 * k + part, done[k])


def advance(real, imag, target, twiddle, stages):
    rows = [None] * (N // GROUP)
    transform_rows(real, imag, twiddle, stages.at[0], rows.__setitem__)
    real, imag = (jnp.concatenate([row[k] for row in rows], axis=0).T for k in range(2))

    def put(k, value):
        place = pl.ds(GROUP * k, GROUP)
        target[0, place], target[1, place] = value

    transform_rows(real, imag, twiddle, stages.at[1], put)


def corner(offsets, position):
    row = offsets[position, 0]
    column = offsets[position, 1]
    tile = column // N
    after = pl.multiple_of(jnp.minimum(tile + 1, 3) * N, N)
    return row % N, pl.multiple_of(tile * N, N), after, column % N


def squared(chirp):
    real, imag = chirp[0], chirp[1]
    return real * real - imag * imag, -2.0 * real * imag


def cut(offsets, position, field, chirp, targets):
    lane = lax.broadcasted_iota(jnp.int32, (N, N), 1)
    unused, tile, after, shift = corner(offsets, position)
    wrapped = lane < shift
    real, imag = squared(chirp)
    factor = (imag * (1.0 / N), real * (-1.0 / N))
    for layer in range(PER_DEVICE):
        value = [
            jnp.where(
                wrapped,
                field[layer, part, :, pl.ds(after, N)],
                field[layer, part, :, pl.ds(tile, N)],
            )
            for part in range(2)
        ]
        value = times(*value, *factor)
        for part in range(2):
            targets[layer][part] = value[part].T if layer % 2 else value[part]


def here():
    device = lax.axis_index("depth")
    return device // (CORES * RING), device // CORES % RING, device % CORES


def cut_own_kernel(offsets, field, chirp, probe, same0, same1, other, wave, *copies):
    core = here()[2]
    cut(offsets, core, field, chirp, (same0, same1))
    cut(offsets, 1 - core, field, chirp, [other.at[k] for k in range(PER_DEVICE)])
    row, unused, unused, shift = corner(offsets, core)
    rolled = [pltpu.roll(pltpu.roll(probe[k], row, 0), shift, 1) for k in range(2)]
    real, imag = times(*rolled, chirp[0], chirp[1])
    wave[0] = -imag
    wave[1] = real
    copies[0][...] = field[...]
    copies[1][...] = chirp[...]


def cut_fore_kernel(before, field, chirp, *targets):
    core = here()[2]
    cut(before, core, field, chirp, targets[:2])
    cut(before, 1 - core, field, chirp, targets[2:])


def cut_own(offsets, field, chirp, probe):
    return pl.pallas_call(
        cut_own_kernel,
        out_shape=(WAVE, WAVE, PIECE, WAVE, jax.ShapeDtypeStruct(field.shape, F32), WAVE),
        in_specs=[SMEM_SPEC] + [VMEM_SPEC] * 3,
        name="cut_own",
        compiler_params=PARAMS,
    )(offsets, field, chirp, probe)


def cut_fore(before, field, chirp):
    return pl.pallas_call(
        cut_fore_kernel,
        out_shape=(WAVE,) * 4,
        in_specs=[SMEM_SPEC] + [VMEM_SPEC] * 2,
        name="cut_fore",
        compiler_params=PARAMS,
    )(before, field, chirp)


def paste(offsets, position, value, target, ahead):
    row = lax.broadcasted_iota(jnp.int32, (N, N), 0)
    lane = lax.broadcasted_iota(jnp.int32, (N, N), 1)
    top, tile, after, shift = corner(offsets, position)
    rows = row < top if ahead else row >= top
    target[:, pl.ds(tile, N)] += jnp.where(rows & (lane >= shift), value, 0.0)
    target[:, pl.ds(after, N)] += jnp.where(rows & (lane < shift), value, 0.0)


def paste_kernel(offsets, before, same, other, prev_same, prev_other, out, total, sems):
    core = here()[2]
    copies = []
    total[...] = jnp.zeros(total.shape, F32)
    for layer in range(PER_DEVICE):
        for part in range(2):
            target = total.at[layer, part]
            paste(offsets, core, same[layer, part], target, False)
            paste(offsets, 1 - core, other[layer, part], target, False)
            paste(before, core, prev_same[layer, part], target, True)
            paste(before, 1 - core, prev_other[layer, part], target, True)
            copy = pltpu.make_async_copy(target, out.at[layer, part], sems.at[layer, part])
            copy.start()
            copies.append(copy)
    for copy in copies:
        copy.wait()


def paste_windows(offsets, before, pieces, shape):
    return pl.pallas_call(
        paste_kernel,
        out_shape=jax.ShapeDtypeStruct(shape, F32),
        in_specs=[SMEM_SPEC] * 2 + [VMEM_SPEC] * 4,
        out_specs=ANY_SPEC,
        scratch_shapes=[pltpu.VMEM(shape, F32), pltpu.SemaphoreType.DMA((PER_DEVICE, 2))],
        name="paste_windows",
        compiler_params=PARAMS,
    )(offsets, before, *pieces)


def steps(first, count, change, windows, trail, twiddle, stages):
    def one(step, unused):
        layer = first + change * step
        slot = layer if change > 0 else layer + 1
        mixed = times(trail[slot, 0], trail[slot, 1], windows[layer, 0], windows[layer, 1])
        advance(*mixed, trail.at[slot + change], twiddle, stages)
        return unused

    lax.fori_loop(0, count, one, 0)


def keep(chip, trail, saved):
    for slot in range(PER_CHIP):
        saved[slot] = trail[chip * PER_CHIP + slot]


def first_kernel(near0, near1, up0, up1, far0, far1, down0, down1, wave, twiddle, *rest):
    leaving, saved, windows, trail, stages = rest
    stage, chip, core = here()
    sources = ((near0, near1), (up0, up1), (far0, far1), (down0, down1))

    @pl.when(stage == 0)
    def _():
        trail[0] = wave[...]

        def one_core(step, unused):
            owner, owner_core = step // CORES, step % CORES
            slot = (owner_core + core) % CORES
            for distance in range(RING):

                @pl.when((owner - chip + RING) % RING == distance)
                def _():
                    for parity in range(PER_DEVICE):
                        layer = step * PER_DEVICE + parity
                        window = sources[distance][parity][slot]
                        windows[layer] = window
                        mixed = times(trail[layer, 0], trail[layer, 1], window[0], window[1])
                        advance(*mixed, trail.at[layer + 1], twiddle, stages)

            return unused

        lax.fori_loop(0, RING * CORES, one_core, 0)
        leaving[...] = trail[PER_STAGE]
        keep(chip, trail, saved)

    @pl.when(stage != 0)
    def _():
        for distance in range(RING):
            owner = (chip + distance) % RING
            for slot in range(CORES):
                owner_core = core if slot == 0 else 1 - core
                for parity in range(PER_DEVICE):
                    layer = owner * PER_CHIP + owner_core * PER_DEVICE + parity
                    windows[layer] = sources[distance][parity][slot]


def forward_kernel(section, windows, wave, saved_in, twiddle, leaving, saved, trail, stages):
    stage, chip, core = here()

    @pl.when(stage == section)
    def _():
        trail[0] = wave[...]
        steps(0, PER_STAGE, 1, windows, trail, twiddle, stages)
        leaving[...] = trail[PER_STAGE]
        keep(chip, trail, saved)

    @pl.when(stage != section)
    def _():
        saved[...] = saved_in[...]


def gradients(chip, core, trail, psi_of, chirp, same, other):
    factor = squared(chirp)
    for slot in range(PER_CHIP):
        mine = slot < PER_DEVICE
        local = (core if mine else 1 - core) * PER_DEVICE + slot % PER_DEVICE
        layer = chip * PER_CHIP + local
        psi_re, psi_im = psi_of(layer, local)
        value = times(trail[layer + 1, 0], trail[layer + 1, 1], psi_re, psi_im)
        real, imag = times(*value, *factor)
        target = (same if mine else other).at[slot % PER_DEVICE]
        target[0] = (-real).T if slot % 2 else -real
        target[1] = imag.T if slot % 2 else imag


def backward_kernel(section, windows, wave, saved, twiddle, chirp, same_in, other_in, *rest):
    leaving, same, other, trail, stages = rest
    stage, chip, core = here()

    @pl.when(stage == section)
    def _():
        trail[PER_STAGE] = wave[...]
        last = PER_STAGE - 1
        steps(last, PER_STAGE, -1, windows, trail, twiddle, stages)
        leaving[...] = trail[0]
        gradients(
            chip,
            core,
            trail,
            lambda layer, local: (saved[local, 0], saved[local, 1]),
            chirp,
            same,
            other,
        )

    @pl.when(stage != section)
    def _():
        same[...] = same_in[...]
        other[...] = other_in[...]


def last_backward_kernel(windows, wave, saved, twiddle, chirp, same_in, other_in, *rest):
    same, other, trail, stages = rest
    stage, chip, core = here()

    @pl.when(stage == 0)
    def _():
        trail[PER_STAGE] = wave[...]
        last = PER_STAGE - 1
        steps(last, last, -1, windows, trail, twiddle, stages)
        gradients(
            chip,
            core,
            trail,
            lambda layer, local: (saved[local, 0], saved[local, 1]),
            chirp,
            same,
            other,
        )

    @pl.when(stage != 0)
    def _():
        same[...] = same_in[...]
        other[...] = other_in[...]


def turn_kernel(section, windows, wave, measured, twiddle, chirp, *rest):
    leaving, same, other, history, trail, stages = rest
    stage, chip, core = here()

    @pl.when(stage == section)
    def _():
        last = PER_STAGE - 1
        history[0] = wave[...]
        steps(0, last, 1, windows, history, twiddle, stages)
        mixed = times(history[last, 0], history[last, 1], windows[last, 0], windows[last, 1])
        mixed = times(*mixed, chirp[0], chirp[1])
        advance(*mixed, history.at[PER_STAGE], twiddle, stages)
        real, imag = history[PER_STAGE, 0], history[PER_STAGE, 1]
        misfit = real * real + imag * imag - measured[...]
        target = trail.at[PER_STAGE]
        advance(misfit * real, -(misfit * imag), target, twiddle, stages)
        real, imag = times(target[0], target[1], chirp[0], chirp[1])
        target[0] = imag * (-1.0 / N)
        target[1] = real * (1.0 / N)
        steps(last, PER_STAGE, -1, windows, trail, twiddle, stages)
        leaving[...] = trail[0]
        gradients(
            chip,
            core,
            trail,
            lambda layer, local: (history[layer, 0], history[layer, 1]),
            chirp,
            same,
            other,
        )


def first_stage(sources, wave, twiddle):
    return pl.pallas_call(
        first_kernel,
        out_shape=(WAVE, SAVED, STACK),
        in_specs=[VMEM_SPEC] * 10,
        scratch_shapes=[TRAIL, ROW_STAGES],
        name="first_stage",
        compiler_params=PARAMS,
    )(*sources, wave, twiddle)


def forward_stage(section, windows, wave, saved, twiddle):
    return pl.pallas_call(
        functools.partial(forward_kernel, section),
        out_shape=(WAVE, SAVED),
        scratch_shapes=[TRAIL, ROW_STAGES],
        name="forward_stage",
        compiler_params=PARAMS,
    )(windows, wave, saved, twiddle)


def backward_stage(section, *operands):
    last = section == 0
    return pl.pallas_call(
        last_backward_kernel if last else functools.partial(backward_kernel, section),
        out_shape=(PIECE, PIECE) if last else (WAVE, PIECE, PIECE),
        scratch_shapes=[TRAIL, ROW_STAGES],
        name="backward_stage",
        compiler_params=PARAMS,
    )(*operands)


def turn_stage(section, *operands):
    return pl.pallas_call(
        functools.partial(turn_kernel, section),
        out_shape=(WAVE, PIECE, PIECE),
        scratch_shapes=[TRAIL, TRAIL, ROW_STAGES],
        name="turn_stage",
        compiler_params=PARAMS,
    )(*operands)


def along_ring(value, steps):
    def target(device):
        stage, rest = divmod(device, RING * CORES)
        chip, core = divmod(rest, CORES)
        return (stage * RING + (chip + steps) % RING) * CORES + core

    pairs = [(device, target(device)) for device in range(STAGES * RING * CORES)]
    return lax.ppermute(value, "depth", pairs)


def along_stages(value, steps):
    count = STAGES * RING * CORES
    pairs = [(device, (device + steps * RING * CORES) % count) for device in range(count)]
    return lax.ppermute(value, "depth", pairs)


def across(value, strips, swap):
    rows, depth = lax.axis_size("pos"), lax.axis_size("depth")
    pairs = []
    for strip in range(rows):
        for device in range(depth):
            other = device ^ 1 if swap else device
            pairs.append((strip * depth + device, (strip + strips) % rows * depth + other))
    return lax.ppermute(value, ("pos", "depth"), pairs)


def body(object_field, offsets, probe, intensity, tables):
    twiddle, chirp = tables
    core = lax.axis_index("depth") % CORES
    rows = lax.axis_size("pos")
    padded = jnp.pad(offsets, ((0, PAD_ROWS - offsets.shape[0]), (0, N - offsets.shape[1])))
    before = lax.ppermute(padded, "pos", [(i, (i + 1) % rows) for i in range(rows)])
    before = before[:GROUP]

    own = cut_own(offsets, object_field, chirp, probe)
    own_same, wave, field = own[:2], own[3], own[4]
    own_other = across(own[2], 0, True)
    fore = cut_fore(before, field, own[5])
    fore_same = [across(fore[parity], -1, False) for parity in range(PER_DEVICE)]
    fore_other = [across(fore[2 + parity], -1, True) for parity in range(PER_DEVICE)]
    row_here = jnp.where(core == 0, offsets[0, 0], offsets[1, 0]) % N

    near, up, down = [], [], []
    index = jnp.arange(N, dtype=jnp.int32)
    for parity in range(PER_DEVICE):
        axis = (None, slice(None)) if parity else (slice(None), None)
        below = jnp.broadcast_to((index >= row_here)[axis], PLANE)
        near.append(
            jnp.stack(
                [
                    jnp.where(below, own_same[parity], fore_same[parity]),
                    jnp.where(below, own_other[parity], fore_other[parity]),
                ]
            )
        )
        up.append(along_ring(near[-1], -1))
        down.append(along_ring(near[-1], 1))
    far = [along_ring(up[0], -1), along_ring(down[1], 1)]

    wave, saved, windows = first_stage((*near, *up, *far, *down), wave, twiddle)
    for section in range(1, STAGES - 1):
        wave = along_stages(wave, 1)
        wave, saved = forward_stage(section, windows, wave, saved, twiddle)
    wave = along_stages(wave, 1)
    measured = lax.dynamic_index_in_dim(intensity, core, 0, keepdims=False)
    wave, same, other = turn_stage(STAGES - 1, windows, wave, measured, twiddle, chirp)
    for section in reversed(range(1, STAGES - 1)):
        wave = along_stages(wave, -1)
        wave, same, other = backward_stage(
            section, windows, wave, saved, twiddle, chirp, same, other
        )
    wave = along_stages(wave, -1)
    same, other = backward_stage(0, windows, wave, saved, twiddle, chirp, same, other)
    prev_same = across(same, 1, False)
    prev_other = across(other, 1, True)
    other, prev_same = lax.optimization_barrier((other, prev_same))
    own_other = across(other, 0, True)
    pieces = (same, own_other, prev_same, prev_other)
    return paste_windows(offsets, before, pieces, object_field.shape)


def solution(mesh):
    mapped = jax.shard_map(
        body,
        mesh=mesh,
        in_specs=(
            P("depth", None, "pos", None),
            P("pos", None),
            P(),
            P("pos", None, None),
            P(),
        ),
        out_specs=P("depth", None, "pos", None),
        check_vma=False,
    )
    tables = make_tables()

    def run(object_field, offsets, probe, intensity):
        constants = tuple(jnp.asarray(table) for table in tables)
        return mapped(object_field, offsets, probe, intensity, constants)

    return run
```

time: 148 us -> 114 us (0.77)
  waiting for transfers between devices: 62.9 us -> 44 us
  Pallas kernels: 24.1 us -> 11.2 us
  starting transfers between devices: 54.2 us -> 51.8 us
    ppermute x6, starting transfers between devices: 34.5 us -> 21.9 us  [along_stages(): return lax.ppermute(value, 'depth', pairs)]
    pallas_call x3 -> x2, Pallas kernels: 9.55 us -> 0.07 us  [forward_stage(): pl.pallas_call(functools.partial(forward_kernel, section), out_shape=(WAV...]
    ppermute x6 -> x8, waiting for transfers between devices: 19.9 us -> 10.8 us  [across(): return lax.ppermute(value, ('pos', 'depth'), pairs)]
    ppermute x6 -> x8, starting transfers between devices: 11.7 us -> 20.8 us  [across(): return lax.ppermute(value, ('pos', 'depth'), pairs)]
    ppermute x4 -> x6, waiting for transfers between devices: 17.9 us -> 13.2 us  [along_ring(): return lax.ppermute(value, 'depth', pairs)]
    ppermute x6, waiting for transfers between devices: 23.5 us -> 20 us  [along_stages(): return lax.ppermute(value, 'depth', pairs)]
    pallas_call x5 -> x6, Pallas kernels: 11.4 us -> 9.28 us  [the longest x1 3.91 us: first_stage(): pl.pallas_call(first_kernel, out_shape=(WAVE, SAVED, STACK), in_specs=[VM...]
    unnamed x24 -> x16, local copies, waits for them, and re-layouts: 5.47 us -> 3.73 us
  transfers between devices with their start and end apart: 17 -> 21, of which waited for: 12 -> 14; matrix products, arithmetic and copies ran while one was open for 0% -> 0% of each run, Pallas kernels for 1% -> 1%
where the time goes in v3:
time: 114 us
  starting transfers between devices  51.8 us (45%)
  waiting for transfers between devices  44 us (39%)
  Pallas kernels  11.2 us (10%)
  local copies, waits for them, and re-layouts  4.98 us (4%)
  between operations  1.42 us (1%)
    ppermute x6, starting transfers between devices, along_stages(): return lax.ppermute(value, 'depth', pairs)  21.9 us
    ppermute x8, starting transfers between devices, across(): return lax.ppermute(value, ('pos', 'depth'), pairs)  20.8 us
    ppermute x6, waiting for transfers between devices, along_stages(): return lax.ppermute(value, 'depth', pairs)  20 us
    ppermute x6, waiting for transfers between devices, along_ring(): return lax.ppermute(value, 'depth', pairs)  13.2 us
    ppermute x8, waiting for transfers between devices, across(): return lax.ppermute(value, ('pos', 'depth'), pairs)  10.8 us
    ppermute x6, starting transfers between devices, along_ring(): return lax.ppermute(value, 'depth', pairs)  7.03 us
    pallas_call x1, Pallas kernels, first_stage(): pl.pallas_call(first_kernel, out_shape=(WAVE, SAVED, STACK), in_specs=[VM...  3.91 us
    unnamed x16, local copies, waits for them, and re-layouts  3.73 us
  transfers between devices with their start and end apart: 21, of which 14 were waited for; matrix products, arithmetic and copies ran while one was open for 0% of the time, Pallas kernels for 1%

profile of v3, /device:TPU:1, one launch (start us, length us, event | category | flops | bytes accessed | tf_op | source)
XLA Modules:
  0.0 113.6 jit_solution(4788754938057845321)
XLA Ops:
  0.7 2.0 %collective-permute-start = (s32[128,128]{1,0:T(8,128)S(1)}, s32[128,128]{1,0:T(8,128)S(1)}, u32[]{:S(2)}, u32[]{:S(2)}) collective-permute-start(s32[128,128]{1,0:T(8,128)S(1)} %pad.4), channel_id=1, source_target_pairs={{0,32},{32,64},{64,96},{96,0},{1,33},{33,65},{65,97},{97,1},{2,34}... | collective-permute-start | bytes 196616 | tf_op jit(solution)/shard_map/ppermute | solution.py:469
  3.7 1.2 %copy-done.4 = f32[2,2,128,512]{3,2,1,0:T(8,128)S(1)} copy-done((f32[2,2,128,512]{3,2,1,0:T(8,128)S(1)}, f32[2,2,128,512]{3,2,1,0:T(8,128)}, u32[]{:S(2)}) %copy-start.4) | copy-done | bytes 1048600
  9.2 1.4 %collective-permute-start.1 = (f32[2,128,128]{2,1,0:T(8,128)S(1)}, f32[2,128,128]{2,1,0:T(8,128)S(1)}, u32[]{:S(2)}, u32[]{:S(2)}) collective-permute-start(f32[2,128,128]{2,1,0:T(8,128)S(1)} %get-tuple-element.38), channel_id=1, source_target_pairs={{0,96},{1,97},{2,98},{3,99},{4,100},{5,101},{6,102},{7,103},{8,104... | collective-permute-start | bytes 393224 | tf_op jit(solution)/shard_map/ppermute | solution.py:461
  10.7 1.6 %collective-permute-start.3 = (f32[2,128,128]{2,1,0:T(8,128)S(1)}, f32[2,128,128]{2,1,0:T(8,128)S(1)}, u32[]{:S(2)}, u32[]{:S(2)}) collective-permute-start(f32[2,128,128]{2,1,0:T(8,128)S(1)} %get-tuple-element.40), channel_id=1, source_target_pairs={{0,97},{1,96},{2,99},{3,98},{4,101},{5,100},{6,103},{7,102},{8,105... | collective-permute-start | bytes 393224 | tf_op jit(solution)/shard_map/ppermute | solution.py:461
  15.2 2.5 %collective-permute-done.3 = f32[2,128,128]{2,1,0:T(8,128)S(1)} collective-permute-done((f32[2,128,128]{2,1,0:T(8,128)S(1)}, f32[2,128,128]{2,1,0:T(8,128)S(1)}, u32[]{:S(2)}, u32[]{:S(2)}) %collective-permute-start.3) | collective-permute-done | bytes 131104 | tf_op jit(solution)/shard_map/ppermute | solution.py:461
  17.7 2.3 %collective-permute-done.4 = f32[2,128,128]{2,1,0:T(8,128)S(1)} collective-permute-done((f32[2,128,128]{2,1,0:T(8,128)S(1)}, f32[2,128,128]{2,1,0:T(8,128)S(1)}, u32[]{:S(2)}, u32[]{:S(2)}) %collective-permute-start.4) | collective-permute-done | bytes 131104 | tf_op jit(solution)/shard_map/ppermute | solution.py:461
  20.0 2.9 %collective-permute-done.5 = f32[2,128,128]{2,1,0:T(8,128)S(1)} collective-permute-done((f32[2,128,128]{2,1,0:T(8,128)S(1)}, f32[2,128,128]{2,1,0:T(8,128)S(1)}, u32[]{:S(2)}, u32[]{:S(2)}) %collective-permute-start.5) | collective-permute-done | bytes 131104 | tf_op jit(solution)/shard_map/ppermute | solution.py:461
  23.1 1.4 %collective-permute-start.9 = (f32[2,2,128,128]{3,2,1,0:T(8,128)S(1)}, f32[2,2,128,128]{3,2,1,0:T(8,128)S(1)}, u32[]{:S(2)}, u32[]{:S(2)}) collective-permute-start(f32[2,2,128,128]{3,2,1,0:T(8,128)S(1)} %pad_maximum_fusion.1.near1), channel_id=1, source_target_pairs={{0,2},{1,3},{2,4},{3,5},{4,6},{5,7},{6,0},{7,1},{8,10},{9,11},{10,... | collective-permute-start | bytes 786440 | tf_op jit(solution)/shard_map/ppermute | solution.py:445
  24.4 1.5 %collective-permute-start.6 = (f32[2,2,128,128]{3,2,1,0:T(8,128)S(1)}, f32[2,2,128,128]{3,2,1,0:T(8,128)S(1)}, u32[]{:S(2)}, u32[]{:S(2)}) collective-permute-start(f32[2,2,128,128]{3,2,1,0:T(8,128)S(1)} %pad_maximum_fusion.near0), channel_id=1, source_target_pairs={{0,6},{1,7},{2,0},{3,1},{4,2},{5,3},{6,4},{7,5},{8,14},{9,15},{10,... | collective-permute-start | bytes 786440 | tf_op jit(solution)/shard_map/ppermute | solution.py:445
  26.0 1.4 %collective-permute-start.7 = (f32[2,2,128,128]{3,2,1,0:T(8,128)S(1)}, f32[2,2,128,128]{3,2,1,0:T(8,128)S(1)}, u32[]{:S(2)}, u32[]{:S(2)}) collective-permute-start(f32[2,2,128,128]{3,2,1,0:T(8,128)S(1)} %pad_maximum_fusion.1.near1), channel_id=1, source_target_pairs={{0,6},{1,7},{2,0},{3,1},{4,2},{5,3},{6,4},{7,5},{8,14},{9,15},{10,... | collective-permute-start | bytes 786440 | tf_op jit(solution)/shard_map/ppermute | solution.py:445
  27.4 4.7 %collective-permute-done.9.down1 = f32[2,2,128,128]{3,2,1,0:T(8,128)S(1)} collective-permute-done((f32[2,2,128,128]{3,2,1,0:T(8,128)S(1)}, f32[2,2,128,128]{3,2,1,0:T(8,128)S(1)}, u32[]{:S(2)}, u32[]{:S(2)}) %collective-permute-start.9) | collective-permute-done | bytes 262176 | tf_op jit(solution)/shard_map/ppermute | solution.py:445
  32.1 2.7 %collective-permute-start.8 = (f32[2,2,128,128]{3,2,1,0:T(8,128)S(1)}, f32[2,2,128,128]{3,2,1,0:T(8,128)S(1)}, u32[]{:S(2)}, u32[]{:S(2)}) collective-permute-start(f32[2,2,128,128]{3,2,1,0:T(8,128)S(1)} %collective-permute-done.6.up0), channel_id=1, source_target_pairs={{0,6},{1,7},{2,0},{3,1},{4,2},{5,3},{6,4},{7,5},{8,14},{9,15},{10,... | collective-permute-start | bytes 786440 | tf_op jit(solution)/shard_map/ppermute | solution.py:445
  34.8 2.7 %collective-permute-done.7.up1 = f32[2,2,128,128]{3,2,1,0:T(8,128)S(1)} collective-permute-done((f32[2,2,128,128]{3,2,1,0:T(8,128)S(1)}, f32[2,2,128,128]{3,2,1,0:T(8,128)S(1)}, u32[]{:S(2)}, u32[]{:S(2)}) %collective-permute-start.7) | collective-permute-done | bytes 262176 | tf_op jit(solution)/shard_map/ppermute | solution.py:445
  37.7 5.6 %collective-permute-done.10.far1 = f32[2,2,128,128]{3,2,1,0:T(8,128)S(1)} collective-permute-done((f32[2,2,128,128]{3,2,1,0:T(8,128)S(1)}, f32[2,2,128,128]{3,2,1,0:T(8,128)S(1)}, u32[]{:S(2)}, u32[]{:S(2)}) %collective-permute-start.10) | collective-permute-done | bytes 262176 | tf_op jit(solution)/shard_map/ppermute | solution.py:445
  43.4 3.9 %first_stage.1 = (f32[2,128,128]{2,1,0:T(8,128)S(1)}, f32[4,2,128,128]{3,2,1,0:T(8,128)S(1)}, f32[16,2,128,128]{3,2,1,0:T(8,128)S(1)}) custom-call(f32[2,2,128,128]{3,2,1,0:T(8,128)S(1)} %pad_maximum_fusion.near0, f32[2,2,128,128]{3,2,1,0:T(8,128)S(1)} %pad_maximum_fusion.1.near1, f32[2,2,128,128]{3,2,1,0:T(8,128)S(1)} %collective-permute-done.6.up0, ...), custom_call_target="tpu_custom_call" | custom-call | tf_op jit(solution)/shard_map/first_stage/pallas_call | solution.py:397
  47.4 5.0 %collective-permute-done.12.wave = f32[2,128,128]{2,1,0:T(8,128)S(1)} collective-permute-done((f32[2,128,128]{2,1,0:T(8,128)S(1)}, f32[2,128,128]{2,1,0:T(8,128)S(1)}, u32[]{:S(2)}, u32[]{:S(2)}) %collective-permute-start.12) | collective-permute-done | bytes 131104 | tf_op jit(solution)/shard_map/ppermute | solution.py:451
  52.4 2.9 %collective-permute-start.13 = (f32[2,128,128]{2,1,0:T(8,128)S(1)}, f32[2,128,128]{2,1,0:T(8,128)S(1)}, u32[]{:S(2)}, u32[]{:S(2)}) collective-permute-start(f32[2,128,128]{2,1,0:T(8,128)S(1)} %get-tuple-element.48), channel_id=1, source_target_pairs={{0,8},{1,9},{2,10},{3,11},{4,12},{5,13},{6,14},{7,15},{8,16},{9,17... | collective-permute-start | bytes 393224 | tf_op jit(solution)/shard_map/ppermute | solution.py:451
  55.3 2.2 %collective-permute-done.13.wave = f32[2,128,128]{2,1,0:T(8,128)S(1)} collective-permute-done((f32[2,128,128]{2,1,0:T(8,128)S(1)}, f32[2,128,128]{2,1,0:T(8,128)S(1)}, u32[]{:S(2)}, u32[]{:S(2)}) %collective-permute-start.13) | collective-permute-done | bytes 131104 | tf_op jit(solution)/shard_map/ppermute | solution.py:451
  57.6 1.7 %collective-permute-start.14 = (f32[2,128,128]{2,1,0:T(8,128)S(1)}, f32[2,128,128]{2,1,0:T(8,128)S(1)}, u32[]{:S(2)}, u32[]{:S(2)}) collective-permute-start(f32[2,128,128]{2,1,0:T(8,128)S(1)} %get-tuple-element.50), channel_id=1, source_target_pairs={{0,8},{1,9},{2,10},{3,11},{4,12},{5,13},{6,14},{7,15},{8,16},{9,17... | collective-permute-start | bytes 393224 | tf_op jit(solution)/shard_map/ppermute | solution.py:451
  59.2 3.4 %collective-permute-done.14.wave = f32[2,128,128]{2,1,0:T(8,128)S(1)} collective-permute-done((f32[2,128,128]{2,1,0:T(8,128)S(1)}, f32[2,128,128]{2,1,0:T(8,128)S(1)}, u32[]{:S(2)}, u32[]{:S(2)}) %collective-permute-start.14) | collective-permute-done | bytes 131104 | tf_op jit(solution)/shard_map/ppermute | solution.py:451
  62.7 11.0 %collective-permute-start.15 = (f32[2,128,128]{2,1,0:T(8,128)S(1)}, f32[2,128,128]{2,1,0:T(8,128)S(1)}, u32[]{:S(2)}, u32[]{:S(2)}) collective-permute-start(f32[2,128,128]{2,1,0:T(8,128)S(1)} %get-tuple-element.51), channel_id=1, source_target_pairs={{0,24},{1,25},{2,26},{3,27},{4,28},{5,29},{6,30},{7,31},{8,0},{9,1... | collective-permute-start | bytes 393224 | tf_op jit(solution)/shard_map/ppermute | solution.py:451
  73.7 1.9 %collective-permute-done.15.wave = f32[2,128,128]{2,1,0:T(8,128)S(1)} collective-permute-done((f32[2,128,128]{2,1,0:T(8,128)S(1)}, f32[2,128,128]{2,1,0:T(8,128)S(1)}, u32[]{:S(2)}, u32[]{:S(2)}) %collective-permute-start.15) | collective-permute-done | bytes 131104 | tf_op jit(solution)/shard_map/ppermute | solution.py:451
  75.6 3.1 %collective-permute-start.16 = (f32[2,128,128]{2,1,0:T(8,128)S(1)}, f32[2,128,128]{2,1,0:T(8,128)S(1)}, u32[]{:S(2)}, u32[]{:S(2)}) collective-permute-start(f32[2,128,128]{2,1,0:T(8,128)S(1)} %get-tuple-element.55), channel_id=1, source_target_pairs={{0,24},{1,25},{2,26},{3,27},{4,28},{5,29},{6,30},{7,31},{8,0},{9,1... | collective-permute-start | bytes 393224 | tf_op jit(solution)/shard_map/ppermute | solution.py:451
  78.8 2.1 %collective-permute-done.16.wave = f32[2,128,128]{2,1,0:T(8,128)S(1)} collective-permute-done((f32[2,128,128]{2,1,0:T(8,128)S(1)}, f32[2,128,128]{2,1,0:T(8,128)S(1)}, u32[]{:S(2)}, u32[]{:S(2)}) %collective-permute-start.16) | collective-permute-done | bytes 131104 | tf_op jit(solution)/shard_map/ppermute | solution.py:451
  81.0 3.2 %collective-permute-start.17 = (f32[2,128,128]{2,1,0:T(8,128)S(1)}, f32[2,128,128]{2,1,0:T(8,128)S(1)}, u32[]{:S(2)}, u32[]{:S(2)}) collective-permute-start(f32[2,128,128]{2,1,0:T(8,128)S(1)} %get-tuple-element.58), channel_id=1, source_target_pairs={{0,24},{1,25},{2,26},{3,27},{4,28},{5,29},{6,30},{7,31},{8,0},{9,1... | collective-permute-start | bytes 393224 | tf_op jit(solution)/shard_map/ppermute | solution.py:451
  84.1 5.3 %collective-permute-done.17.wave = f32[2,128,128]{2,1,0:T(8,128)S(1)} collective-permute-done((f32[2,128,128]{2,1,0:T(8,128)S(1)}, f32[2,128,128]{2,1,0:T(8,128)S(1)}, u32[]{:S(2)}, u32[]{:S(2)}) %collective-permute-start.17) | collective-permute-done | bytes 131104 | tf_op jit(solution)/shard_map/ppermute | solution.py:451
  89.5 3.6 %backward_stage.5 = (f32[2,2,128,128]{3,2,1,0:T(8,128)S(1)}, f32[2,2,128,128]{3,2,1,0:T(8,128)S(1)}) custom-call(f32[16,2,128,128]{3,2,1,0:T(8,128)S(1)} %get-tuple-element.45.windows, f32[2,128,128]{2,1,0:T(8,128)S(1)} %collective-permute-done.17.wave, f32[4,2,128,128]{3,2,1,0:T(8,128)S(1)} %get-tuple-element.52.saved, f32[2,128,128]{2,1,0:T(8,128)S(1)} %copy-done.1, ...), custom_call_target="tpu_custom_call" | custom-call | tf_op jit(solution)/shard_map/backward_stage/pallas_call | solution.py:419
  93.1 1.3 %collective-permute-start.18 = (f32[2,2,128,128]{3,2,1,0:T(8,128)S(1)}, f32[2,2,128,128]{3,2,1,0:T(8,128)S(1)}, u32[]{:S(2)}, u32[]{:S(2)}) collective-permute-start(f32[2,2,128,128]{3,2,1,0:T(8,128)S(1)} %get-tuple-element.61.same), channel_id=1, source_target_pairs={{0,32},{1,33},{2,34},{3,35},{4,36},{5,37},{6,38},{7,39},{8,40},{9,... | collective-permute-start | bytes 786440 | tf_op jit(solution)/shard_map/ppermute | solution.py:461
  94.4 7.2 %collective-permute-start.20 = (f32[2,2,128,128]{3,2,1,0:T(8,128)S(1)}, f32[2,2,128,128]{3,2,1,0:T(8,128)S(1)}, u32[]{:S(2)}, u32[]{:S(2)}) collective-permute-start(f32[2,2,128,128]{3,2,1,0:T(8,128)S(1)} %get-tuple-element.63), channel_id=1, source_target_pairs={{0,33},{1,32},{2,35},{3,34},{4,37},{5,36},{6,39},{7,38},{8,41},{9,... | collective-permute-start | bytes 786440 | tf_op jit(solution)/shard_map/ppermute | solution.py:461
  101.5 7.2 %collective-permute-start.19 = (f32[2,2,128,128]{3,2,1,0:T(8,128)S(1)}, f32[2,2,128,128]{3,2,1,0:T(8,128)S(1)}, u32[]{:S(2)}, u32[]{:S(2)}) collective-permute-start(f32[2,2,128,128]{3,2,1,0:T(8,128)S(1)} %get-tuple-element.63), channel_id=1, source_target_pairs={{0,1},{1,0},{2,3},{3,2},{4,5},{5,4},{6,7},{7,6},{8,9},{9,8},{10,11... | collective-permute-start | bytes 786440 | tf_op jit(solution)/shard_map/ppermute | solution.py:461
  108.7 3.0 %collective-permute-done.20.prev_other = f32[2,2,128,128]{3,2,1,0:T(8,128)S(1)} collective-permute-done((f32[2,2,128,128]{3,2,1,0:T(8,128)S(1)}, f32[2,2,128,128]{3,2,1,0:T(8,128)S(1)}, u32[]{:S(2)}, u32[]{:S(2)}) %collective-permute-start.20) | collective-permute-done | bytes 262176 | tf_op jit(solution)/shard_map/ppermute | solution.py:461
  111.8 1.8 %paste_windows.1 = f32[2,2,128,512]{3,2,1,0:T(8,128)} custom-call(s32[2,2]{1,0:T(2,128)S(1)} %copy-done.7, s32[8,128]{1,0:T(8,128)S(1)} %slice.20.before, f32[2,2,128,128]{3,2,1,0:T(8,128)S(1)} %get-tuple-element.61.same, f32[2,2,128,128]{3,2,1,0:T(8,128)S(1)} %collective-permute-done.19.other, f32[2,2,128,128]{3,2,1,0:T(8,128)S(1)} %collective-permute-done.18.prev_same, ...), custom_call_target="tpu_custom_call" | custom-call | tf_op jit(solution)/shard_map/paste_windows/pallas_call | solution.py:217
  (44 shorter events, 8.3 us)
Async XLA Ops:
  0.0 59.2 %copy-start = (f32[2,128,128]{2,1,0:T(8,128)S(1)}, f32[2,128,128]{2,1,0:T(8,128)}, u32[]{:S(2)}) copy-start(f32[2,128,128]{2,1,0:T(8,128)} %param.9) | copy-start | bytes 393220
  0.7 7.7 %collective-permute-start = (s32[128,128]{1,0:T(8,128)S(1)}, s32[128,128]{1,0:T(8,128)S(1)}, u32[]{:S(2)}, u32[]{:S(2)}) collective-permute-start(s32[128,128]{1,0:T(8,128)S(1)} %pad.4), channel_id=1, source_target_pairs={{0,32},{32,64},{64,96},{96,0},{1,33},{33,65},{65,97},{97,1},{2,34}... | collective-permute-start | bytes 196616 | tf_op jit(solution)/shard_map/ppermute | solution.py:469
  2.8 0.9 copy-start.2
  3.7 1.2 %copy-start.4 = (f32[2,2,128,512]{3,2,1,0:T(8,128)S(1)}, f32[2,2,128,512]{3,2,1,0:T(8,128)}, u32[]{:S(2)}) copy-start(f32[2,2,128,512]{3,2,1,0:T(8,128)} %field.1) | copy-start | bytes 3145732
  4.9 0.9 copy-start.5
  5.8 0.7 copy-start.6
  7.3 36.0 %copy-start.1 = (f32[2,128,128]{2,1,0:T(8,128)S(1)}, f32[2,128,128]{2,1,0:T(8,128)}, u32[]{:S(2)}) copy-start(f32[2,128,128]{2,1,0:T(8,128)} %constant.36.clone.twiddle) | copy-start | bytes 393220
  7.3 15.6 %collective-permute-start.2 = (f32[2,2,128,128]{3,2,1,0:T(8,128)S(1)}, f32[2,2,128,128]{3,2,1,0:T(8,128)S(1)}, u32[]{:S(2)}, u32[]{:S(2)}) collective-permute-start(f32[2,2,128,128]{3,2,1,0:T(8,128)S(1)} %get-tuple-element.39), channel_id=1, source_target_pairs={{0,1},{1,0},{2,3},{3,2},{4,5},{5,4},{6,7},{7,6},{8,9},{9,8},{10,11... | collective-permute-start | bytes 786440 | tf_op jit(solution)/shard_map/ppermute | solution.py:461
  9.2 6.0 %collective-permute-start.1 = (f32[2,128,128]{2,1,0:T(8,128)S(1)}, f32[2,128,128]{2,1,0:T(8,128)S(1)}, u32[]{:S(2)}, u32[]{:S(2)}) collective-permute-start(f32[2,128,128]{2,1,0:T(8,128)S(1)} %get-tuple-element.38), channel_id=1, source_target_pairs={{0,96},{1,97},{2,98},{3,99},{4,100},{5,101},{6,102},{7,103},{8,104... | collective-permute-start | bytes 393224 | tf_op jit(solution)/shard_map/ppermute | solution.py:461
  10.7 7.1 %collective-permute-start.3 = (f32[2,128,128]{2,1,0:T(8,128)S(1)}, f32[2,128,128]{2,1,0:T(8,128)S(1)}, u32[]{:S(2)}, u32[]{:S(2)}) collective-permute-start(f32[2,128,128]{2,1,0:T(8,128)S(1)} %get-tuple-element.40), channel_id=1, source_target_pairs={{0,97},{1,96},{2,99},{3,98},{4,101},{5,100},{6,103},{7,102},{8,105... | collective-permute-start | bytes 393224 | tf_op jit(solution)/shard_map/ppermute | solution.py:461
  12.2 7.8 %collective-permute-start.4 = (f32[2,128,128]{2,1,0:T(8,128)S(1)}, f32[2,128,128]{2,1,0:T(8,128)S(1)}, u32[]{:S(2)}, u32[]{:S(2)}) collective-permute-start(f32[2,128,128]{2,1,0:T(8,128)S(1)} %get-tuple-element.42), channel_id=1, source_target_pairs={{0,96},{1,97},{2,98},{3,99},{4,100},{5,101},{6,102},{7,103},{8,104... | collective-permute-start | bytes 393224 | tf_op jit(solution)/shard_map/ppermute | solution.py:461
  12.8 10.2 %collective-permute-start.5 = (f32[2,128,128]{2,1,0:T(8,128)S(1)}, f32[2,128,128]{2,1,0:T(8,128)S(1)}, u32[]{:S(2)}, u32[]{:S(2)}) collective-permute-start(f32[2,128,128]{2,1,0:T(8,128)S(1)} %get-tuple-element.43), channel_id=1, source_target_pairs={{0,97},{1,96},{2,99},{3,98},{4,101},{5,100},{6,103},{7,102},{8,105... | collective-permute-start | bytes 393224 | tf_op jit(solution)/shard_map/ppermute | solution.py:461
  23.1 9.1 %collective-permute-start.9 = (f32[2,2,128,128]{3,2,1,0:T(8,128)S(1)}, f32[2,2,128,128]{3,2,1,0:T(8,128)S(1)}, u32[]{:S(2)}, u32[]{:S(2)}) collective-permute-start(f32[2,2,128,128]{3,2,1,0:T(8,128)S(1)} %pad_maximum_fusion.1.near1), channel_id=1, source_target_pairs={{0,2},{1,3},{2,4},{3,5},{4,6},{5,7},{6,0},{7,1},{8,10},{9,11},{10,... | collective-permute-start | bytes 786440 | tf_op jit(solution)/shard_map/ppermute | solution.py:445
  24.4 7.7 %collective-permute-start.6 = (f32[2,2,128,128]{3,2,1,0:T(8,128)S(1)}, f32[2,2,128,128]{3,2,1,0:T(8,128)S(1)}, u32[]{:S(2)}, u32[]{:S(2)}) collective-permute-start(f32[2,2,128,128]{3,2,1,0:T(8,128)S(1)} %pad_maximum_fusion.near0), channel_id=1, source_target_pairs={{0,6},{1,7},{2,0},{3,1},{4,2},{5,3},{6,4},{7,5},{8,14},{9,15},{10,... | collective-permute-start | bytes 786440 | tf_op jit(solution)/shard_map/ppermute | solution.py:445
  26.0 11.5 %collective-permute-start.7 = (f32[2,2,128,128]{3,2,1,0:T(8,128)S(1)}, f32[2,2,128,128]{3,2,1,0:T(8,128)S(1)}, u32[]{:S(2)}, u32[]{:S(2)}) collective-permute-start(f32[2,2,128,128]{3,2,1,0:T(8,128)S(1)} %pad_maximum_fusion.1.near1), channel_id=1, source_target_pairs={{0,6},{1,7},{2,0},{3,1},{4,2},{5,3},{6,4},{7,5},{8,14},{9,15},{10,... | collective-permute-start | bytes 786440 | tf_op jit(solution)/shard_map/ppermute | solution.py:445
  27.4 10.3 %collective-permute-start.11 = (f32[2,2,128,128]{3,2,1,0:T(8,128)S(1)}, f32[2,2,128,128]{3,2,1,0:T(8,128)S(1)}, u32[]{:S(2)}, u32[]{:S(2)}) collective-permute-start(f32[2,2,128,128]{3,2,1,0:T(8,128)S(1)} %pad_maximum_fusion.near0), channel_id=1, source_target_pairs={{0,2},{1,3},{2,4},{3,5},{4,6},{5,7},{6,0},{7,1},{8,10},{9,11},{10,... | collective-permute-start | bytes 786440 | tf_op jit(solution)/shard_map/ppermute | solution.py:445
  32.1 11.2 %collective-permute-start.10 = (f32[2,2,128,128]{3,2,1,0:T(8,128)S(1)}, f32[2,2,128,128]{3,2,1,0:T(8,128)S(1)}, u32[]{:S(2)}, u32[]{:S(2)}) collective-permute-start(f32[2,2,128,128]{3,2,1,0:T(8,128)S(1)} %collective-permute-done.9.down1), channel_id=1, source_target_pairs={{0,2},{1,3},{2,4},{3,5},{4,6},{5,7},{6,0},{7,1},{8,10},{9,11},{10,... | collective-permute-start | bytes 786440 | tf_op jit(solution)/shard_map/ppermute | solution.py:445
  32.1 11.2 %collective-permute-start.8 = (f32[2,2,128,128]{3,2,1,0:T(8,128)S(1)}, f32[2,2,128,128]{3,2,1,0:T(8,128)S(1)}, u32[]{:S(2)}, u32[]{:S(2)}) collective-permute-start(f32[2,2,128,128]{3,2,1,0:T(8,128)S(1)} %collective-permute-done.6.up0), channel_id=1, source_target_pairs={{0,6},{1,7},{2,0},{3,1},{4,2},{5,3},{6,4},{7,5},{8,14},{9,15},{10,... | collective-permute-start | bytes 786440 | tf_op jit(solution)/shard_map/ppermute | solution.py:445
  47.3 5.1 %collective-permute-start.12 = (f32[2,128,128]{2,1,0:T(8,128)S(1)}, f32[2,128,128]{2,1,0:T(8,128)S(1)}, u32[]{:S(2)}, u32[]{:S(2)}) collective-permute-start(f32[2,128,128]{2,1,0:T(8,128)S(1)} %get-tuple-element.46), channel_id=1, source_target_pairs={{0,8},{1,9},{2,10},{3,11},{4,12},{5,13},{6,14},{7,15},{8,16},{9,17... | collective-permute-start | bytes 393224 | tf_op jit(solution)/shard_map/ppermute | solution.py:451
  52.4 10.3 %copy-start.3 = (f32[2,128,128]{2,1,0:T(8,128)S(1)}, f32[2,128,128]{2,1,0:T(8,128)}, u32[]{:S(2)}) copy-start(f32[2,128,128]{2,1,0:T(8,128)} %constant.37.clone.chirp) | copy-start | bytes 393220
  52.4 5.1 %collective-permute-start.13 = (f32[2,128,128]{2,1,0:T(8,128)S(1)}, f32[2,128,128]{2,1,0:T(8,128)S(1)}, u32[]{:S(2)}, u32[]{:S(2)}) collective-permute-start(f32[2,128,128]{2,1,0:T(8,128)S(1)} %get-tuple-element.48), channel_id=1, source_target_pairs={{0,8},{1,9},{2,10},{3,11},{4,12},{5,13},{6,14},{7,15},{8,16},{9,17... | collective-permute-start | bytes 393224 | tf_op jit(solution)/shard_map/ppermute | solution.py:451
  57.6 5.1 %collective-permute-start.14 = (f32[2,128,128]{2,1,0:T(8,128)S(1)}, f32[2,128,128]{2,1,0:T(8,128)S(1)}, u32[]{:S(2)}, u32[]{:S(2)}) collective-permute-start(f32[2,128,128]{2,1,0:T(8,128)S(1)} %get-tuple-element.50), channel_id=1, source_target_pairs={{0,8},{1,9},{2,10},{3,11},{4,12},{5,13},{6,14},{7,15},{8,16},{9,17... | collective-permute-start | bytes 393224 | tf_op jit(solution)/shard_map/ppermute | solution.py:451
  62.7 12.9 %collective-permute-start.15 = (f32[2,128,128]{2,1,0:T(8,128)S(1)}, f32[2,128,128]{2,1,0:T(8,128)S(1)}, u32[]{:S(2)}, u32[]{:S(2)}) collective-permute-start(f32[2,128,128]{2,1,0:T(8,128)S(1)} %get-tuple-element.51), channel_id=1, source_target_pairs={{0,24},{1,25},{2,26},{3,27},{4,28},{5,29},{6,30},{7,31},{8,0},{9,1... | collective-permute-start | bytes 393224 | tf_op jit(solution)/shard_map/ppermute | solution.py:451
  75.6 5.3 %collective-permute-start.16 = (f32[2,128,128]{2,1,0:T(8,128)S(1)}, f32[2,128,128]{2,1,0:T(8,128)S(1)}, u32[]{:S(2)}, u32[]{:S(2)}) collective-permute-start(f32[2,128,128]{2,1,0:T(8,128)S(1)} %get-tuple-element.55), channel_id=1, source_target_pairs={{0,24},{1,25},{2,26},{3,27},{4,28},{5,29},{6,30},{7,31},{8,0},{9,1... | collective-permute-start | bytes 393224 | tf_op jit(solution)/shard_map/ppermute | solution.py:451
  80.9 30.8 %copy-start.7 = (s32[2,2]{1,0:T(2,128)S(1)}, s32[2,2]{1,0:T(2,128)}, u32[]{:S(2)}) copy-start(s32[2,2]{1,0:T(2,128)} %offsets.3) | copy-start | bytes 52
  81.0 8.5 %collective-permute-start.17 = (f32[2,128,128]{2,1,0:T(8,128)S(1)}, f32[2,128,128]{2,1,0:T(8,128)S(1)}, u32[]{:S(2)}, u32[]{:S(2)}) collective-permute-start(f32[2,128,128]{2,1,0:T(8,128)S(1)} %get-tuple-element.58), channel_id=1, source_target_pairs={{0,24},{1,25},{2,26},{3,27},{4,28},{5,29},{6,30},{7,31},{8,0},{9,1... | collective-permute-start | bytes 393224 | tf_op jit(solution)/shard_map/ppermute | solution.py:451
  93.1 8.5 %collective-permute-start.18 = (f32[2,2,128,128]{3,2,1,0:T(8,128)S(1)}, f32[2,2,128,128]{3,2,1,0:T(8,128)S(1)}, u32[]{:S(2)}, u32[]{:S(2)}) collective-permute-start(f32[2,2,128,128]{3,2,1,0:T(8,128)S(1)} %get-tuple-element.61.same), channel_id=1, source_target_pairs={{0,32},{1,33},{2,34},{3,35},{4,36},{5,37},{6,38},{7,39},{8,40},{9,... | collective-permute-start | bytes 786440 | tf_op jit(solution)/shard_map/ppermute | solution.py:461
  94.4 17.4 %collective-permute-start.20 = (f32[2,2,128,128]{3,2,1,0:T(8,128)S(1)}, f32[2,2,128,128]{3,2,1,0:T(8,128)S(1)}, u32[]{:S(2)}, u32[]{:S(2)}) collective-permute-start(f32[2,2,128,128]{3,2,1,0:T(8,128)S(1)} %get-tuple-element.63), channel_id=1, source_target_pairs={{0,33},{1,32},{2,35},{3,34},{4,37},{5,36},{6,39},{7,38},{8,41},{9,... | collective-permute-start | bytes 786440 | tf_op jit(solution)/shard_map/ppermute | solution.py:461
  101.5 10.2 %collective-permute-start.19 = (f32[2,2,128,128]{3,2,1,0:T(8,128)S(1)}, f32[2,2,128,128]{3,2,1,0:T(8,128)S(1)}, u32[]{:S(2)}, u32[]{:S(2)}) collective-permute-start(f32[2,2,128,128]{3,2,1,0:T(8,128)S(1)} %get-tuple-element.63), channel_id=1, source_target_pairs={{0,1},{1,0},{2,3},{3,2},{4,5},{5,4},{6,7},{7,6},{8,9},{9,8},{10,11... | collective-permute-start | bytes 786440 | tf_op jit(solution)/shard_map/ppermute | solution.py:461

commit v4 on v3

--- a/solution.py
+++ b/solution.py
@@ -20,7 +20,6 @@
 F32 = jnp.float32
 PARAMS = pltpu.CompilerParams(vmem_limit_bytes=20 << 20)
 GROUP = 8
-PAD_ROWS = 128
 PITCH = GROUP + 1
 TRAIL = pltpu.VMEM((PER_STAGE + 1,) + PLANE, F32)
 ROW_STAGES = pltpu.VMEM((2, 2, 160, N), F32)
@@ -109,12 +108,22 @@
     transform_rows(real, imag, twiddle, stages.at[1], put)
 
 
-def corner(offsets, position):
-    row = offsets[position, 0]
-    column = offsets[position, 1]
+def role(core, kind):
+    flip = kind % 2
+    number = jnp.where(core == flip, 0, 1)
+    previous = number if kind < 2 else 1 - number
+    return previous, number
+
+
+def corner(offsets, before, core, kind):
+    previous, number = role(core, kind)
+    row = jnp.where(previous == 1, before[number, 0], offsets[number, 0]) % N
+    column = jnp.where(previous == 1, before[number, 1], offsets[number, 1])
     tile = column // N
     after = pl.multiple_of(jnp.minimum(tile + 1, 3) * N, N)
-    return row % N, pl.multiple_of(tile * N, N), after, column % N
+    low = jnp.where(previous == 1, 0, row)
+    high = jnp.where(previous == 1, row, N)
+    return row, low, high, pl.multiple_of(tile * N, N), after, column % N
 
 
 def squared(chirp):
@@ -122,9 +131,9 @@
     return real * real - imag * imag, -2.0 * real * imag
 
 
-def cut(offsets, position, field, chirp, targets):
+def cut(place, field, chirp, targets):
     lane = lax.broadcasted_iota(jnp.int32, (N, N), 1)
-    unused, tile, after, shift = corner(offsets, position)
+    unused, unused, unused, tile, after, shift = place
     wrapped = lane < shift
     real, imag = squared(chirp)
     factor = (imag * (1.0 / N), real * (-1.0 / N))
@@ -139,7 +148,7 @@
         ]
         value = times(*value, *factor)
         for part in range(2):
-            targets[layer][part] = value[part].T if layer % 2 else value[part]
+            targets[layer, part] = value[part].T if layer % 2 else value[part]
 
 
 def here():
@@ -147,65 +156,61 @@
     return device // (CORES * RING), device // CORES % RING, device % CORES
 
 
-def cut_own_kernel(offsets, field, chirp, probe, same0, same1, other, wave, *copies):
+def load_kernel(field, chirp, probe, field_out, chirp_out, probe_out):
+    field_out[...] = field[...]
+    chirp_out[...] = chirp[...]
+    probe_out[...] = probe[...]
+
+
+def cut_kernel(offsets, before, field, chirp, probe, same, other, moved_same, moved_other, wave):
     core = here()[2]
-    cut(offsets, core, field, chirp, (same0, same1))
-    cut(offsets, 1 - core, field, chirp, [other.at[k] for k in range(PER_DEVICE)])
-    row, unused, unused, shift = corner(offsets, core)
-    rolled = [pltpu.roll(pltpu.roll(probe[k], row, 0), shift, 1) for k in range(2)]
+    for kind, target in ((2, moved_same), (3, moved_other), (0, same), (1, other)):
+        cut(corner(offsets, before, core, kind), field, chirp, target)
+    place = corner(offsets, before, core, 0)
+    rolled = [pltpu.roll(pltpu.roll(probe[k], place[0], 0), place[5], 1) for k in range(2)]
     real, imag = times(*rolled, chirp[0], chirp[1])
     wave[0] = -imag
     wave[1] = real
-    copies[0][...] = field[...]
-    copies[1][...] = chirp[...]
-
-
-def cut_fore_kernel(before, field, chirp, *targets):
-    core = here()[2]
-    cut(before, core, field, chirp, targets[:2])
-    cut(before, 1 - core, field, chirp, targets[2:])
-
-
-def cut_own(offsets, field, chirp, probe):
-    return pl.pallas_call(
-        cut_own_kernel,
-        out_shape=(WAVE, WAVE, PIECE, WAVE, jax.ShapeDtypeStruct(field.shape, F32), WAVE),
-        in_specs=[SMEM_SPEC] + [VMEM_SPEC] * 3,
-        name="cut_own",
-        compiler_params=PARAMS,
-    )(offsets, field, chirp, probe)
-
-
-def cut_fore(before, field, chirp):
-    return pl.pallas_call(
-        cut_fore_kernel,
-        out_shape=(WAVE,) * 4,
-        in_specs=[SMEM_SPEC] + [VMEM_SPEC] * 2,
-        name="cut_fore",
-        compiler_params=PARAMS,
-    )(before, field, chirp)
-
-
-def paste(offsets, position, value, target, ahead):
+
+
+def load(field, chirp, probe):
+    return pl.pallas_call(
+        load_kernel,
+        out_shape=(jax.ShapeDtypeStruct(field.shape, F32), WAVE, WAVE),
+        name="load",
+        compiler_params=PARAMS,
+    )(field, chirp, probe)
+
+
+def cut_windows(offsets, before, field, chirp, probe):
+    return pl.pallas_call(
+        cut_kernel,
+        out_shape=(PIECE,) * 4 + (WAVE,),
+        in_specs=[SMEM_SPEC] * 2 + [VMEM_SPEC] * 3,
+        name="cut_windows",
+        compiler_params=PARAMS,
+    )(offsets, before, field, chirp, probe)
+
+
+def paste(place, value, target):
     row = lax.broadcasted_iota(jnp.int32, (N, N), 0)
     lane = lax.broadcasted_iota(jnp.int32, (N, N), 1)
-    top, tile, after, shift = corner(offsets, position)
-    rows = row < top if ahead else row >= top
+    unused, low, high, tile, after, shift = place
+    rows = (row >= low) & (row < high)
     target[:, pl.ds(tile, N)] += jnp.where(rows & (lane >= shift), value, 0.0)
     target[:, pl.ds(after, N)] += jnp.where(rows & (lane < shift), value, 0.0)
 
 
-def paste_kernel(offsets, before, same, other, prev_same, prev_other, out, total, sems):
+def paste_kernel(offsets, before, same, other, moved_same, moved_other, out, total, sems):
     core = here()[2]
+    places = [corner(offsets, before, core, kind) for kind in range(4)]
     copies = []
     total[...] = jnp.zeros(total.shape, F32)
     for layer in range(PER_DEVICE):
         for part in range(2):
             target = total.at[layer, part]
-            paste(offsets, core, same[layer, part], target, False)
-            paste(offsets, 1 - core, other[layer, part], target, False)
-            paste(before, core, prev_same[layer, part], target, True)
-            paste(before, 1 - core, prev_other[layer, part], target, True)
+            for place, source in zip(places, (same, other, moved_same, moved_other)):
+                paste(place, source[layer, part], target)
             copy = pltpu.make_async_copy(target, out.at[layer, part], sems.at[layer, part])
             copy.start()
             copies.append(copy)
@@ -451,13 +456,23 @@
     return lax.ppermute(value, "depth", pairs)
 
 
-def across(value, strips, swap):
+def swap_cores(value):
+    depth = lax.axis_size("depth")
+    return lax.ppermute(value, "depth", [(device, device ^ 1) for device in range(depth)])
+
+
+def across(value, swap, outward):
     rows, depth = lax.axis_size("pos"), lax.axis_size("depth")
     pairs = []
     for strip in range(rows):
         for device in range(depth):
-            other = device ^ 1 if swap else device
-            pairs.append((strip * depth + device, (strip + strips) % rows * depth + other))
+            core = device % CORES
+            target = core ^ swap
+            owner = core if outward else target
+            step = (1 if owner == 0 else -1) * (1 if outward else -1)
+            pairs.append(
+                (strip * depth + device, (strip + step) % rows * depth + (device ^ swap))
+            )
     return lax.ppermute(value, ("pos", "depth"), pairs)
 
 
@@ -465,28 +480,33 @@
     twiddle, chirp = tables
     core = lax.axis_index("depth") % CORES
     rows = lax.axis_size("pos")
-    padded = jnp.pad(offsets, ((0, PAD_ROWS - offsets.shape[0]), (0, N - offsets.shape[1])))
-    before = lax.ppermute(padded, "pos", [(i, (i + 1) % rows) for i in range(rows)])
-    before = before[:GROUP]
-
-    own = cut_own(offsets, object_field, chirp, probe)
-    own_same, wave, field = own[:2], own[3], own[4]
-    own_other = across(own[2], 0, True)
-    fore = cut_fore(before, field, own[5])
-    fore_same = [across(fore[parity], -1, False) for parity in range(PER_DEVICE)]
-    fore_other = [across(fore[2 + parity], -1, True) for parity in range(PER_DEVICE)]
-    row_here = jnp.where(core == 0, offsets[0, 0], offsets[1, 0]) % N
-
+    padding = ((0, GROUP - offsets.shape[0]), (0, N - offsets.shape[1]))
+    message = jnp.concatenate([intensity[1], jnp.pad(offsets.astype(F32), padding)])
+    message = lax.ppermute(message, "pos", [(i, (i + 1) % rows) for i in range(rows)])
+    before = message[N:].astype(jnp.int32)
+    measured = jnp.where(core == 0, intensity[0], message[:N])
+
+    field, chirp_here, probe_here = load(object_field, chirp, probe)
+    cuts = cut_windows(offsets, before, field, chirp_here, probe_here)
+    same, other, moved_same, moved_other, wave = cuts
+    moved_same = across(moved_same, 0, False)
+    moved_other = across(moved_other, 1, False)
+    other = swap_cores(other)
+
+    row_here = jnp.where(core == 0, offsets[0, 0], before[1, 0]) % N
+    low = jnp.where(core == 0, row_here, 0)
+    high = jnp.where(core == 0, N, row_here)
     near, up, down = [], [], []
     index = jnp.arange(N, dtype=jnp.int32)
+    inside = (index >= low) & (index < high)
     for parity in range(PER_DEVICE):
         axis = (None, slice(None)) if parity else (slice(None), None)
-        below = jnp.broadcast_to((index >= row_here)[axis], PLANE)
+        here_rows = jnp.broadcast_to(inside[axis], PLANE)
         near.append(
             jnp.stack(
                 [
-                    jnp.where(below, own_same[parity], fore_same[parity]),
-                    jnp.where(below, own_other[parity], fore_other[parity]),
+                    jnp.where(here_rows, same[parity], moved_same[parity]),
+                    jnp.where(here_rows, other[parity], moved_other[parity]),
                 ]
             )
         )
@@ -499,7 +519,6 @@
         wave = along_stages(wave, 1)
         wave, saved = forward_stage(section, windows, wave, saved, twiddle)
     wave = along_stages(wave, 1)
-    measured = lax.dynamic_index_in_dim(intensity, core, 0, keepdims=False)
     wave, same, other = turn_stage(STAGES - 1, windows, wave, measured, twiddle, chirp)
     for section in reversed(range(1, STAGES - 1)):
         wave = along_stages(wave, -1)
@@ -508,11 +527,11 @@
         )
     wave = along_stages(wave, -1)
     same, other = backward_stage(0, windows, wave, saved, twiddle, chirp, same, other)
-    prev_same = across(same, 1, False)
-    prev_other = across(other, 1, True)
-    other, prev_same = lax.optimization_barrier((other, prev_same))
-    own_other = across(other, 0, True)
-    pieces = (same, own_other, prev_same, prev_other)
+    moved_same = across(same, 0, True)
+    moved_other = across(other, 1, True)
+    other, moved_same = lax.optimization_barrier((other, moved_same))
+    other = swap_cores(other)
+    pieces = (same, other, moved_same, moved_other)
     return paste_windows(offsets, before, pieces, object_field.shape)
 
 

time: 114 us -> 110 us (0.965)
  waiting for transfers between devices: 44 us -> 40 us
    ppermute x8 -> x4, starting transfers between devices: 20.8 us -> 11.7 us  [across(): return lax.ppermute(value, ('pos', 'depth'), pairs)]
    ppermute x1 -> x3, starting transfers between devices: 2.04 us -> 8.98 us  [the longest x2 6.87 us: swap_cores(): lax.ppermute(value, 'depth', [(device, device ^ 1) for device in range(de...]
    ppermute x8 -> x4, waiting for transfers between devices: 10.8 us -> 6.16 us  [across(): return lax.ppermute(value, ('pos', 'depth'), pairs)]
    ppermute x6, starting transfers between devices: 7.03 us -> 9.03 us  [along_ring(): return lax.ppermute(value, 'depth', pairs)]
  transfers between devices with their start and end apart: 21 -> 19, of which waited for: 14 -> 13; matrix products, arithmetic and copies ran while one was open for 0% -> 1% of each run, Pallas kernels for 1% -> 0%
where the time goes in v4:
time: 110 us
  starting transfers between devices  50.7 us (46%)
  waiting for transfers between devices  40 us (36%)
  Pallas kernels  10.8 us (10%)
  local copies, waits for them, and re-layouts  5.69 us (5%)
  between operations  1.51 us (1%)
    ppermute x6, starting transfers between devices, along_stages(): return lax.ppermute(value, 'depth', pairs)  20.9 us
    ppermute x6, waiting for transfers between devices, along_stages(): return lax.ppermute(value, 'depth', pairs)  20.7 us
    ppermute x6, waiting for transfers between devices, along_ring(): return lax.ppermute(value, 'depth', pairs)  13.2 us
    ppermute x4, starting transfers between devices, across(): return lax.ppermute(value, ('pos', 'depth'), pairs)  11.7 us
    ppermute x6, starting transfers between devices, along_ring(): return lax.ppermute(value, 'depth', pairs)  9.03 us
    ppermute x2, starting transfers between devices, swap_cores(): lax.ppermute(value, 'depth', [(device, device ^ 1) for device in range(de...  6.87 us
    ppermute x4, waiting for transfers between devices, across(): return lax.ppermute(value, ('pos', 'depth'), pairs)  6.16 us
    pallas_call x1, Pallas kernels, first_stage(): pl.pallas_call(first_kernel, out_shape=(WAVE, SAVED, STACK), in_specs=[VM...  3.91 us
  transfers between devices with their start and end apart: 19, of which 13 were waited for; matrix products, arithmetic and copies ran while one was open for 1% of the time, Pallas kernels for 0%

profile of v4, /device:TPU:1, one launch (start us, length us, event | category | flops | bytes accessed | tf_op | source)
XLA Modules:
  0.0 109.6 jit_solution(9813069900895987499)
XLA Ops:
  1.6 2.1 %collective-permute-start = (f32[136,128]{1,0:T(8,128)S(1)}, f32[136,128]{1,0:T(8,128)S(1)}, u32[]{:S(2)}, u32[]{:S(2)}) collective-permute-start(f32[136,128]{1,0:T(8,128)S(1)} %select_maximum_fusion), channel_id=1, source_target_pairs={{0,32},{32,64},{64,96},{96,0},{1,33},{33,65},{65,97},{97,1},{2,34}... | collective-permute-start | bytes 208904 | tf_op jit(solution)/shard_map/ppermute | solution.py:485
  3.7 0.9 copy-done.1
  4.6 1.2 %copy-done.3 = f32[2,2,128,512]{3,2,1,0:T(8,128)S(1)} copy-done((f32[2,2,128,512]{3,2,1,0:T(8,128)S(1)}, f32[2,2,128,512]{3,2,1,0:T(8,128)}, u32[]{:S(2)}) %copy-start.3) | copy-done | bytes 1048600
  5.9 0.9 copy-done.4
  7.6 1.1 cut_windows.1
  8.6 1.3 %collective-permute-start.1 = (f32[2,2,128,128]{3,2,1,0:T(8,128)S(1)}, f32[2,2,128,128]{3,2,1,0:T(8,128)S(1)}, u32[]{:S(2)}, u32[]{:S(2)}) collective-permute-start(f32[2,2,128,128]{3,2,1,0:T(8,128)S(1)} %get-tuple-element.37), channel_id=1, source_target_pairs={{0,96},{1,33},{2,98},{3,35},{4,100},{5,37},{6,102},{7,39},{8,104},... | collective-permute-start | bytes 786440 | tf_op jit(solution)/shard_map/ppermute | solution.py:476
  9.9 2.1 %collective-permute-start.2 = (f32[2,2,128,128]{3,2,1,0:T(8,128)S(1)}, f32[2,2,128,128]{3,2,1,0:T(8,128)S(1)}, u32[]{:S(2)}, u32[]{:S(2)}) collective-permute-start(f32[2,2,128,128]{3,2,1,0:T(8,128)S(1)} %get-tuple-element.38), channel_id=1, source_target_pairs={{0,1},{1,0},{2,3},{3,2},{4,5},{5,4},{6,7},{7,6},{8,9},{9,8},{10,11... | collective-permute-start | bytes 786440 | tf_op jit(solution)/shard_map/ppermute | solution.py:461
  15.2 3.9 %collective-permute-done.3 = f32[2,2,128,128]{3,2,1,0:T(8,128)S(1)} collective-permute-done((f32[2,2,128,128]{3,2,1,0:T(8,128)S(1)}, f32[2,2,128,128]{3,2,1,0:T(8,128)S(1)}, u32[]{:S(2)}, u32[]{:S(2)}) %collective-permute-start.3) | collective-permute-done | bytes 262176 | tf_op jit(solution)/shard_map/ppermute | solution.py:476
  19.2 2.8 %collective-permute-start.4 = (f32[2,2,128,128]{3,2,1,0:T(8,128)S(1)}, f32[2,2,128,128]{3,2,1,0:T(8,128)S(1)}, u32[]{:S(2)}, u32[]{:S(2)}) collective-permute-start(f32[2,2,128,128]{3,2,1,0:T(8,128)S(1)} %pad_maximum_fusion.near0), channel_id=1, source_target_pairs={{0,6},{1,7},{2,0},{3,1},{4,2},{5,3},{6,4},{7,5},{8,14},{9,15},{10,... | collective-permute-start | bytes 786440 | tf_op jit(solution)/shard_map/ppermute | solution.py:450
  22.2 2.7 %collective-permute-start.5 = (f32[2,2,128,128]{3,2,1,0:T(8,128)S(1)}, f32[2,2,128,128]{3,2,1,0:T(8,128)S(1)}, u32[]{:S(2)}, u32[]{:S(2)}) collective-permute-start(f32[2,2,128,128]{3,2,1,0:T(8,128)S(1)} %pad_maximum_fusion.1.near1), channel_id=1, source_target_pairs={{0,6},{1,7},{2,0},{3,1},{4,2},{5,3},{6,4},{7,5},{8,14},{9,15},{10,... | collective-permute-start | bytes 786440 | tf_op jit(solution)/shard_map/ppermute | solution.py:450
  24.8 2.2 %collective-permute-done.4.up0 = f32[2,2,128,128]{3,2,1,0:T(8,128)S(1)} collective-permute-done((f32[2,2,128,128]{3,2,1,0:T(8,128)S(1)}, f32[2,2,128,128]{3,2,1,0:T(8,128)S(1)}, u32[]{:S(2)}, u32[]{:S(2)}) %collective-permute-start.4) | collective-permute-done | bytes 262176 | tf_op jit(solution)/shard_map/ppermute | solution.py:450
  27.0 3.4 %collective-permute-start.6 = (f32[2,2,128,128]{3,2,1,0:T(8,128)S(1)}, f32[2,2,128,128]{3,2,1,0:T(8,128)S(1)}, u32[]{:S(2)}, u32[]{:S(2)}) collective-permute-start(f32[2,2,128,128]{3,2,1,0:T(8,128)S(1)} %collective-permute-done.4.up0), channel_id=1, source_target_pairs={{0,6},{1,7},{2,0},{3,1},{4,2},{5,3},{6,4},{7,5},{8,14},{9,15},{10,... | collective-permute-start | bytes 786440 | tf_op jit(solution)/shard_map/ppermute | solution.py:450
  30.4 5.4 %collective-permute-done.9.down0 = f32[2,2,128,128]{3,2,1,0:T(8,128)S(1)} collective-permute-done((f32[2,2,128,128]{3,2,1,0:T(8,128)S(1)}, f32[2,2,128,128]{3,2,1,0:T(8,128)S(1)}, u32[]{:S(2)}, u32[]{:S(2)}) %collective-permute-start.9) | collective-permute-done | bytes 262176 | tf_op jit(solution)/shard_map/ppermute | solution.py:450
  35.8 2.4 %collective-permute-done.6.far0 = f32[2,2,128,128]{3,2,1,0:T(8,128)S(1)} collective-permute-done((f32[2,2,128,128]{3,2,1,0:T(8,128)S(1)}, f32[2,2,128,128]{3,2,1,0:T(8,128)S(1)}, u32[]{:S(2)}, u32[]{:S(2)}) %collective-permute-start.6) | collective-permute-done | bytes 262176 | tf_op jit(solution)/shard_map/ppermute | solution.py:450
  38.3 3.2 %collective-permute-done.8.far1 = f32[2,2,128,128]{3,2,1,0:T(8,128)S(1)} collective-permute-done((f32[2,2,128,128]{3,2,1,0:T(8,128)S(1)}, f32[2,2,128,128]{3,2,1,0:T(8,128)S(1)}, u32[]{:S(2)}, u32[]{:S(2)}) %collective-permute-start.8) | collective-permute-done | bytes 262176 | tf_op jit(solution)/shard_map/ppermute | solution.py:450
  41.4 3.9 %first_stage.1 = (f32[2,128,128]{2,1,0:T(8,128)S(1)}, f32[4,2,128,128]{3,2,1,0:T(8,128)S(1)}, f32[16,2,128,128]{3,2,1,0:T(8,128)S(1)}) custom-call(f32[2,2,128,128]{3,2,1,0:T(8,128)S(1)} %pad_maximum_fusion.near0, f32[2,2,128,128]{3,2,1,0:T(8,128)S(1)} %pad_maximum_fusion.1.near1, f32[2,2,128,128]{3,2,1,0:T(8,128)S(1)} %collective-permute-done.4.up0, ...), custom_call_target="tpu_custom_call" | custom-call | tf_op jit(solution)/shard_map/first_stage/pallas_call | solution.py:402
  45.4 5.0 %collective-permute-done.10.wave = f32[2,128,128]{2,1,0:T(8,128)S(1)} collective-permute-done((f32[2,128,128]{2,1,0:T(8,128)S(1)}, f32[2,128,128]{2,1,0:T(8,128)S(1)}, u32[]{:S(2)}, u32[]{:S(2)}) %collective-permute-start.10) | collective-permute-done | bytes 131104 | tf_op jit(solution)/shard_map/ppermute | solution.py:456
  50.5 2.5 %collective-permute-start.11 = (f32[2,128,128]{2,1,0:T(8,128)S(1)}, f32[2,128,128]{2,1,0:T(8,128)S(1)}, u32[]{:S(2)}, u32[]{:S(2)}) collective-permute-start(f32[2,128,128]{2,1,0:T(8,128)S(1)} %get-tuple-element.44), channel_id=1, source_target_pairs={{0,8},{1,9},{2,10},{3,11},{4,12},{5,13},{6,14},{7,15},{8,16},{9,17... | collective-permute-start | bytes 393224 | tf_op jit(solution)/shard_map/ppermute | solution.py:456
  53.0 2.6 %collective-permute-done.11.wave = f32[2,128,128]{2,1,0:T(8,128)S(1)} collective-permute-done((f32[2,128,128]{2,1,0:T(8,128)S(1)}, f32[2,128,128]{2,1,0:T(8,128)S(1)}, u32[]{:S(2)}, u32[]{:S(2)}) %collective-permute-start.11) | collective-permute-done | bytes 131104 | tf_op jit(solution)/shard_map/ppermute | solution.py:456
  55.7 1.3 %collective-permute-start.12 = (f32[2,128,128]{2,1,0:T(8,128)S(1)}, f32[2,128,128]{2,1,0:T(8,128)S(1)}, u32[]{:S(2)}, u32[]{:S(2)}) collective-permute-start(f32[2,128,128]{2,1,0:T(8,128)S(1)} %get-tuple-element.46), channel_id=1, source_target_pairs={{0,8},{1,9},{2,10},{3,11},{4,12},{5,13},{6,14},{7,15},{8,16},{9,17... | collective-permute-start | bytes 393224 | tf_op jit(solution)/shard_map/ppermute | solution.py:456
  57.0 3.8 %collective-permute-done.12.wave = f32[2,128,128]{2,1,0:T(8,128)S(1)} collective-permute-done((f32[2,128,128]{2,1,0:T(8,128)S(1)}, f32[2,128,128]{2,1,0:T(8,128)S(1)}, u32[]{:S(2)}, u32[]{:S(2)}) %collective-permute-start.12) | collective-permute-done | bytes 131104 | tf_op jit(solution)/shard_map/ppermute | solution.py:456
  60.8 10.6 %collective-permute-start.13 = (f32[2,128,128]{2,1,0:T(8,128)S(1)}, f32[2,128,128]{2,1,0:T(8,128)S(1)}, u32[]{:S(2)}, u32[]{:S(2)}) collective-permute-start(f32[2,128,128]{2,1,0:T(8,128)S(1)} %get-tuple-element.47), channel_id=1, source_target_pairs={{0,24},{1,25},{2,26},{3,27},{4,28},{5,29},{6,30},{7,31},{8,0},{9,1... | collective-permute-start | bytes 393224 | tf_op jit(solution)/shard_map/ppermute | solution.py:456
  71.4 1.9 %collective-permute-done.13.wave = f32[2,128,128]{2,1,0:T(8,128)S(1)} collective-permute-done((f32[2,128,128]{2,1,0:T(8,128)S(1)}, f32[2,128,128]{2,1,0:T(8,128)S(1)}, u32[]{:S(2)}, u32[]{:S(2)}) %collective-permute-start.13) | collective-permute-done | bytes 131104 | tf_op jit(solution)/shard_map/ppermute | solution.py:456
  73.4 3.1 %collective-permute-start.14 = (f32[2,128,128]{2,1,0:T(8,128)S(1)}, f32[2,128,128]{2,1,0:T(8,128)S(1)}, u32[]{:S(2)}, u32[]{:S(2)}) collective-permute-start(f32[2,128,128]{2,1,0:T(8,128)S(1)} %get-tuple-element.51), channel_id=1, source_target_pairs={{0,24},{1,25},{2,26},{3,27},{4,28},{5,29},{6,30},{7,31},{8,0},{9,1... | collective-permute-start | bytes 393224 | tf_op jit(solution)/shard_map/ppermute | solution.py:456
  76.5 3.1 %collective-permute-done.14.wave = f32[2,128,128]{2,1,0:T(8,128)S(1)} collective-permute-done((f32[2,128,128]{2,1,0:T(8,128)S(1)}, f32[2,128,128]{2,1,0:T(8,128)S(1)}, u32[]{:S(2)}, u32[]{:S(2)}) %collective-permute-start.14) | collective-permute-done | bytes 131104 | tf_op jit(solution)/shard_map/ppermute | solution.py:456
  79.7 3.2 %collective-permute-start.15 = (f32[2,128,128]{2,1,0:T(8,128)S(1)}, f32[2,128,128]{2,1,0:T(8,128)S(1)}, u32[]{:S(2)}, u32[]{:S(2)}) collective-permute-start(f32[2,128,128]{2,1,0:T(8,128)S(1)} %get-tuple-element.54), channel_id=1, source_target_pairs={{0,24},{1,25},{2,26},{3,27},{4,28},{5,29},{6,30},{7,31},{8,0},{9,1... | collective-permute-start | bytes 393224 | tf_op jit(solution)/shard_map/ppermute | solution.py:456
  82.9 4.3 %collective-permute-done.15.wave = f32[2,128,128]{2,1,0:T(8,128)S(1)} collective-permute-done((f32[2,128,128]{2,1,0:T(8,128)S(1)}, f32[2,128,128]{2,1,0:T(8,128)S(1)}, u32[]{:S(2)}, u32[]{:S(2)}) %collective-permute-start.15) | collective-permute-done | bytes 131104 | tf_op jit(solution)/shard_map/ppermute | solution.py:456
  87.2 3.6 %backward_stage.5 = (f32[2,2,128,128]{3,2,1,0:T(8,128)S(1)}, f32[2,2,128,128]{3,2,1,0:T(8,128)S(1)}) custom-call(f32[16,2,128,128]{3,2,1,0:T(8,128)S(1)} %get-tuple-element.41.windows, f32[2,128,128]{2,1,0:T(8,128)S(1)} %collective-permute-done.15.wave, f32[4,2,128,128]{3,2,1,0:T(8,128)S(1)} %get-tuple-element.48.saved, f32[2,128,128]{2,1,0:T(8,128)S(1)} %copy-done, ...), custom_call_target="tpu_custom_call" | custom-call | tf_op jit(solution)/shard_map/backward_stage/pallas_call | solution.py:424
  90.9 9.9 %collective-permute-start.18 = (f32[2,2,128,128]{3,2,1,0:T(8,128)S(1)}, f32[2,2,128,128]{3,2,1,0:T(8,128)S(1)}, u32[]{:S(2)}, u32[]{:S(2)}) collective-permute-start(f32[2,2,128,128]{3,2,1,0:T(8,128)S(1)} %get-tuple-element.59), channel_id=1, source_target_pairs={{0,33},{1,96},{2,35},{3,98},{4,37},{5,100},{6,39},{7,102},{8,41},{... | collective-permute-start | bytes 786440 | tf_op jit(solution)/shard_map/ppermute | solution.py:476
  100.8 4.7 %collective-permute-start.17 = (f32[2,2,128,128]{3,2,1,0:T(8,128)S(1)}, f32[2,2,128,128]{3,2,1,0:T(8,128)S(1)}, u32[]{:S(2)}, u32[]{:S(2)}) collective-permute-start(f32[2,2,128,128]{3,2,1,0:T(8,128)S(1)} %get-tuple-element.59), channel_id=1, source_target_pairs={{0,1},{1,0},{2,3},{3,2},{4,5},{5,4},{6,7},{7,6},{8,9},{9,8},{10,11... | collective-permute-start | bytes 786440 | tf_op jit(solution)/shard_map/ppermute | solution.py:461
  105.5 2.1 %collective-permute-done.18.moved_other = f32[2,2,128,128]{3,2,1,0:T(8,128)S(1)} collective-permute-done((f32[2,2,128,128]{3,2,1,0:T(8,128)S(1)}, f32[2,2,128,128]{3,2,1,0:T(8,128)S(1)}, u32[]{:S(2)}, u32[]{:S(2)}) %collective-permute-start.18) | collective-permute-done | bytes 262176 | tf_op jit(solution)/shard_map/ppermute | solution.py:476
  107.6 2.0 %paste_windows.1 = f32[2,2,128,512]{3,2,1,0:T(8,128)} custom-call(s32[2,2]{1,0:T(2,128)S(1)} %copy-done.6, s32[8,128]{1,0:T(8,128)S(1)} %slice_convert_fusion.before, f32[2,2,128,128]{3,2,1,0:T(8,128)S(1)} %get-tuple-element.57.same, f32[2,2,128,128]{3,2,1,0:T(8,128)S(1)} %collective-permute-done.17.other, ...), custom_call_target="tpu_custom_call" | custom-call | tf_op jit(solution)/shard_map/paste_windows/pallas_call | solution.py:222
  (43 shorter events, 4.8 us)
Async XLA Ops:
  0.0 12.6 %copy-start.6 = (s32[2,2]{1,0:T(2,128)S(1)}, s32[2,2]{1,0:T(2,128)}, u32[]{:S(2)}) copy-start(s32[2,2]{1,0:T(2,128)} %offsets.3) | copy-start | bytes 52
  1.6 5.2 %collective-permute-start = (f32[136,128]{1,0:T(8,128)S(1)}, f32[136,128]{1,0:T(8,128)S(1)}, u32[]{:S(2)}, u32[]{:S(2)}) collective-permute-start(f32[136,128]{1,0:T(8,128)S(1)} %select_maximum_fusion), channel_id=1, source_target_pairs={{0,32},{32,64},{64,96},{96,0},{1,33},{33,65},{65,97},{97,1},{2,34}... | collective-permute-start | bytes 208904 | tf_op jit(solution)/shard_map/ppermute | solution.py:485
  3.7 0.9 copy-start.1
  4.6 1.2 %copy-start.3 = (f32[2,2,128,512]{3,2,1,0:T(8,128)S(1)}, f32[2,2,128,512]{3,2,1,0:T(8,128)}, u32[]{:S(2)}) copy-start(f32[2,2,128,512]{3,2,1,0:T(8,128)} %field.1) | copy-start | bytes 3145732
  5.8 0.9 copy-start.4
  6.8 34.6 %copy-start = (f32[2,128,128]{2,1,0:T(8,128)S(1)}, f32[2,128,128]{2,1,0:T(8,128)}, u32[]{:S(2)}) copy-start(f32[2,128,128]{2,1,0:T(8,128)} %constant.34.clone.twiddle) | copy-start | bytes 393220
  6.9 0.7 copy-start.5
  8.6 6.5 %collective-permute-start.1 = (f32[2,2,128,128]{3,2,1,0:T(8,128)S(1)}, f32[2,2,128,128]{3,2,1,0:T(8,128)S(1)}, u32[]{:S(2)}, u32[]{:S(2)}) collective-permute-start(f32[2,2,128,128]{3,2,1,0:T(8,128)S(1)} %get-tuple-element.37), channel_id=1, source_target_pairs={{0,96},{1,33},{2,98},{3,35},{4,100},{5,37},{6,102},{7,39},{8,104},... | collective-permute-start | bytes 786440 | tf_op jit(solution)/shard_map/ppermute | solution.py:476
  9.9 5.2 %collective-permute-start.2 = (f32[2,2,128,128]{3,2,1,0:T(8,128)S(1)}, f32[2,2,128,128]{3,2,1,0:T(8,128)S(1)}, u32[]{:S(2)}, u32[]{:S(2)}) collective-permute-start(f32[2,2,128,128]{3,2,1,0:T(8,128)S(1)} %get-tuple-element.38), channel_id=1, source_target_pairs={{0,1},{1,0},{2,3},{3,2},{4,5},{5,4},{6,7},{7,6},{8,9},{9,8},{10,11... | collective-permute-start | bytes 786440 | tf_op jit(solution)/shard_map/ppermute | solution.py:461
  12.1 7.0 %collective-permute-start.3 = (f32[2,2,128,128]{3,2,1,0:T(8,128)S(1)}, f32[2,2,128,128]{3,2,1,0:T(8,128)S(1)}, u32[]{:S(2)}, u32[]{:S(2)}) collective-permute-start(f32[2,2,128,128]{3,2,1,0:T(8,128)S(1)} %get-tuple-element.39), channel_id=1, source_target_pairs={{0,33},{1,96},{2,35},{3,98},{4,37},{5,100},{6,39},{7,102},{8,41},{... | collective-permute-start | bytes 786440 | tf_op jit(solution)/shard_map/ppermute | solution.py:476
  19.2 7.8 %collective-permute-start.4 = (f32[2,2,128,128]{3,2,1,0:T(8,128)S(1)}, f32[2,2,128,128]{3,2,1,0:T(8,128)S(1)}, u32[]{:S(2)}, u32[]{:S(2)}) collective-permute-start(f32[2,2,128,128]{3,2,1,0:T(8,128)S(1)} %pad_maximum_fusion.near0), channel_id=1, source_target_pairs={{0,6},{1,7},{2,0},{3,1},{4,2},{5,3},{6,4},{7,5},{8,14},{9,15},{10,... | collective-permute-start | bytes 786440 | tf_op jit(solution)/shard_map/ppermute | solution.py:450
  22.0 8.4 %collective-permute-start.7 = (f32[2,2,128,128]{3,2,1,0:T(8,128)S(1)}, f32[2,2,128,128]{3,2,1,0:T(8,128)S(1)}, u32[]{:S(2)}, u32[]{:S(2)}) collective-permute-start(f32[2,2,128,128]{3,2,1,0:T(8,128)S(1)} %pad_maximum_fusion.1.near1), channel_id=1, source_target_pairs={{0,2},{1,3},{2,4},{3,5},{4,6},{5,7},{6,0},{7,1},{8,10},{9,11},{10,... | collective-permute-start | bytes 786440 | tf_op jit(solution)/shard_map/ppermute | solution.py:450
  22.1 13.7 %collective-permute-start.9 = (f32[2,2,128,128]{3,2,1,0:T(8,128)S(1)}, f32[2,2,128,128]{3,2,1,0:T(8,128)S(1)}, u32[]{:S(2)}, u32[]{:S(2)}) collective-permute-start(f32[2,2,128,128]{3,2,1,0:T(8,128)S(1)} %pad_maximum_fusion.near0), channel_id=1, source_target_pairs={{0,2},{1,3},{2,4},{3,5},{4,6},{5,7},{6,0},{7,1},{8,10},{9,11},{10,... | collective-permute-start | bytes 786440 | tf_op jit(solution)/shard_map/ppermute | solution.py:450
  22.2 13.6 %collective-permute-start.5 = (f32[2,2,128,128]{3,2,1,0:T(8,128)S(1)}, f32[2,2,128,128]{3,2,1,0:T(8,128)S(1)}, u32[]{:S(2)}, u32[]{:S(2)}) collective-permute-start(f32[2,2,128,128]{3,2,1,0:T(8,128)S(1)} %pad_maximum_fusion.1.near1), channel_id=1, source_target_pairs={{0,6},{1,7},{2,0},{3,1},{4,2},{5,3},{6,4},{7,5},{8,14},{9,15},{10,... | collective-permute-start | bytes 786440 | tf_op jit(solution)/shard_map/ppermute | solution.py:450
  27.0 11.2 %collective-permute-start.6 = (f32[2,2,128,128]{3,2,1,0:T(8,128)S(1)}, f32[2,2,128,128]{3,2,1,0:T(8,128)S(1)}, u32[]{:S(2)}, u32[]{:S(2)}) collective-permute-start(f32[2,2,128,128]{3,2,1,0:T(8,128)S(1)} %collective-permute-done.4.up0), channel_id=1, source_target_pairs={{0,6},{1,7},{2,0},{3,1},{4,2},{5,3},{6,4},{7,5},{8,14},{9,15},{10,... | collective-permute-start | bytes 786440 | tf_op jit(solution)/shard_map/ppermute | solution.py:450
  30.4 11.0 %collective-permute-start.8 = (f32[2,2,128,128]{3,2,1,0:T(8,128)S(1)}, f32[2,2,128,128]{3,2,1,0:T(8,128)S(1)}, u32[]{:S(2)}, u32[]{:S(2)}) collective-permute-start(f32[2,2,128,128]{3,2,1,0:T(8,128)S(1)} %collective-permute-done.7.down1), channel_id=1, source_target_pairs={{0,2},{1,3},{2,4},{3,5},{4,6},{5,7},{6,0},{7,1},{8,10},{9,11},{10,... | collective-permute-start | bytes 786440 | tf_op jit(solution)/shard_map/ppermute | solution.py:450
  45.4 5.1 %collective-permute-start.10 = (f32[2,128,128]{2,1,0:T(8,128)S(1)}, f32[2,128,128]{2,1,0:T(8,128)S(1)}, u32[]{:S(2)}, u32[]{:S(2)}) collective-permute-start(f32[2,128,128]{2,1,0:T(8,128)S(1)} %get-tuple-element.42), channel_id=1, source_target_pairs={{0,8},{1,9},{2,10},{3,11},{4,12},{5,13},{6,14},{7,15},{8,16},{9,17... | collective-permute-start | bytes 393224 | tf_op jit(solution)/shard_map/ppermute | solution.py:456
  50.5 6.5 %copy-start.7 = (f32[2,128,128]{2,1,0:T(8,128)S(1)}, f32[2,128,128]{2,1,0:T(8,128)}, u32[]{:S(2)}) copy-start(f32[2,128,128]{2,1,0:T(8,128)} %param.9) | copy-start | bytes 393220
  50.5 10.3 %copy-start.2 = (f32[2,128,128]{2,1,0:T(8,128)S(1)}, f32[2,128,128]{2,1,0:T(8,128)}, u32[]{:S(2)}) copy-start(f32[2,128,128]{2,1,0:T(8,128)} %constant.35.clone.chirp) | copy-start | bytes 393220
  50.5 5.1 %collective-permute-start.11 = (f32[2,128,128]{2,1,0:T(8,128)S(1)}, f32[2,128,128]{2,1,0:T(8,128)S(1)}, u32[]{:S(2)}, u32[]{:S(2)}) collective-permute-start(f32[2,128,128]{2,1,0:T(8,128)S(1)} %get-tuple-element.44), channel_id=1, source_target_pairs={{0,8},{1,9},{2,10},{3,11},{4,12},{5,13},{6,14},{7,15},{8,16},{9,17... | collective-permute-start | bytes 393224 | tf_op jit(solution)/shard_map/ppermute | solution.py:456
  55.7 5.1 %collective-permute-start.12 = (f32[2,128,128]{2,1,0:T(8,128)S(1)}, f32[2,128,128]{2,1,0:T(8,128)S(1)}, u32[]{:S(2)}, u32[]{:S(2)}) collective-permute-start(f32[2,128,128]{2,1,0:T(8,128)S(1)} %get-tuple-element.46), channel_id=1, source_target_pairs={{0,8},{1,9},{2,10},{3,11},{4,12},{5,13},{6,14},{7,15},{8,16},{9,17... | collective-permute-start | bytes 393224 | tf_op jit(solution)/shard_map/ppermute | solution.py:456
  60.8 12.6 %collective-permute-start.13 = (f32[2,128,128]{2,1,0:T(8,128)S(1)}, f32[2,128,128]{2,1,0:T(8,128)S(1)}, u32[]{:S(2)}, u32[]{:S(2)}) collective-permute-start(f32[2,128,128]{2,1,0:T(8,128)S(1)} %get-tuple-element.47), channel_id=1, source_target_pairs={{0,24},{1,25},{2,26},{3,27},{4,28},{5,29},{6,30},{7,31},{8,0},{9,1... | collective-permute-start | bytes 393224 | tf_op jit(solution)/shard_map/ppermute | solution.py:456
  73.4 6.2 %collective-permute-start.14 = (f32[2,128,128]{2,1,0:T(8,128)S(1)}, f32[2,128,128]{2,1,0:T(8,128)S(1)}, u32[]{:S(2)}, u32[]{:S(2)}) collective-permute-start(f32[2,128,128]{2,1,0:T(8,128)S(1)} %get-tuple-element.51), channel_id=1, source_target_pairs={{0,24},{1,25},{2,26},{3,27},{4,28},{5,29},{6,30},{7,31},{8,0},{9,1... | collective-permute-start | bytes 393224 | tf_op jit(solution)/shard_map/ppermute | solution.py:456
  79.7 7.6 %collective-permute-start.15 = (f32[2,128,128]{2,1,0:T(8,128)S(1)}, f32[2,128,128]{2,1,0:T(8,128)S(1)}, u32[]{:S(2)}, u32[]{:S(2)}) collective-permute-start(f32[2,128,128]{2,1,0:T(8,128)S(1)} %get-tuple-element.54), channel_id=1, source_target_pairs={{0,24},{1,25},{2,26},{3,27},{4,28},{5,29},{6,30},{7,31},{8,0},{9,1... | collective-permute-start | bytes 393224 | tf_op jit(solution)/shard_map/ppermute | solution.py:456
  90.8 9.9 %collective-permute-start.16 = (f32[2,2,128,128]{3,2,1,0:T(8,128)S(1)}, f32[2,2,128,128]{3,2,1,0:T(8,128)S(1)}, u32[]{:S(2)}, u32[]{:S(2)}) collective-permute-start(f32[2,2,128,128]{3,2,1,0:T(8,128)S(1)} %get-tuple-element.57.same), channel_id=1, source_target_pairs={{0,32},{1,97},{2,34},{3,99},{4,36},{5,101},{6,38},{7,103},{8,40},{... | collective-permute-start | bytes 786440 | tf_op jit(solution)/shard_map/ppermute | solution.py:476
  90.9 16.7 %collective-permute-start.18 = (f32[2,2,128,128]{3,2,1,0:T(8,128)S(1)}, f32[2,2,128,128]{3,2,1,0:T(8,128)S(1)}, u32[]{:S(2)}, u32[]{:S(2)}) collective-permute-start(f32[2,2,128,128]{3,2,1,0:T(8,128)S(1)} %get-tuple-element.59), channel_id=1, source_target_pairs={{0,33},{1,96},{2,35},{3,98},{4,37},{5,100},{6,39},{7,102},{8,41},{... | collective-permute-start | bytes 786440 | tf_op jit(solution)/shard_map/ppermute | solution.py:476
  100.8 6.9 %collective-permute-start.17 = (f32[2,2,128,128]{3,2,1,0:T(8,128)S(1)}, f32[2,2,128,128]{3,2,1,0:T(8,128)S(1)}, u32[]{:S(2)}, u32[]{:S(2)}) collective-permute-start(f32[2,2,128,128]{3,2,1,0:T(8,128)S(1)} %get-tuple-element.59), channel_id=1, source_target_pairs={{0,1},{1,0},{2,3},{3,2},{4,5},{5,4},{6,7},{7,6},{8,9},{9,8},{10,11... | collective-permute-start | bytes 786440 | tf_op jit(solution)/shard_map/ppermute | solution.py:461

commit v5 on v4

--- a/solution.py
+++ b/solution.py
@@ -20,9 +20,9 @@
 F32 = jnp.float32
 PARAMS = pltpu.CompilerParams(vmem_limit_bytes=20 << 20)
 GROUP = 8
-PITCH = GROUP + 1
+PITCH = N // GROUP + 1
 TRAIL = pltpu.VMEM((PER_STAGE + 1,) + PLANE, F32)
-ROW_STAGES = pltpu.VMEM((2, 2, 160, N), F32)
+ROW_STAGES = pltpu.VMEM((2, 2, 176, N), F32)
 WAVE = jax.ShapeDtypeStruct(PLANE, F32)
 PIECE = jax.ShapeDtypeStruct((PER_DEVICE,) + PLANE, F32)
 SAVED = jax.ShapeDtypeStruct((PER_CHIP,) + PLANE, F32)
@@ -36,7 +36,7 @@
     index = np.arange(N)
     turn = np.exp(1j * np.pi * (index * index % (2 * N)) / N)
     chirp = np.outer(turn, turn)
-    first, second = np.divmod(index, GROUP)
+    first, second = np.divmod(index, N // GROUP)
     twiddle = np.exp(-2j * np.pi * first * second / N)[:, None] * np.ones((1, N))
     tables = (twiddle, np.conj(chirp))
     return tuple(np.stack([t.real, t.imag]).astype(np.float32) for t in tables)
@@ -79,21 +79,20 @@
 
 
 def transform_rows(real, imag, twiddle, stage, put):
-    groups = [
-        (real[GROUP * k : GROUP * (k + 1)], imag[GROUP * k : GROUP * (k + 1)])
-        for k in range(N // GROUP)
-    ]
-    for k, value in enumerate(transform(groups)):
-        rows = pl.ds(GROUP * k, GROUP)
-        if k:
-            value = times(*value, twiddle[0, rows], twiddle[1, rows])
-        rows = pl.ds(PITCH * k, GROUP)
-        stage[0, rows], stage[1, rows] = value
     for part in range(2):
-        picked = [pl.ds(PITCH * GROUP * part + k, GROUP, stride=PITCH) for k in range(GROUP)]
-        done = transform([(stage[0, rows], stage[1, rows]) for rows in picked])
+        blocks = []
         for k in range(GROUP):
-            put(2 * k + part, done[k])
+            rows = slice(N // GROUP * k + GROUP * part, N // GROUP * k + GROUP * (part + 1))
+            blocks.append((real[rows], imag[rows]))
+        for k, value in enumerate(transform(blocks)):
+            rows = pl.ds(N // GROUP * k + GROUP * part, GROUP)
+            if k:
+                value = times(*value, twiddle[0, rows], twiddle[1, rows])
+            rows = pl.ds(PITCH * k + GROUP * part, GROUP)
+            stage[0, rows], stage[1, rows] = value
+    picked = [pl.ds(k, GROUP, stride=PITCH) for k in range(N // GROUP)]
+    for k, value in enumerate(transform([(stage[0, rows], stage[1, rows]) for rows in picked])):
+        put(k, value)
 
 
 def advance(real, imag, target, twiddle, stages):
@@ -115,10 +114,11 @@
     return previous, number
 
 
-def corner(offsets, before, core, kind):
+def corner(corners, core, kind):
     previous, number = role(core, kind)
-    row = jnp.where(previous == 1, before[number, 0], offsets[number, 0]) % N
-    column = jnp.where(previous == 1, before[number, 1], offsets[number, 1])
+    line = 2 * previous + number
+    row = corners[line, 0] % N
+    column = corners[line, 1]
     tile = column // N
     after = pl.multiple_of(jnp.minimum(tile + 1, 3) * N, N)
     low = jnp.where(previous == 1, 0, row)
@@ -156,40 +156,54 @@
     return device // (CORES * RING), device // CORES % RING, device % CORES
 
 
-def load_kernel(field, chirp, probe, field_out, chirp_out, probe_out):
+def load_kernel(field, chirp, offsets, field_out, chirp_out, offsets_out):
     field_out[...] = field[...]
     chirp_out[...] = chirp[...]
-    probe_out[...] = probe[...]
-
-
-def cut_kernel(offsets, before, field, chirp, probe, same, other, moved_same, moved_other, wave):
-    core = here()[2]
-    for kind, target in ((2, moved_same), (3, moved_other), (0, same), (1, other)):
-        cut(corner(offsets, before, core, kind), field, chirp, target)
-    place = corner(offsets, before, core, 0)
+    offsets_out[...] = offsets[...]
+
+
+def wave_kernel(corners, chirp, probe, wave):
+    place = corner(corners, here()[2], 0)
     rolled = [pltpu.roll(pltpu.roll(probe[k], place[0], 0), place[5], 1) for k in range(2)]
     real, imag = times(*rolled, chirp[0], chirp[1])
     wave[0] = -imag
     wave[1] = real
 
 
-def load(field, chirp, probe):
+def cut_kernel(corners, field, chirp, same, other, moved_same, moved_other):
+    core = here()[2]
+    for kind, target in ((2, moved_same), (3, moved_other), (0, same), (1, other)):
+        cut(corner(corners, core, kind), field, chirp, target)
+
+
+def load(field, chirp, offsets):
+    whole = jax.ShapeDtypeStruct(field.shape, F32)
     return pl.pallas_call(
         load_kernel,
-        out_shape=(jax.ShapeDtypeStruct(field.shape, F32), WAVE, WAVE),
+        out_shape=(whole, WAVE, jax.ShapeDtypeStruct(offsets.shape, offsets.dtype)),
         name="load",
         compiler_params=PARAMS,
-    )(field, chirp, probe)
-
-
-def cut_windows(offsets, before, field, chirp, probe):
+    )(field, chirp, offsets)
+
+
+def cut_windows(corners, field, chirp):
     return pl.pallas_call(
         cut_kernel,
-        out_shape=(PIECE,) * 4 + (WAVE,),
-        in_specs=[SMEM_SPEC] * 2 + [VMEM_SPEC] * 3,
+        out_shape=(PIECE,) * 4,
+        in_specs=[SMEM_SPEC] + [VMEM_SPEC] * 2,
         name="cut_windows",
         compiler_params=PARAMS,
-    )(offsets, before, field, chirp, probe)
+    )(corners, field, chirp)
+
+
+def first_wave(corners, chirp, probe):
+    return pl.pallas_call(
+        wave_kernel,
+        out_shape=WAVE,
+        in_specs=[SMEM_SPEC] + [VMEM_SPEC] * 2,
+        name="first_wave",
+        compiler_params=PARAMS,
+    )(corners, chirp, probe)
 
 
 def paste(place, value, target):
@@ -201,9 +215,9 @@
     target[:, pl.ds(after, N)] += jnp.where(rows & (lane < shift), value, 0.0)
 
 
-def paste_kernel(offsets, before, same, other, moved_same, moved_other, out, total, sems):
+def paste_kernel(corners, same, other, moved_same, moved_other, out, total, sems):
     core = here()[2]
-    places = [corner(offsets, before, core, kind) for kind in range(4)]
+    places = [corner(corners, core, kind) for kind in range(4)]
     copies = []
     total[...] = jnp.zeros(total.shape, F32)
     for layer in range(PER_DEVICE):
@@ -218,16 +232,16 @@
         copy.wait()
 
 
-def paste_windows(offsets, before, pieces, shape):
+def paste_windows(corners, pieces, shape):
     return pl.pallas_call(
         paste_kernel,
         out_shape=jax.ShapeDtypeStruct(shape, F32),
-        in_specs=[SMEM_SPEC] * 2 + [VMEM_SPEC] * 4,
+        in_specs=[SMEM_SPEC] + [VMEM_SPEC] * 4,
         out_specs=ANY_SPEC,
         scratch_shapes=[pltpu.VMEM(shape, F32), pltpu.SemaphoreType.DMA((PER_DEVICE, 2))],
         name="paste_windows",
         compiler_params=PARAMS,
-    )(offsets, before, *pieces)
+    )(corners, *pieces)
 
 
 def steps(first, count, change, windows, trail, twiddle, stages):
@@ -480,15 +494,15 @@
     twiddle, chirp = tables
     core = lax.axis_index("depth") % CORES
     rows = lax.axis_size("pos")
-    padding = ((0, GROUP - offsets.shape[0]), (0, N - offsets.shape[1]))
-    message = jnp.concatenate([intensity[1], jnp.pad(offsets.astype(F32), padding)])
-    message = lax.ppermute(message, "pos", [(i, (i + 1) % rows) for i in range(rows)])
-    before = message[N:].astype(jnp.int32)
-    measured = jnp.where(core == 0, intensity[0], message[:N])
-
-    field, chirp_here, probe_here = load(object_field, chirp, probe)
-    cuts = cut_windows(offsets, before, field, chirp_here, probe_here)
-    same, other, moved_same, moved_other, wave = cuts
+    onward = [(i, (i + 1) % rows) for i in range(rows)]
+    intensity_before = lax.ppermute(intensity, "pos", onward)
+    before = lax.ppermute(offsets, "pos", onward)
+    before, intensity_before = lax.optimization_barrier((before, intensity_before))
+    field, chirp_here, offsets = load(object_field, chirp, offsets)
+    corners = jnp.concatenate([offsets, before])
+    measured = jnp.where(core == 0, intensity[0], intensity_before[1])
+
+    same, other, moved_same, moved_other = cut_windows(corners, field, chirp_here)
     moved_same = across(moved_same, 0, False)
     moved_other = across(moved_other, 1, False)
     other = swap_cores(other)
@@ -512,8 +526,9 @@
         )
         up.append(along_ring(near[-1], -1))
         down.append(along_ring(near[-1], 1))
-    far = [along_ring(up[0], -1), along_ring(down[1], 1)]
-
+    far = [along_ring(down[0], 1), along_ring(up[1], -1)]
+
+    wave = first_wave(corners, chirp, probe)
     wave, saved, windows = first_stage((*near, *up, *far, *down), wave, twiddle)
     for section in range(1, STAGES - 1):
         wave = along_stages(wave, 1)
@@ -529,10 +544,9 @@
     same, other = backward_stage(0, windows, wave, saved, twiddle, chirp, same, other)
     moved_same = across(same, 0, True)
     moved_other = across(other, 1, True)
-    other, moved_same = lax.optimization_barrier((other, moved_same))
     other = swap_cores(other)
     pieces = (same, other, moved_same, moved_other)
-    return paste_windows(offsets, before, pieces, object_field.shape)
+    return paste_windows(corners, pieces, object_field.shape)
 
 
 def solution(mesh):

time: 110 us -> 105 us (0.955)
  starting transfers between devices: 50.7 us -> 43.9 us
  waiting for transfers between devices: 40 us -> 44.2 us
  local copies, waits for them, and re-layouts: 5.69 us -> 3.92 us
    ppermute x4, waiting for transfers between devices: 6.16 us -> 11 us  [across(): return lax.ppermute(value, ('pos', 'depth'), pairs)]
    ppermute x2, starting transfers between devices: 6.87 us -> 2.66 us  [swap_cores(): lax.ppermute(value, 'depth', [(device, device ^ 1) for device in range(de...]
    ppermute x6, starting transfers between devices: 9.03 us -> 7.03 us  [along_ring(): return lax.ppermute(value, 'depth', pairs)]
    ppermute x1 -> x2, starting transfers between devices: 2.11 us -> 3.25 us  [the longest x1 2.04 us: body(): intensity_before = lax.ppermute(intensity, 'pos', onward)]
    unnamed x16 -> x14, local copies, waits for them, and re-layouts: 3.76 us -> 2.83 us
  transfers between devices with their start and end apart: 19 -> 20, of which waited for: 13 -> 14; matrix products, arithmetic and copies ran while one was open for 1% -> 1% of each run, Pallas kernels for 0% -> 1%
where the time goes in v5:
time: 105 us
  waiting for transfers between devices  44.2 us (42%)
  starting transfers between devices  43.9 us (42%)
  Pallas kernels  11.2 us (11%)
  local copies, waits for them, and re-layouts  3.92 us (4%)
  between operations  1.48 us (1%)
    ppermute x6, waiting for transfers between devices, along_stages(): return lax.ppermute(value, 'depth', pairs)  20.7 us
    ppermute x6, starting transfers between devices, along_stages(): return lax.ppermute(value, 'depth', pairs)  20.2 us
    ppermute x6, waiting for transfers between devices, along_ring(): return lax.ppermute(value, 'depth', pairs)  12.3 us
    ppermute x4, waiting for transfers between devices, across(): return lax.ppermute(value, ('pos', 'depth'), pairs)  11 us
    ppermute x4, starting transfers between devices, across(): return lax.ppermute(value, ('pos', 'depth'), pairs)  10.7 us
    ppermute x6, starting transfers between devices, along_ring(): return lax.ppermute(value, 'depth', pairs)  7.03 us
    pallas_call x1, Pallas kernels, first_stage(): pl.pallas_call(first_kernel, out_shape=(WAVE, SAVED, STACK), in_specs=[VM...  3.87 us
    pallas_call x3, Pallas kernels, backward_stage(): pl.pallas_call(last_backward_kernel if last else functools.partial(backwa...  3.58 us
  transfers between devices with their start and end apart: 20, of which 14 were waited for; matrix products, arithmetic and copies ran while one was open for 1% of the time, Pallas kernels for 1%

profile of v5, /device:TPU:1, one launch (start us, length us, event | category | flops | bytes accessed | tf_op | source)
XLA Modules:
  0.0 104.8 jit_solution(14188286903997780734)
XLA Ops:
  0.0 2.0 %collective-permute-start.1 = (f32[2,128,128]{2,1,0:T(8,128)}, f32[2,128,128]{2,1,0:T(8,128)S(1)}, u32[]{:S(2)}, u32[]{:S(2)}) collective-permute-start(f32[2,128,128]{2,1,0:T(8,128)} %param.9), channel_id=1, source_target_pairs={{0,32},{32,64},{64,96},{96,0},{1,33},{33,65},{65,97},{97,1},{2,34}... | collective-permute-start | bytes 393224 | tf_op jit(solution)/shard_map/ppermute | solution.py:498
  2.0 1.2 %collective-permute-start = (s32[2,2]{1,0:T(2,128)}, s32[2,2]{1,0:T(2,128)S(1)}, u32[]{:S(2)}, u32[]{:S(2)}) collective-permute-start(s32[2,2]{1,0:T(2,128)} %offsets.1), channel_id=1, source_target_pairs={{0,32},{32,64},{64,96},{96,0},{1,33},{33,65},{65,97},{97,1},{2,34}... | collective-permute-start | bytes 56 | tf_op jit(solution)/shard_map/ppermute | solution.py:499
  3.3 0.9 copy-done.1
  4.2 1.2 %copy-done.3 = f32[2,2,128,512]{3,2,1,0:T(8,128)S(1)} copy-done((f32[2,2,128,512]{3,2,1,0:T(8,128)S(1)}, f32[2,2,128,512]{3,2,1,0:T(8,128)}, u32[]{:S(2)}) %copy-start.3) | copy-done | bytes 1048600
  6.3 1.0 cut_windows.1
  7.3 0.9 collective-permute-start.2
  8.2 2.7 %collective-permute-start.3 = (f32[2,2,128,128]{3,2,1,0:T(8,128)S(1)}, f32[2,2,128,128]{3,2,1,0:T(8,128)S(1)}, u32[]{:S(2)}, u32[]{:S(2)}) collective-permute-start(f32[2,2,128,128]{3,2,1,0:T(8,128)S(1)} %get-tuple-element.38), channel_id=1, source_target_pairs={{0,1},{1,0},{2,3},{3,2},{4,5},{5,4},{6,7},{7,6},{8,9},{9,8},{10,11... | collective-permute-start | bytes 786440 | tf_op jit(solution)/shard_map/ppermute | solution.py:475
  13.8 4.0 %collective-permute-done.4 = f32[2,2,128,128]{3,2,1,0:T(8,128)S(1)} collective-permute-done((f32[2,2,128,128]{3,2,1,0:T(8,128)S(1)}, f32[2,2,128,128]{3,2,1,0:T(8,128)S(1)}, u32[]{:S(2)}, u32[]{:S(2)}) %collective-permute-start.4) | collective-permute-done | bytes 262176 | tf_op jit(solution)/shard_map/ppermute | solution.py:490
  18.0 1.4 %collective-permute-start.7 = (f32[2,2,128,128]{3,2,1,0:T(8,128)S(1)}, f32[2,2,128,128]{3,2,1,0:T(8,128)S(1)}, u32[]{:S(2)}, u32[]{:S(2)}) collective-permute-start(f32[2,2,128,128]{3,2,1,0:T(8,128)S(1)} %pad_maximum_fusion.near0), channel_id=1, source_target_pairs={{0,2},{1,3},{2,4},{3,5},{4,6},{5,7},{6,0},{7,1},{8,10},{9,11},{10,... | collective-permute-start | bytes 786440 | tf_op jit(solution)/shard_map/ppermute | solution.py:464
  19.3 1.5 %collective-permute-start.6 = (f32[2,2,128,128]{3,2,1,0:T(8,128)S(1)}, f32[2,2,128,128]{3,2,1,0:T(8,128)S(1)}, u32[]{:S(2)}, u32[]{:S(2)}) collective-permute-start(f32[2,2,128,128]{3,2,1,0:T(8,128)S(1)} %pad_maximum_fusion.1.near1), channel_id=1, source_target_pairs={{0,6},{1,7},{2,0},{3,1},{4,2},{5,3},{6,4},{7,5},{8,14},{9,15},{10,... | collective-permute-start | bytes 786440 | tf_op jit(solution)/shard_map/ppermute | solution.py:464
  20.9 1.4 %collective-permute-start.5 = (f32[2,2,128,128]{3,2,1,0:T(8,128)S(1)}, f32[2,2,128,128]{3,2,1,0:T(8,128)S(1)}, u32[]{:S(2)}, u32[]{:S(2)}) collective-permute-start(f32[2,2,128,128]{3,2,1,0:T(8,128)S(1)} %pad_maximum_fusion.near0), channel_id=1, source_target_pairs={{0,6},{1,7},{2,0},{3,1},{4,2},{5,3},{6,4},{7,5},{8,14},{9,15},{10,... | collective-permute-start | bytes 786440 | tf_op jit(solution)/shard_map/ppermute | solution.py:464
  22.3 4.5 %collective-permute-done.7.down0 = f32[2,2,128,128]{3,2,1,0:T(8,128)S(1)} collective-permute-done((f32[2,2,128,128]{3,2,1,0:T(8,128)S(1)}, f32[2,2,128,128]{3,2,1,0:T(8,128)S(1)}, u32[]{:S(2)}, u32[]{:S(2)}) %collective-permute-start.7) | collective-permute-done | bytes 262176 | tf_op jit(solution)/shard_map/ppermute | solution.py:464
  26.8 2.7 %collective-permute-start.9 = (f32[2,2,128,128]{3,2,1,0:T(8,128)S(1)}, f32[2,2,128,128]{3,2,1,0:T(8,128)S(1)}, u32[]{:S(2)}, u32[]{:S(2)}) collective-permute-start(f32[2,2,128,128]{3,2,1,0:T(8,128)S(1)} %collective-permute-done.6.up1), channel_id=1, source_target_pairs={{0,6},{1,7},{2,0},{3,1},{4,2},{5,3},{6,4},{7,5},{8,14},{9,15},{10,... | collective-permute-start | bytes 786440 | tf_op jit(solution)/shard_map/ppermute | solution.py:464
  29.5 0.7 first_wave.1.wave
  30.2 1.7 %collective-permute-done.5.up0 = f32[2,2,128,128]{3,2,1,0:T(8,128)S(1)} collective-permute-done((f32[2,2,128,128]{3,2,1,0:T(8,128)S(1)}, f32[2,2,128,128]{3,2,1,0:T(8,128)S(1)}, u32[]{:S(2)}, u32[]{:S(2)}) %collective-permute-start.5) | collective-permute-done | bytes 262176 | tf_op jit(solution)/shard_map/ppermute | solution.py:464
  32.4 5.6 %collective-permute-done.8.far0 = f32[2,2,128,128]{3,2,1,0:T(8,128)S(1)} collective-permute-done((f32[2,2,128,128]{3,2,1,0:T(8,128)S(1)}, f32[2,2,128,128]{3,2,1,0:T(8,128)S(1)}, u32[]{:S(2)}, u32[]{:S(2)}) %collective-permute-start.8) | collective-permute-done | bytes 262176 | tf_op jit(solution)/shard_map/ppermute | solution.py:464
  38.1 3.9 %first_stage.1 = (f32[2,128,128]{2,1,0:T(8,128)S(1)}, f32[4,2,128,128]{3,2,1,0:T(8,128)S(1)}, f32[16,2,128,128]{3,2,1,0:T(8,128)S(1)}) custom-call(f32[2,2,128,128]{3,2,1,0:T(8,128)S(1)} %pad_maximum_fusion.near0, f32[2,2,128,128]{3,2,1,0:T(8,128)S(1)} %pad_maximum_fusion.1.near1, f32[2,2,128,128]{3,2,1,0:T(8,128)S(1)} %collective-permute-done.5.up0, ...), custom_call_target="tpu_custom_call" | custom-call | tf_op jit(solution)/shard_map/first_stage/pallas_call | solution.py:416
  42.0 5.0 %collective-permute-done.11.wave = f32[2,128,128]{2,1,0:T(8,128)S(1)} collective-permute-done((f32[2,128,128]{2,1,0:T(8,128)S(1)}, f32[2,128,128]{2,1,0:T(8,128)S(1)}, u32[]{:S(2)}, u32[]{:S(2)}) %collective-permute-start.11) | collective-permute-done | bytes 131104 | tf_op jit(solution)/shard_map/ppermute | solution.py:470
  47.1 2.4 %collective-permute-start.12 = (f32[2,128,128]{2,1,0:T(8,128)S(1)}, f32[2,128,128]{2,1,0:T(8,128)S(1)}, u32[]{:S(2)}, u32[]{:S(2)}) collective-permute-start(f32[2,128,128]{2,1,0:T(8,128)S(1)} %get-tuple-element.43), channel_id=1, source_target_pairs={{0,8},{1,9},{2,10},{3,11},{4,12},{5,13},{6,14},{7,15},{8,16},{9,17... | collective-permute-start | bytes 393224 | tf_op jit(solution)/shard_map/ppermute | solution.py:470
  49.5 2.7 %collective-permute-done.12.wave = f32[2,128,128]{2,1,0:T(8,128)S(1)} collective-permute-done((f32[2,128,128]{2,1,0:T(8,128)S(1)}, f32[2,128,128]{2,1,0:T(8,128)S(1)}, u32[]{:S(2)}, u32[]{:S(2)}) %collective-permute-start.12) | collective-permute-done | bytes 131104 | tf_op jit(solution)/shard_map/ppermute | solution.py:470
  52.2 1.2 %collective-permute-start.13 = (f32[2,128,128]{2,1,0:T(8,128)S(1)}, f32[2,128,128]{2,1,0:T(8,128)S(1)}, u32[]{:S(2)}, u32[]{:S(2)}) collective-permute-start(f32[2,128,128]{2,1,0:T(8,128)S(1)} %get-tuple-element.45), channel_id=1, source_target_pairs={{0,8},{1,9},{2,10},{3,11},{4,12},{5,13},{6,14},{7,15},{8,16},{9,17... | collective-permute-start | bytes 393224 | tf_op jit(solution)/shard_map/ppermute | solution.py:470
  53.4 3.9 %collective-permute-done.13.wave = f32[2,128,128]{2,1,0:T(8,128)S(1)} collective-permute-done((f32[2,128,128]{2,1,0:T(8,128)S(1)}, f32[2,128,128]{2,1,0:T(8,128)S(1)}, u32[]{:S(2)}, u32[]{:S(2)}) %collective-permute-start.13) | collective-permute-done | bytes 131104 | tf_op jit(solution)/shard_map/ppermute | solution.py:470
  57.3 10.2 %collective-permute-start.14 = (f32[2,128,128]{2,1,0:T(8,128)S(1)}, f32[2,128,128]{2,1,0:T(8,128)S(1)}, u32[]{:S(2)}, u32[]{:S(2)}) collective-permute-start(f32[2,128,128]{2,1,0:T(8,128)S(1)} %get-tuple-element.47), channel_id=1, source_target_pairs={{0,24},{1,25},{2,26},{3,27},{4,28},{5,29},{6,30},{7,31},{8,0},{9,1... | collective-permute-start | bytes 393224 | tf_op jit(solution)/shard_map/ppermute | solution.py:470
  67.5 1.9 %collective-permute-done.14.wave = f32[2,128,128]{2,1,0:T(8,128)S(1)} collective-permute-done((f32[2,128,128]{2,1,0:T(8,128)S(1)}, f32[2,128,128]{2,1,0:T(8,128)S(1)}, u32[]{:S(2)}, u32[]{:S(2)}) %collective-permute-start.14) | collective-permute-done | bytes 131104 | tf_op jit(solution)/shard_map/ppermute | solution.py:470
  69.5 3.1 %collective-permute-start.15 = (f32[2,128,128]{2,1,0:T(8,128)S(1)}, f32[2,128,128]{2,1,0:T(8,128)S(1)}, u32[]{:S(2)}, u32[]{:S(2)}) collective-permute-start(f32[2,128,128]{2,1,0:T(8,128)S(1)} %get-tuple-element.51), channel_id=1, source_target_pairs={{0,24},{1,25},{2,26},{3,27},{4,28},{5,29},{6,30},{7,31},{8,0},{9,1... | collective-permute-start | bytes 393224 | tf_op jit(solution)/shard_map/ppermute | solution.py:470
  72.7 2.5 %collective-permute-done.15.wave = f32[2,128,128]{2,1,0:T(8,128)S(1)} collective-permute-done((f32[2,128,128]{2,1,0:T(8,128)S(1)}, f32[2,128,128]{2,1,0:T(8,128)S(1)}, u32[]{:S(2)}, u32[]{:S(2)}) %collective-permute-start.15) | collective-permute-done | bytes 131104 | tf_op jit(solution)/shard_map/ppermute | solution.py:470
  75.2 3.2 %collective-permute-start.16 = (f32[2,128,128]{2,1,0:T(8,128)S(1)}, f32[2,128,128]{2,1,0:T(8,128)S(1)}, u32[]{:S(2)}, u32[]{:S(2)}) collective-permute-start(f32[2,128,128]{2,1,0:T(8,128)S(1)} %get-tuple-element.54), channel_id=1, source_target_pairs={{0,24},{1,25},{2,26},{3,27},{4,28},{5,29},{6,30},{7,31},{8,0},{9,1... | collective-permute-start | bytes 393224 | tf_op jit(solution)/shard_map/ppermute | solution.py:470
  78.4 4.7 %collective-permute-done.16.wave = f32[2,128,128]{2,1,0:T(8,128)S(1)} collective-permute-done((f32[2,128,128]{2,1,0:T(8,128)S(1)}, f32[2,128,128]{2,1,0:T(8,128)S(1)}, u32[]{:S(2)}, u32[]{:S(2)}) %collective-permute-start.16) | collective-permute-done | bytes 131104 | tf_op jit(solution)/shard_map/ppermute | solution.py:470
  83.1 3.5 %backward_stage.5 = (f32[2,2,128,128]{3,2,1,0:T(8,128)S(1)}, f32[2,2,128,128]{3,2,1,0:T(8,128)S(1)}) custom-call(f32[16,2,128,128]{3,2,1,0:T(8,128)S(1)} %get-tuple-element.40.windows, f32[2,128,128]{2,1,0:T(8,128)S(1)} %collective-permute-done.16.wave, f32[4,2,128,128]{3,2,1,0:T(8,128)S(1)} %get-tuple-element.48.saved, f32[2,128,128]{2,1,0:T(8,128)S(1)} %copy-done, ...), custom_call_target="tpu_custom_call" | custom-call | tf_op jit(solution)/shard_map/backward_stage/pallas_call | solution.py:438
  86.7 9.3 %collective-permute-start.19 = (f32[2,2,128,128]{3,2,1,0:T(8,128)S(1)}, f32[2,2,128,128]{3,2,1,0:T(8,128)S(1)}, u32[]{:S(2)}, u32[]{:S(2)}) collective-permute-start(f32[2,2,128,128]{3,2,1,0:T(8,128)S(1)} %get-tuple-element.58), channel_id=1, source_target_pairs={{0,33},{1,96},{2,35},{3,98},{4,37},{5,100},{6,39},{7,102},{8,41},{... | collective-permute-start | bytes 786440 | tf_op jit(solution)/shard_map/ppermute | solution.py:490
  96.0 6.9 %collective-permute-done.19.moved_other = f32[2,2,128,128]{3,2,1,0:T(8,128)S(1)} collective-permute-done((f32[2,2,128,128]{3,2,1,0:T(8,128)S(1)}, f32[2,2,128,128]{3,2,1,0:T(8,128)S(1)}, u32[]{:S(2)}, u32[]{:S(2)}) %collective-permute-start.19) | collective-permute-done | bytes 262176 | tf_op jit(solution)/shard_map/ppermute | solution.py:490
  102.9 1.9 %paste_windows.1 = f32[2,2,128,512]{3,2,1,0:T(8,128)} custom-call(s32[4,2]{1,0:T(4,128)S(1)} %pad_add_fusion.corners, f32[2,2,128,128]{3,2,1,0:T(8,128)S(1)} %get-tuple-element.57.same, f32[2,2,128,128]{3,2,1,0:T(8,128)S(1)} %collective-permute-done.17.other, f32[2,2,128,128]{3,2,1,0:T(8,128)S(1)} %collective-permute-done.18.moved_same, ...), custom_call_target="tpu_custom_call" | custom-call | tf_op jit(solution)/shard_map/paste_windows/pallas_call | solution.py:236
  (41 shorter events, 3.5 us)
Async XLA Ops:
  0.0 6.3 %collective-permute-start.1 = (f32[2,128,128]{2,1,0:T(8,128)}, f32[2,128,128]{2,1,0:T(8,128)S(1)}, u32[]{:S(2)}, u32[]{:S(2)}) collective-permute-start(f32[2,128,128]{2,1,0:T(8,128)} %param.9), channel_id=1, source_target_pairs={{0,32},{32,64},{64,96},{96,0},{1,33},{33,65},{65,97},{97,1},{2,34}... | collective-permute-start | bytes 393224 | tf_op jit(solution)/shard_map/ppermute | solution.py:498
  2.0 4.3 %collective-permute-start = (s32[2,2]{1,0:T(2,128)}, s32[2,2]{1,0:T(2,128)S(1)}, u32[]{:S(2)}, u32[]{:S(2)}) collective-permute-start(s32[2,2]{1,0:T(2,128)} %offsets.1), channel_id=1, source_target_pairs={{0,32},{32,64},{64,96},{96,0},{1,33},{33,65},{65,97},{97,1},{2,34}... | collective-permute-start | bytes 56 | tf_op jit(solution)/shard_map/ppermute | solution.py:499
  3.3 0.9 copy-start.1
  4.2 1.2 %copy-start.3 = (f32[2,2,128,512]{3,2,1,0:T(8,128)S(1)}, f32[2,2,128,512]{3,2,1,0:T(8,128)}, u32[]{:S(2)}) copy-start(f32[2,2,128,512]{3,2,1,0:T(8,128)} %field.1) | copy-start | bytes 3145732
  5.4 0.7 copy-start.5
  6.1 23.4 %copy-start.2 = (f32[2,128,128]{2,1,0:T(8,128)S(1)}, f32[2,128,128]{2,1,0:T(8,128)}, u32[]{:S(2)}) copy-start(f32[2,128,128]{2,1,0:T(8,128)} %constant.33.clone.chirp) | copy-start | bytes 393220
  6.2 23.4 %copy-start.4 = (f32[2,128,128]{2,1,0:T(8,128)S(1)}, f32[2,128,128]{2,1,0:T(8,128)}, u32[]{:S(2)}) copy-start(f32[2,128,128]{2,1,0:T(8,128)} %probe.1) | copy-start | bytes 393220
  6.3 31.8 %copy-start = (f32[2,128,128]{2,1,0:T(8,128)S(1)}, f32[2,128,128]{2,1,0:T(8,128)}, u32[]{:S(2)}) copy-start(f32[2,128,128]{2,1,0:T(8,128)} %constant.32.clone.twiddle) | copy-start | bytes 393220
  7.3 6.5 %collective-permute-start.2 = (f32[2,2,128,128]{3,2,1,0:T(8,128)S(1)}, f32[2,2,128,128]{3,2,1,0:T(8,128)S(1)}, u32[]{:S(2)}, u32[]{:S(2)}) collective-permute-start(f32[2,2,128,128]{3,2,1,0:T(8,128)S(1)} %get-tuple-element.37), channel_id=1, source_target_pairs={{0,96},{1,33},{2,98},{3,35},{4,100},{5,37},{6,102},{7,39},{8,104},... | collective-permute-start | bytes 786440 | tf_op jit(solution)/shard_map/ppermute | solution.py:490
  8.2 5.6 %collective-permute-start.3 = (f32[2,2,128,128]{3,2,1,0:T(8,128)S(1)}, f32[2,2,128,128]{3,2,1,0:T(8,128)S(1)}, u32[]{:S(2)}, u32[]{:S(2)}) collective-permute-start(f32[2,2,128,128]{3,2,1,0:T(8,128)S(1)} %get-tuple-element.38), channel_id=1, source_target_pairs={{0,1},{1,0},{2,3},{3,2},{4,5},{5,4},{6,7},{7,6},{8,9},{9,8},{10,11... | collective-permute-start | bytes 786440 | tf_op jit(solution)/shard_map/ppermute | solution.py:475
  10.8 7.0 %collective-permute-start.4 = (f32[2,2,128,128]{3,2,1,0:T(8,128)S(1)}, f32[2,2,128,128]{3,2,1,0:T(8,128)S(1)}, u32[]{:S(2)}, u32[]{:S(2)}) collective-permute-start(f32[2,2,128,128]{3,2,1,0:T(8,128)S(1)} %get-tuple-element.39), channel_id=1, source_target_pairs={{0,33},{1,96},{2,35},{3,98},{4,37},{5,100},{6,39},{7,102},{8,41},{... | collective-permute-start | bytes 786440 | tf_op jit(solution)/shard_map/ppermute | solution.py:490
  18.0 8.9 %collective-permute-start.7 = (f32[2,2,128,128]{3,2,1,0:T(8,128)S(1)}, f32[2,2,128,128]{3,2,1,0:T(8,128)S(1)}, u32[]{:S(2)}, u32[]{:S(2)}) collective-permute-start(f32[2,2,128,128]{3,2,1,0:T(8,128)S(1)} %pad_maximum_fusion.near0), channel_id=1, source_target_pairs={{0,2},{1,3},{2,4},{3,5},{4,6},{5,7},{6,0},{7,1},{8,10},{9,11},{10,... | collective-permute-start | bytes 786440 | tf_op jit(solution)/shard_map/ppermute | solution.py:464
  19.3 7.5 %collective-permute-start.6 = (f32[2,2,128,128]{3,2,1,0:T(8,128)S(1)}, f32[2,2,128,128]{3,2,1,0:T(8,128)S(1)}, u32[]{:S(2)}, u32[]{:S(2)}) collective-permute-start(f32[2,2,128,128]{3,2,1,0:T(8,128)S(1)} %pad_maximum_fusion.1.near1), channel_id=1, source_target_pairs={{0,6},{1,7},{2,0},{3,1},{4,2},{5,3},{6,4},{7,5},{8,14},{9,15},{10,... | collective-permute-start | bytes 786440 | tf_op jit(solution)/shard_map/ppermute | solution.py:464
  20.9 11.1 %collective-permute-start.5 = (f32[2,2,128,128]{3,2,1,0:T(8,128)S(1)}, f32[2,2,128,128]{3,2,1,0:T(8,128)S(1)}, u32[]{:S(2)}, u32[]{:S(2)}) collective-permute-start(f32[2,2,128,128]{3,2,1,0:T(8,128)S(1)} %pad_maximum_fusion.near0), channel_id=1, source_target_pairs={{0,6},{1,7},{2,0},{3,1},{4,2},{5,3},{6,4},{7,5},{8,14},{9,15},{10,... | collective-permute-start | bytes 786440 | tf_op jit(solution)/shard_map/ppermute | solution.py:464
  22.3 10.1 %collective-permute-start.10 = (f32[2,2,128,128]{3,2,1,0:T(8,128)S(1)}, f32[2,2,128,128]{3,2,1,0:T(8,128)S(1)}, u32[]{:S(2)}, u32[]{:S(2)}) collective-permute-start(f32[2,2,128,128]{3,2,1,0:T(8,128)S(1)} %pad_maximum_fusion.1.near1), channel_id=1, source_target_pairs={{0,2},{1,3},{2,4},{3,5},{4,6},{5,7},{6,0},{7,1},{8,10},{9,11},{10,... | collective-permute-start | bytes 786440 | tf_op jit(solution)/shard_map/ppermute | solution.py:464
  26.8 11.2 %collective-permute-start.8 = (f32[2,2,128,128]{3,2,1,0:T(8,128)S(1)}, f32[2,2,128,128]{3,2,1,0:T(8,128)S(1)}, u32[]{:S(2)}, u32[]{:S(2)}) collective-permute-start(f32[2,2,128,128]{3,2,1,0:T(8,128)S(1)} %collective-permute-done.7.down0), channel_id=1, source_target_pairs={{0,2},{1,3},{2,4},{3,5},{4,6},{5,7},{6,0},{7,1},{8,10},{9,11},{10,... | collective-permute-start | bytes 786440 | tf_op jit(solution)/shard_map/ppermute | solution.py:464
  26.8 11.2 %collective-permute-start.9 = (f32[2,2,128,128]{3,2,1,0:T(8,128)S(1)}, f32[2,2,128,128]{3,2,1,0:T(8,128)S(1)}, u32[]{:S(2)}, u32[]{:S(2)}) collective-permute-start(f32[2,2,128,128]{3,2,1,0:T(8,128)S(1)} %collective-permute-done.6.up1), channel_id=1, source_target_pairs={{0,6},{1,7},{2,0},{3,1},{4,2},{5,3},{6,4},{7,5},{8,14},{9,15},{10,... | collective-permute-start | bytes 786440 | tf_op jit(solution)/shard_map/ppermute | solution.py:464
  41.9 5.1 %collective-permute-start.11 = (f32[2,128,128]{2,1,0:T(8,128)S(1)}, f32[2,128,128]{2,1,0:T(8,128)S(1)}, u32[]{:S(2)}, u32[]{:S(2)}) collective-permute-start(f32[2,128,128]{2,1,0:T(8,128)S(1)} %get-tuple-element.41), channel_id=1, source_target_pairs={{0,8},{1,9},{2,10},{3,11},{4,12},{5,13},{6,14},{7,15},{8,16},{9,17... | collective-permute-start | bytes 393224 | tf_op jit(solution)/shard_map/ppermute | solution.py:470
  47.1 6.3 %copy-start.6 = (f32[2,128,128]{2,1,0:T(8,128)S(1)}, f32[2,128,128]{2,1,0:T(8,128)}, u32[]{:S(2)}) copy-start(f32[2,128,128]{2,1,0:T(8,128)} %param.9) | copy-start | bytes 393220
  47.1 5.1 %collective-permute-start.12 = (f32[2,128,128]{2,1,0:T(8,128)S(1)}, f32[2,128,128]{2,1,0:T(8,128)S(1)}, u32[]{:S(2)}, u32[]{:S(2)}) collective-permute-start(f32[2,128,128]{2,1,0:T(8,128)S(1)} %get-tuple-element.43), channel_id=1, source_target_pairs={{0,8},{1,9},{2,10},{3,11},{4,12},{5,13},{6,14},{7,15},{8,16},{9,17... | collective-permute-start | bytes 393224 | tf_op jit(solution)/shard_map/ppermute | solution.py:470
  52.2 5.1 %collective-permute-start.13 = (f32[2,128,128]{2,1,0:T(8,128)S(1)}, f32[2,128,128]{2,1,0:T(8,128)S(1)}, u32[]{:S(2)}, u32[]{:S(2)}) collective-permute-start(f32[2,128,128]{2,1,0:T(8,128)S(1)} %get-tuple-element.45), channel_id=1, source_target_pairs={{0,8},{1,9},{2,10},{3,11},{4,12},{5,13},{6,14},{7,15},{8,16},{9,17... | collective-permute-start | bytes 393224 | tf_op jit(solution)/shard_map/ppermute | solution.py:470
  57.3 12.1 %collective-permute-start.14 = (f32[2,128,128]{2,1,0:T(8,128)S(1)}, f32[2,128,128]{2,1,0:T(8,128)S(1)}, u32[]{:S(2)}, u32[]{:S(2)}) collective-permute-start(f32[2,128,128]{2,1,0:T(8,128)S(1)} %get-tuple-element.47), channel_id=1, source_target_pairs={{0,24},{1,25},{2,26},{3,27},{4,28},{5,29},{6,30},{7,31},{8,0},{9,1... | collective-permute-start | bytes 393224 | tf_op jit(solution)/shard_map/ppermute | solution.py:470
  69.5 5.7 %collective-permute-start.15 = (f32[2,128,128]{2,1,0:T(8,128)S(1)}, f32[2,128,128]{2,1,0:T(8,128)S(1)}, u32[]{:S(2)}, u32[]{:S(2)}) collective-permute-start(f32[2,128,128]{2,1,0:T(8,128)S(1)} %get-tuple-element.51), channel_id=1, source_target_pairs={{0,24},{1,25},{2,26},{3,27},{4,28},{5,29},{6,30},{7,31},{8,0},{9,1... | collective-permute-start | bytes 393224 | tf_op jit(solution)/shard_map/ppermute | solution.py:470
  75.2 7.8 %collective-permute-start.16 = (f32[2,128,128]{2,1,0:T(8,128)S(1)}, f32[2,128,128]{2,1,0:T(8,128)S(1)}, u32[]{:S(2)}, u32[]{:S(2)}) collective-permute-start(f32[2,128,128]{2,1,0:T(8,128)S(1)} %get-tuple-element.54), channel_id=1, source_target_pairs={{0,24},{1,25},{2,26},{3,27},{4,28},{5,29},{6,30},{7,31},{8,0},{9,1... | collective-permute-start | bytes 393224 | tf_op jit(solution)/shard_map/ppermute | solution.py:470
  86.6 9.4 %collective-permute-start.18 = (f32[2,2,128,128]{3,2,1,0:T(8,128)S(1)}, f32[2,2,128,128]{3,2,1,0:T(8,128)S(1)}, u32[]{:S(2)}, u32[]{:S(2)}) collective-permute-start(f32[2,2,128,128]{3,2,1,0:T(8,128)S(1)} %get-tuple-element.57.same), channel_id=1, source_target_pairs={{0,32},{1,97},{2,34},{3,99},{4,36},{5,101},{6,38},{7,103},{8,40},{... | collective-permute-start | bytes 786440 | tf_op jit(solution)/shard_map/ppermute | solution.py:490
  86.7 16.2 %collective-permute-start.19 = (f32[2,2,128,128]{3,2,1,0:T(8,128)S(1)}, f32[2,2,128,128]{3,2,1,0:T(8,128)S(1)}, u32[]{:S(2)}, u32[]{:S(2)}) collective-permute-start(f32[2,2,128,128]{3,2,1,0:T(8,128)S(1)} %get-tuple-element.58), channel_id=1, source_target_pairs={{0,33},{1,96},{2,35},{3,98},{4,37},{5,100},{6,39},{7,102},{8,41},{... | collective-permute-start | bytes 786440 | tf_op jit(solution)/shard_map/ppermute | solution.py:490
  96.0 6.9 %collective-permute-start.17 = (f32[2,2,128,128]{3,2,1,0:T(8,128)S(1)}, f32[2,2,128,128]{3,2,1,0:T(8,128)S(1)}, u32[]{:S(2)}, u32[]{:S(2)}) collective-permute-start(f32[2,2,128,128]{3,2,1,0:T(8,128)S(1)} %get-tuple-element.58), channel_id=1, source_target_pairs={{0,1},{1,0},{2,3},{3,2},{4,5},{5,4},{6,7},{7,6},{8,9},{9,8},{10,11... | collective-permute-start | bytes 786440 | tf_op jit(solution)/shard_map/ppermute | solution.py:475

commit v6 on v5

--- a/solution.py
+++ b/solution.py
@@ -495,12 +495,10 @@
     core = lax.axis_index("depth") % CORES
     rows = lax.axis_size("pos")
     onward = [(i, (i + 1) % rows) for i in range(rows)]
-    intensity_before = lax.ppermute(intensity, "pos", onward)
-    before = lax.ppermute(offsets, "pos", onward)
-    before, intensity_before = lax.optimization_barrier((before, intensity_before))
+    padded = jnp.pad(offsets, ((0, N - offsets.shape[0]), (0, N - offsets.shape[1])))
+    before = lax.ppermute(padded, "pos", onward)[: offsets.shape[0], : offsets.shape[1]]
     field, chirp_here, offsets = load(object_field, chirp, offsets)
     corners = jnp.concatenate([offsets, before])
-    measured = jnp.where(core == 0, intensity[0], intensity_before[1])
 
     same, other, moved_same, moved_other = cut_windows(corners, field, chirp_here)
     moved_same = across(moved_same, 0, False)
@@ -530,10 +528,13 @@
 
     wave = first_wave(corners, chirp, probe)
     wave, saved, windows = first_stage((*near, *up, *far, *down), wave, twiddle)
+    wave, intensity = lax.optimization_barrier((wave, intensity))
+    intensity_before = lax.ppermute(intensity, "pos", onward)
     for section in range(1, STAGES - 1):
         wave = along_stages(wave, 1)
         wave, saved = forward_stage(section, windows, wave, saved, twiddle)
     wave = along_stages(wave, 1)
+    measured = jnp.where(core == 0, intensity[0], intensity_before[1])
     wave, same, other = turn_stage(STAGES - 1, windows, wave, measured, twiddle, chirp)
     for section in reversed(range(1, STAGES - 1)):
         wave = along_stages(wave, -1)

time: 105 us -> 104 us (level)
  starting transfers between devices: 43.9 us -> 42.6 us
    ppermute x1, starting transfers between devices: 2.04 us -> 0.01 us  [body(): intensity_before = lax.ppermute(intensity, 'pos', onward)]
    ppermute x1, waiting for transfers between devices: 0.01 us -> 1.4 us  [body(): intensity_before = lax.ppermute(intensity, 'pos', onward)]
    ppermute x6, waiting for transfers between devices: 20.7 us -> 19.6 us  [along_stages(): return lax.ppermute(value, 'depth', pairs)]
  transfers between devices with their start and end apart: 20 -> 20, of which waited for: 14 -> 13; matrix products, arithmetic and copies ran while one was open for 1% -> 1% of each run, Pallas kernels for 1% -> 1%
where the time goes in v6:
time: 104 us
  waiting for transfers between devices  44.2 us (42%)
  starting transfers between devices  42.6 us (41%)
  Pallas kernels  11.2 us (11%)
  local copies, waits for them, and re-layouts  4.61 us (4%)
  between operations  1.52 us (1%)
    ppermute x6, starting transfers between devices, along_stages(): return lax.ppermute(value, 'depth', pairs)  19.9 us
    ppermute x6, waiting for transfers between devices, along_stages(): return lax.ppermute(value, 'depth', pairs)  19.6 us
    ppermute x6, waiting for transfers between devices, along_ring(): return lax.ppermute(value, 'depth', pairs)  12.2 us
    ppermute x4, starting transfers between devices, across(): return lax.ppermute(value, ('pos', 'depth'), pairs)  11.3 us
    ppermute x4, waiting for transfers between devices, across(): return lax.ppermute(value, ('pos', 'depth'), pairs)  11 us
    ppermute x6, starting transfers between devices, along_ring(): return lax.ppermute(value, 'depth', pairs)  7.03 us
    pallas_call x1, Pallas kernels, first_stage(): pl.pallas_call(first_kernel, out_shape=(WAVE, SAVED, STACK), in_specs=[VM...  3.87 us
    pallas_call x3, Pallas kernels, backward_stage(): pl.pallas_call(last_backward_kernel if last else functools.partial(backwa...  3.58 us
  transfers between devices with their start and end apart: 20, of which 13 were waited for; matrix products, arithmetic and copies ran while one was open for 1% of the time, Pallas kernels for 1%

profile of v6, /device:TPU:1, one launch (start us, length us, event | category | flops | bytes accessed | tf_op | source)
XLA Modules:
  0.0 104.2 jit_solution(2278479474723937366)
XLA Ops:
  0.7 2.0 %collective-permute-start = (s32[128,128]{1,0:T(8,128)S(1)}, s32[128,128]{1,0:T(8,128)S(1)}, u32[]{:S(2)}, u32[]{:S(2)}) collective-permute-start(s32[128,128]{1,0:T(8,128)S(1)} %pad.4), channel_id=1, source_target_pairs={{0,32},{32,64},{64,96},{96,0},{1,33},{33,65},{65,97},{97,1},{2,34}... | collective-permute-start | bytes 196616 | tf_op jit(solution)/shard_map/ppermute | solution.py:499
  2.7 0.9 copy-done.1
  3.6 1.2 %copy-done.3 = f32[2,2,128,512]{3,2,1,0:T(8,128)S(1)} copy-done((f32[2,2,128,512]{3,2,1,0:T(8,128)S(1)}, f32[2,2,128,512]{3,2,1,0:T(8,128)}, u32[]{:S(2)}) %copy-start.3) | copy-done | bytes 1048600
  5.7 1.0 cut_windows.1
  6.6 1.3 %collective-permute-start.1 = (f32[2,2,128,128]{3,2,1,0:T(8,128)S(1)}, f32[2,2,128,128]{3,2,1,0:T(8,128)S(1)}, u32[]{:S(2)}, u32[]{:S(2)}) collective-permute-start(f32[2,2,128,128]{3,2,1,0:T(8,128)S(1)} %get-tuple-element.36), channel_id=1, source_target_pairs={{0,96},{1,33},{2,98},{3,35},{4,100},{5,37},{6,102},{7,39},{8,104},... | collective-permute-start | bytes 786440 | tf_op jit(solution)/shard_map/ppermute | solution.py:490
  7.9 2.3 %collective-permute-start.2 = (f32[2,2,128,128]{3,2,1,0:T(8,128)S(1)}, f32[2,2,128,128]{3,2,1,0:T(8,128)S(1)}, u32[]{:S(2)}, u32[]{:S(2)}) collective-permute-start(f32[2,2,128,128]{3,2,1,0:T(8,128)S(1)} %get-tuple-element.37), channel_id=1, source_target_pairs={{0,1},{1,0},{2,3},{3,2},{4,5},{5,4},{6,7},{7,6},{8,9},{9,8},{10,11... | collective-permute-start | bytes 786440 | tf_op jit(solution)/shard_map/ppermute | solution.py:475
  13.2 4.1 %collective-permute-done.3 = f32[2,2,128,128]{3,2,1,0:T(8,128)S(1)} collective-permute-done((f32[2,2,128,128]{3,2,1,0:T(8,128)S(1)}, f32[2,2,128,128]{3,2,1,0:T(8,128)S(1)}, u32[]{:S(2)}, u32[]{:S(2)}) %collective-permute-start.3) | collective-permute-done | bytes 262176 | tf_op jit(solution)/shard_map/ppermute | solution.py:490
  17.4 1.4 %collective-permute-start.6 = (f32[2,2,128,128]{3,2,1,0:T(8,128)S(1)}, f32[2,2,128,128]{3,2,1,0:T(8,128)S(1)}, u32[]{:S(2)}, u32[]{:S(2)}) collective-permute-start(f32[2,2,128,128]{3,2,1,0:T(8,128)S(1)} %pad_maximum_fusion.near0), channel_id=1, source_target_pairs={{0,2},{1,3},{2,4},{3,5},{4,6},{5,7},{6,0},{7,1},{8,10},{9,11},{10,... | collective-permute-start | bytes 786440 | tf_op jit(solution)/shard_map/ppermute | solution.py:464
  18.8 1.5 %collective-permute-start.5 = (f32[2,2,128,128]{3,2,1,0:T(8,128)S(1)}, f32[2,2,128,128]{3,2,1,0:T(8,128)S(1)}, u32[]{:S(2)}, u32[]{:S(2)}) collective-permute-start(f32[2,2,128,128]{3,2,1,0:T(8,128)S(1)} %pad_maximum_fusion.1.near1), channel_id=1, source_target_pairs={{0,6},{1,7},{2,0},{3,1},{4,2},{5,3},{6,4},{7,5},{8,14},{9,15},{10,... | collective-permute-start | bytes 786440 | tf_op jit(solution)/shard_map/ppermute | solution.py:464
  20.3 1.4 %collective-permute-start.4 = (f32[2,2,128,128]{3,2,1,0:T(8,128)S(1)}, f32[2,2,128,128]{3,2,1,0:T(8,128)S(1)}, u32[]{:S(2)}, u32[]{:S(2)}) collective-permute-start(f32[2,2,128,128]{3,2,1,0:T(8,128)S(1)} %pad_maximum_fusion.near0), channel_id=1, source_target_pairs={{0,6},{1,7},{2,0},{3,1},{4,2},{5,3},{6,4},{7,5},{8,14},{9,15},{10,... | collective-permute-start | bytes 786440 | tf_op jit(solution)/shard_map/ppermute | solution.py:464
  21.8 4.4 %collective-permute-done.6.down0 = f32[2,2,128,128]{3,2,1,0:T(8,128)S(1)} collective-permute-done((f32[2,2,128,128]{3,2,1,0:T(8,128)S(1)}, f32[2,2,128,128]{3,2,1,0:T(8,128)S(1)}, u32[]{:S(2)}, u32[]{:S(2)}) %collective-permute-start.6) | collective-permute-done | bytes 262176 | tf_op jit(solution)/shard_map/ppermute | solution.py:464
  26.1 2.7 %collective-permute-start.8 = (f32[2,2,128,128]{3,2,1,0:T(8,128)S(1)}, f32[2,2,128,128]{3,2,1,0:T(8,128)S(1)}, u32[]{:S(2)}, u32[]{:S(2)}) collective-permute-start(f32[2,2,128,128]{3,2,1,0:T(8,128)S(1)} %collective-permute-done.5.up1), channel_id=1, source_target_pairs={{0,6},{1,7},{2,0},{3,1},{4,2},{5,3},{6,4},{7,5},{8,14},{9,15},{10,... | collective-permute-start | bytes 786440 | tf_op jit(solution)/shard_map/ppermute | solution.py:464
  28.8 0.7 first_wave.1.wave
  29.5 1.8 %collective-permute-done.4.up0 = f32[2,2,128,128]{3,2,1,0:T(8,128)S(1)} collective-permute-done((f32[2,2,128,128]{3,2,1,0:T(8,128)S(1)}, f32[2,2,128,128]{3,2,1,0:T(8,128)S(1)}, u32[]{:S(2)}, u32[]{:S(2)}) %collective-permute-start.4) | collective-permute-done | bytes 262176 | tf_op jit(solution)/shard_map/ppermute | solution.py:464
  31.8 5.6 %collective-permute-done.7.far0 = f32[2,2,128,128]{3,2,1,0:T(8,128)S(1)} collective-permute-done((f32[2,2,128,128]{3,2,1,0:T(8,128)S(1)}, f32[2,2,128,128]{3,2,1,0:T(8,128)S(1)}, u32[]{:S(2)}, u32[]{:S(2)}) %collective-permute-start.7) | collective-permute-done | bytes 262176 | tf_op jit(solution)/shard_map/ppermute | solution.py:464
  37.4 3.9 %first_stage.1 = (f32[2,128,128]{2,1,0:T(8,128)S(1)}, f32[4,2,128,128]{3,2,1,0:T(8,128)S(1)}, f32[16,2,128,128]{3,2,1,0:T(8,128)S(1)}) custom-call(f32[2,2,128,128]{3,2,1,0:T(8,128)S(1)} %pad_maximum_fusion.near0, f32[2,2,128,128]{3,2,1,0:T(8,128)S(1)} %pad_maximum_fusion.1.near1, f32[2,2,128,128]{3,2,1,0:T(8,128)S(1)} %collective-permute-done.4.up0, ...), custom_call_target="tpu_custom_call" | custom-call | tf_op jit(solution)/shard_map/first_stage/pallas_call | solution.py:416
  41.3 5.0 %collective-permute-done.10.wave = f32[2,128,128]{2,1,0:T(8,128)S(1)} collective-permute-done((f32[2,128,128]{2,1,0:T(8,128)S(1)}, f32[2,128,128]{2,1,0:T(8,128)S(1)}, u32[]{:S(2)}, u32[]{:S(2)}) %collective-permute-start.10) | collective-permute-done | bytes 131104 | tf_op jit(solution)/shard_map/ppermute | solution.py:470
  46.4 2.4 %collective-permute-start.11 = (f32[2,128,128]{2,1,0:T(8,128)S(1)}, f32[2,128,128]{2,1,0:T(8,128)S(1)}, u32[]{:S(2)}, u32[]{:S(2)}) collective-permute-start(f32[2,128,128]{2,1,0:T(8,128)S(1)} %get-tuple-element.43), channel_id=1, source_target_pairs={{0,8},{1,9},{2,10},{3,11},{4,12},{5,13},{6,14},{7,15},{8,16},{9,17... | collective-permute-start | bytes 393224 | tf_op jit(solution)/shard_map/ppermute | solution.py:470
  48.8 2.7 %collective-permute-done.11.wave = f32[2,128,128]{2,1,0:T(8,128)S(1)} collective-permute-done((f32[2,128,128]{2,1,0:T(8,128)S(1)}, f32[2,128,128]{2,1,0:T(8,128)S(1)}, u32[]{:S(2)}, u32[]{:S(2)}) %collective-permute-start.11) | collective-permute-done | bytes 131104 | tf_op jit(solution)/shard_map/ppermute | solution.py:470
  51.5 1.2 %collective-permute-start.12 = (f32[2,128,128]{2,1,0:T(8,128)S(1)}, f32[2,128,128]{2,1,0:T(8,128)S(1)}, u32[]{:S(2)}, u32[]{:S(2)}) collective-permute-start(f32[2,128,128]{2,1,0:T(8,128)S(1)} %get-tuple-element.45), channel_id=1, source_target_pairs={{0,8},{1,9},{2,10},{3,11},{4,12},{5,13},{6,14},{7,15},{8,16},{9,17... | collective-permute-start | bytes 393224 | tf_op jit(solution)/shard_map/ppermute | solution.py:470
  52.7 1.4 %collective-permute-done.13 = f32[2,128,128]{2,1,0:T(8,128)S(1)} collective-permute-done((f32[2,128,128]{2,1,0:T(8,128)S(1)}, f32[2,128,128]{2,1,0:T(8,128)S(1)}, u32[]{:S(2)}, u32[]{:S(2)}) %collective-permute-start.13) | collective-permute-done | bytes 131104 | tf_op jit(solution)/shard_map/ppermute | solution.py:532
  54.1 2.8 %collective-permute-done.12.wave = f32[2,128,128]{2,1,0:T(8,128)S(1)} collective-permute-done((f32[2,128,128]{2,1,0:T(8,128)S(1)}, f32[2,128,128]{2,1,0:T(8,128)S(1)}, u32[]{:S(2)}, u32[]{:S(2)}) %collective-permute-start.12) | collective-permute-done | bytes 131104 | tf_op jit(solution)/shard_map/ppermute | solution.py:470
  56.9 9.9 %collective-permute-start.14 = (f32[2,128,128]{2,1,0:T(8,128)S(1)}, f32[2,128,128]{2,1,0:T(8,128)S(1)}, u32[]{:S(2)}, u32[]{:S(2)}) collective-permute-start(f32[2,128,128]{2,1,0:T(8,128)S(1)} %get-tuple-element.47), channel_id=1, source_target_pairs={{0,24},{1,25},{2,26},{3,27},{4,28},{5,29},{6,30},{7,31},{8,0},{9,1... | collective-permute-start | bytes 393224 | tf_op jit(solution)/shard_map/ppermute | solution.py:470
  66.8 1.9 %collective-permute-done.14.wave = f32[2,128,128]{2,1,0:T(8,128)S(1)} collective-permute-done((f32[2,128,128]{2,1,0:T(8,128)S(1)}, f32[2,128,128]{2,1,0:T(8,128)S(1)}, u32[]{:S(2)}, u32[]{:S(2)}) %collective-permute-start.14) | collective-permute-done | bytes 131104 | tf_op jit(solution)/shard_map/ppermute | solution.py:470
  68.8 3.1 %collective-permute-start.15 = (f32[2,128,128]{2,1,0:T(8,128)S(1)}, f32[2,128,128]{2,1,0:T(8,128)S(1)}, u32[]{:S(2)}, u32[]{:S(2)}) collective-permute-start(f32[2,128,128]{2,1,0:T(8,128)S(1)} %get-tuple-element.51), channel_id=1, source_target_pairs={{0,24},{1,25},{2,26},{3,27},{4,28},{5,29},{6,30},{7,31},{8,0},{9,1... | collective-permute-start | bytes 393224 | tf_op jit(solution)/shard_map/ppermute | solution.py:470
  72.0 2.7 %collective-permute-done.15.wave = f32[2,128,128]{2,1,0:T(8,128)S(1)} collective-permute-done((f32[2,128,128]{2,1,0:T(8,128)S(1)}, f32[2,128,128]{2,1,0:T(8,128)S(1)}, u32[]{:S(2)}, u32[]{:S(2)}) %collective-permute-start.15) | collective-permute-done | bytes 131104 | tf_op jit(solution)/shard_map/ppermute | solution.py:470
  74.7 3.2 %collective-permute-start.16 = (f32[2,128,128]{2,1,0:T(8,128)S(1)}, f32[2,128,128]{2,1,0:T(8,128)S(1)}, u32[]{:S(2)}, u32[]{:S(2)}) collective-permute-start(f32[2,128,128]{2,1,0:T(8,128)S(1)} %get-tuple-element.54), channel_id=1, source_target_pairs={{0,24},{1,25},{2,26},{3,27},{4,28},{5,29},{6,30},{7,31},{8,0},{9,1... | collective-permute-start | bytes 393224 | tf_op jit(solution)/shard_map/ppermute | solution.py:470
  77.9 4.5 %collective-permute-done.16.wave = f32[2,128,128]{2,1,0:T(8,128)S(1)} collective-permute-done((f32[2,128,128]{2,1,0:T(8,128)S(1)}, f32[2,128,128]{2,1,0:T(8,128)S(1)}, u32[]{:S(2)}, u32[]{:S(2)}) %collective-permute-start.16) | collective-permute-done | bytes 131104 | tf_op jit(solution)/shard_map/ppermute | solution.py:470
  82.4 3.5 %backward_stage.5 = (f32[2,2,128,128]{3,2,1,0:T(8,128)S(1)}, f32[2,2,128,128]{3,2,1,0:T(8,128)S(1)}) custom-call(f32[16,2,128,128]{3,2,1,0:T(8,128)S(1)} %get-tuple-element.39.windows, f32[2,128,128]{2,1,0:T(8,128)S(1)} %collective-permute-done.16.wave, f32[4,2,128,128]{3,2,1,0:T(8,128)S(1)} %get-tuple-element.48.saved, f32[2,128,128]{2,1,0:T(8,128)S(1)} %copy-done, ...), custom_call_target="tpu_custom_call" | custom-call | tf_op jit(solution)/shard_map/backward_stage/pallas_call | solution.py:438
  86.0 9.5 %collective-permute-start.19 = (f32[2,2,128,128]{3,2,1,0:T(8,128)S(1)}, f32[2,2,128,128]{3,2,1,0:T(8,128)S(1)}, u32[]{:S(2)}, u32[]{:S(2)}) collective-permute-start(f32[2,2,128,128]{3,2,1,0:T(8,128)S(1)} %get-tuple-element.58), channel_id=1, source_target_pairs={{0,33},{1,96},{2,35},{3,98},{4,37},{5,100},{6,39},{7,102},{8,41},{... | collective-permute-start | bytes 786440 | tf_op jit(solution)/shard_map/ppermute | solution.py:490
  95.5 6.9 %collective-permute-done.19.moved_other = f32[2,2,128,128]{3,2,1,0:T(8,128)S(1)} collective-permute-done((f32[2,2,128,128]{3,2,1,0:T(8,128)S(1)}, f32[2,2,128,128]{3,2,1,0:T(8,128)S(1)}, u32[]{:S(2)}, u32[]{:S(2)}) %collective-permute-start.19) | collective-permute-done | bytes 262176 | tf_op jit(solution)/shard_map/ppermute | solution.py:490
  102.3 1.9 %paste_windows.1 = f32[2,2,128,512]{3,2,1,0:T(8,128)} custom-call(s32[4,2]{1,0:T(4,128)S(1)} %pad_add_fusion.corners, f32[2,2,128,128]{3,2,1,0:T(8,128)S(1)} %get-tuple-element.57.same, f32[2,2,128,128]{3,2,1,0:T(8,128)S(1)} %collective-permute-done.17.other, f32[2,2,128,128]{3,2,1,0:T(8,128)S(1)} %collective-permute-done.18.moved_same, ...), custom_call_target="tpu_custom_call" | custom-call | tf_op jit(solution)/shard_map/paste_windows/pallas_call | solution.py:236
  (43 shorter events, 3.9 us)
Async XLA Ops:
  0.7 5.0 %collective-permute-start = (s32[128,128]{1,0:T(8,128)S(1)}, s32[128,128]{1,0:T(8,128)S(1)}, u32[]{:S(2)}, u32[]{:S(2)}) collective-permute-start(s32[128,128]{1,0:T(8,128)S(1)} %pad.4), channel_id=1, source_target_pairs={{0,32},{32,64},{64,96},{96,0},{1,33},{33,65},{65,97},{97,1},{2,34}... | collective-permute-start | bytes 196616 | tf_op jit(solution)/shard_map/ppermute | solution.py:499
  2.7 0.9 copy-start.1
  3.6 1.2 %copy-start.3 = (f32[2,2,128,512]{3,2,1,0:T(8,128)S(1)}, f32[2,2,128,512]{3,2,1,0:T(8,128)}, u32[]{:S(2)}) copy-start(f32[2,2,128,512]{3,2,1,0:T(8,128)} %field.1) | copy-start | bytes 3145732
  4.9 0.7 copy-start.5
  5.6 23.2 %copy-start.2 = (f32[2,128,128]{2,1,0:T(8,128)S(1)}, f32[2,128,128]{2,1,0:T(8,128)}, u32[]{:S(2)}) copy-start(f32[2,128,128]{2,1,0:T(8,128)} %constant.33.clone.chirp) | copy-start | bytes 393220
  5.6 23.2 %copy-start.4 = (f32[2,128,128]{2,1,0:T(8,128)S(1)}, f32[2,128,128]{2,1,0:T(8,128)}, u32[]{:S(2)}) copy-start(f32[2,128,128]{2,1,0:T(8,128)} %probe.1) | copy-start | bytes 393220
  5.7 31.7 %copy-start = (f32[2,128,128]{2,1,0:T(8,128)S(1)}, f32[2,128,128]{2,1,0:T(8,128)}, u32[]{:S(2)}) copy-start(f32[2,128,128]{2,1,0:T(8,128)} %constant.32.clone.twiddle) | copy-start | bytes 393220
  6.6 6.5 %collective-permute-start.1 = (f32[2,2,128,128]{3,2,1,0:T(8,128)S(1)}, f32[2,2,128,128]{3,2,1,0:T(8,128)S(1)}, u32[]{:S(2)}, u32[]{:S(2)}) collective-permute-start(f32[2,2,128,128]{3,2,1,0:T(8,128)S(1)} %get-tuple-element.36), channel_id=1, source_target_pairs={{0,96},{1,33},{2,98},{3,35},{4,100},{5,37},{6,102},{7,39},{8,104},... | collective-permute-start | bytes 786440 | tf_op jit(solution)/shard_map/ppermute | solution.py:490
  7.9 5.2 %collective-permute-start.2 = (f32[2,2,128,128]{3,2,1,0:T(8,128)S(1)}, f32[2,2,128,128]{3,2,1,0:T(8,128)S(1)}, u32[]{:S(2)}, u32[]{:S(2)}) collective-permute-start(f32[2,2,128,128]{3,2,1,0:T(8,128)S(1)} %get-tuple-element.37), channel_id=1, source_target_pairs={{0,1},{1,0},{2,3},{3,2},{4,5},{5,4},{6,7},{7,6},{8,9},{9,8},{10,11... | collective-permute-start | bytes 786440 | tf_op jit(solution)/shard_map/ppermute | solution.py:475
  10.3 7.0 %collective-permute-start.3 = (f32[2,2,128,128]{3,2,1,0:T(8,128)S(1)}, f32[2,2,128,128]{3,2,1,0:T(8,128)S(1)}, u32[]{:S(2)}, u32[]{:S(2)}) collective-permute-start(f32[2,2,128,128]{3,2,1,0:T(8,128)S(1)} %get-tuple-element.38), channel_id=1, source_target_pairs={{0,33},{1,96},{2,35},{3,98},{4,37},{5,100},{6,39},{7,102},{8,41},{... | collective-permute-start | bytes 786440 | tf_op jit(solution)/shard_map/ppermute | solution.py:490
  17.4 8.7 %collective-permute-start.6 = (f32[2,2,128,128]{3,2,1,0:T(8,128)S(1)}, f32[2,2,128,128]{3,2,1,0:T(8,128)S(1)}, u32[]{:S(2)}, u32[]{:S(2)}) collective-permute-start(f32[2,2,128,128]{3,2,1,0:T(8,128)S(1)} %pad_maximum_fusion.near0), channel_id=1, source_target_pairs={{0,2},{1,3},{2,4},{3,5},{4,6},{5,7},{6,0},{7,1},{8,10},{9,11},{10,... | collective-permute-start | bytes 786440 | tf_op jit(solution)/shard_map/ppermute | solution.py:464
  18.8 7.4 %collective-permute-start.5 = (f32[2,2,128,128]{3,2,1,0:T(8,128)S(1)}, f32[2,2,128,128]{3,2,1,0:T(8,128)S(1)}, u32[]{:S(2)}, u32[]{:S(2)}) collective-permute-start(f32[2,2,128,128]{3,2,1,0:T(8,128)S(1)} %pad_maximum_fusion.1.near1), channel_id=1, source_target_pairs={{0,6},{1,7},{2,0},{3,1},{4,2},{5,3},{6,4},{7,5},{8,14},{9,15},{10,... | collective-permute-start | bytes 786440 | tf_op jit(solution)/shard_map/ppermute | solution.py:464
  20.3 11.1 %collective-permute-start.4 = (f32[2,2,128,128]{3,2,1,0:T(8,128)S(1)}, f32[2,2,128,128]{3,2,1,0:T(8,128)S(1)}, u32[]{:S(2)}, u32[]{:S(2)}) collective-permute-start(f32[2,2,128,128]{3,2,1,0:T(8,128)S(1)} %pad_maximum_fusion.near0), channel_id=1, source_target_pairs={{0,6},{1,7},{2,0},{3,1},{4,2},{5,3},{6,4},{7,5},{8,14},{9,15},{10,... | collective-permute-start | bytes 786440 | tf_op jit(solution)/shard_map/ppermute | solution.py:464
  21.8 10.0 %collective-permute-start.9 = (f32[2,2,128,128]{3,2,1,0:T(8,128)S(1)}, f32[2,2,128,128]{3,2,1,0:T(8,128)S(1)}, u32[]{:S(2)}, u32[]{:S(2)}) collective-permute-start(f32[2,2,128,128]{3,2,1,0:T(8,128)S(1)} %pad_maximum_fusion.1.near1), channel_id=1, source_target_pairs={{0,2},{1,3},{2,4},{3,5},{4,6},{5,7},{6,0},{7,1},{8,10},{9,11},{10,... | collective-permute-start | bytes 786440 | tf_op jit(solution)/shard_map/ppermute | solution.py:464
  26.1 11.2 %collective-permute-start.7 = (f32[2,2,128,128]{3,2,1,0:T(8,128)S(1)}, f32[2,2,128,128]{3,2,1,0:T(8,128)S(1)}, u32[]{:S(2)}, u32[]{:S(2)}) collective-permute-start(f32[2,2,128,128]{3,2,1,0:T(8,128)S(1)} %collective-permute-done.6.down0), channel_id=1, source_target_pairs={{0,2},{1,3},{2,4},{3,5},{4,6},{5,7},{6,0},{7,1},{8,10},{9,11},{10,... | collective-permute-start | bytes 786440 | tf_op jit(solution)/shard_map/ppermute | solution.py:464
  26.1 11.2 %collective-permute-start.8 = (f32[2,2,128,128]{3,2,1,0:T(8,128)S(1)}, f32[2,2,128,128]{3,2,1,0:T(8,128)S(1)}, u32[]{:S(2)}, u32[]{:S(2)}) collective-permute-start(f32[2,2,128,128]{3,2,1,0:T(8,128)S(1)} %collective-permute-done.5.up1), channel_id=1, source_target_pairs={{0,6},{1,7},{2,0},{3,1},{4,2},{5,3},{6,4},{7,5},{8,14},{9,15},{10,... | collective-permute-start | bytes 786440 | tf_op jit(solution)/shard_map/ppermute | solution.py:464
  29.5 19.3 %copy-start.6 = (f32[2,128,128]{2,1,0:T(8,128)S(1)}, f32[2,128,128]{2,1,0:T(8,128)}, u32[]{:S(2)}) copy-start(f32[2,128,128]{2,1,0:T(8,128)} %param.9) | copy-start | bytes 393220
  41.3 5.1 %collective-permute-start.10 = (f32[2,128,128]{2,1,0:T(8,128)S(1)}, f32[2,128,128]{2,1,0:T(8,128)S(1)}, u32[]{:S(2)}, u32[]{:S(2)}) collective-permute-start(f32[2,128,128]{2,1,0:T(8,128)S(1)} %get-tuple-element.41), channel_id=1, source_target_pairs={{0,8},{1,9},{2,10},{3,11},{4,12},{5,13},{6,14},{7,15},{8,16},{9,17... | collective-permute-start | bytes 393224 | tf_op jit(solution)/shard_map/ppermute | solution.py:470
  46.4 5.1 %collective-permute-start.11 = (f32[2,128,128]{2,1,0:T(8,128)S(1)}, f32[2,128,128]{2,1,0:T(8,128)S(1)}, u32[]{:S(2)}, u32[]{:S(2)}) collective-permute-start(f32[2,128,128]{2,1,0:T(8,128)S(1)} %get-tuple-element.43), channel_id=1, source_target_pairs={{0,8},{1,9},{2,10},{3,11},{4,12},{5,13},{6,14},{7,15},{8,16},{9,17... | collective-permute-start | bytes 393224 | tf_op jit(solution)/shard_map/ppermute | solution.py:470
  48.8 5.3 %collective-permute-start.13 = (f32[2,128,128]{2,1,0:T(8,128)S(1)}, f32[2,128,128]{2,1,0:T(8,128)S(1)}, u32[]{:S(2)}, u32[]{:S(2)}) collective-permute-start(f32[2,128,128]{2,1,0:T(8,128)S(1)} %copy-done.6), channel_id=1, source_target_pairs={{0,32},{32,64},{64,96},{96,0},{1,33},{33,65},{65,97},{97,1},{2,34}... | collective-permute-start | bytes 393224 | tf_op jit(solution)/shard_map/ppermute | solution.py:532
  51.5 5.4 %collective-permute-start.12 = (f32[2,128,128]{2,1,0:T(8,128)S(1)}, f32[2,128,128]{2,1,0:T(8,128)S(1)}, u32[]{:S(2)}, u32[]{:S(2)}) collective-permute-start(f32[2,128,128]{2,1,0:T(8,128)S(1)} %get-tuple-element.45), channel_id=1, source_target_pairs={{0,8},{1,9},{2,10},{3,11},{4,12},{5,13},{6,14},{7,15},{8,16},{9,17... | collective-permute-start | bytes 393224 | tf_op jit(solution)/shard_map/ppermute | solution.py:470
  56.9 11.8 %collective-permute-start.14 = (f32[2,128,128]{2,1,0:T(8,128)S(1)}, f32[2,128,128]{2,1,0:T(8,128)S(1)}, u32[]{:S(2)}, u32[]{:S(2)}) collective-permute-start(f32[2,128,128]{2,1,0:T(8,128)S(1)} %get-tuple-element.47), channel_id=1, source_target_pairs={{0,24},{1,25},{2,26},{3,27},{4,28},{5,29},{6,30},{7,31},{8,0},{9,1... | collective-permute-start | bytes 393224 | tf_op jit(solution)/shard_map/ppermute | solution.py:470
  68.8 5.8 %collective-permute-start.15 = (f32[2,128,128]{2,1,0:T(8,128)S(1)}, f32[2,128,128]{2,1,0:T(8,128)S(1)}, u32[]{:S(2)}, u32[]{:S(2)}) collective-permute-start(f32[2,128,128]{2,1,0:T(8,128)S(1)} %get-tuple-element.51), channel_id=1, source_target_pairs={{0,24},{1,25},{2,26},{3,27},{4,28},{5,29},{6,30},{7,31},{8,0},{9,1... | collective-permute-start | bytes 393224 | tf_op jit(solution)/shard_map/ppermute | solution.py:470
  74.7 7.7 %collective-permute-start.16 = (f32[2,128,128]{2,1,0:T(8,128)S(1)}, f32[2,128,128]{2,1,0:T(8,128)S(1)}, u32[]{:S(2)}, u32[]{:S(2)}) collective-permute-start(f32[2,128,128]{2,1,0:T(8,128)S(1)} %get-tuple-element.54), channel_id=1, source_target_pairs={{0,24},{1,25},{2,26},{3,27},{4,28},{5,29},{6,30},{7,31},{8,0},{9,1... | collective-permute-start | bytes 393224 | tf_op jit(solution)/shard_map/ppermute | solution.py:470
  85.9 9.6 %collective-permute-start.18 = (f32[2,2,128,128]{3,2,1,0:T(8,128)S(1)}, f32[2,2,128,128]{3,2,1,0:T(8,128)S(1)}, u32[]{:S(2)}, u32[]{:S(2)}) collective-permute-start(f32[2,2,128,128]{3,2,1,0:T(8,128)S(1)} %get-tuple-element.57.same), channel_id=1, source_target_pairs={{0,32},{1,97},{2,34},{3,99},{4,36},{5,101},{6,38},{7,103},{8,40},{... | collective-permute-start | bytes 786440 | tf_op jit(solution)/shard_map/ppermute | solution.py:490
  86.0 16.3 %collective-permute-start.19 = (f32[2,2,128,128]{3,2,1,0:T(8,128)S(1)}, f32[2,2,128,128]{3,2,1,0:T(8,128)S(1)}, u32[]{:S(2)}, u32[]{:S(2)}) collective-permute-start(f32[2,2,128,128]{3,2,1,0:T(8,128)S(1)} %get-tuple-element.58), channel_id=1, source_target_pairs={{0,33},{1,96},{2,35},{3,98},{4,37},{5,100},{6,39},{7,102},{8,41},{... | collective-permute-start | bytes 786440 | tf_op jit(solution)/shard_map/ppermute | solution.py:490
  95.5 6.9 %collective-permute-start.17 = (f32[2,2,128,128]{3,2,1,0:T(8,128)S(1)}, f32[2,2,128,128]{3,2,1,0:T(8,128)S(1)}, u32[]{:S(2)}, u32[]{:S(2)}) collective-permute-start(f32[2,2,128,128]{3,2,1,0:T(8,128)S(1)} %get-tuple-element.58), channel_id=1, source_target_pairs={{0,1},{1,0},{2,3},{3,2},{4,5},{5,4},{6,7},{7,6},{8,9},{9,8},{10,11... | collective-permute-start | bytes 786440 | tf_op jit(solution)/shard_map/ppermute | solution.py:475

commit v7 on v6

--- a/solution.py
+++ b/solution.py
@@ -170,9 +170,13 @@
     wave[1] = real
 
 
-def cut_kernel(corners, field, chirp, same, other, moved_same, moved_other):
+def cut_other_kernel(corners, field, chirp, other):
+    cut(corner(corners, here()[2], 1), field, chirp, other)
+
+
+def cut_kernel(corners, field, chirp, same, moved_same, moved_other):
     core = here()[2]
-    for kind, target in ((2, moved_same), (3, moved_other), (0, same), (1, other)):
+    for kind, target in ((2, moved_same), (3, moved_other), (0, same)):
         cut(corner(corners, core, kind), field, chirp, target)
 
 
@@ -186,10 +190,20 @@
     )(field, chirp, offsets)
 
 
+def cut_other(corners, field, chirp):
+    return pl.pallas_call(
+        cut_other_kernel,
+        out_shape=PIECE,
+        in_specs=[SMEM_SPEC] + [VMEM_SPEC] * 2,
+        name="cut_other",
+        compiler_params=PARAMS,
+    )(corners, field, chirp)
+
+
 def cut_windows(corners, field, chirp):
     return pl.pallas_call(
         cut_kernel,
-        out_shape=(PIECE,) * 4,
+        out_shape=(PIECE,) * 3,
         in_specs=[SMEM_SPEC] + [VMEM_SPEC] * 2,
         name="cut_windows",
         compiler_params=PARAMS,
@@ -219,10 +233,10 @@
     core = here()[2]
     places = [corner(corners, core, kind) for kind in range(4)]
     copies = []
-    total[...] = jnp.zeros(total.shape, F32)
     for layer in range(PER_DEVICE):
         for part in range(2):
             target = total.at[layer, part]
+            target[...] = jnp.zeros(target.shape, F32)
             for place, source in zip(places, (same, other, moved_same, moved_other)):
                 paste(place, source[layer, part], target)
             copy = pltpu.make_async_copy(target, out.at[layer, part], sems.at[layer, part])
@@ -500,7 +514,8 @@
     field, chirp_here, offsets = load(object_field, chirp, offsets)
     corners = jnp.concatenate([offsets, before])
 
-    same, other, moved_same, moved_other = cut_windows(corners, field, chirp_here)
+    other = cut_other(corners, field, chirp_here)
+    same, moved_same, moved_other = cut_windows(corners, field, chirp_here)
     moved_same = across(moved_same, 0, False)
     moved_other = across(moved_other, 1, False)
     other = swap_cores(other)

time: 104 us -> 104 us (level)
  waiting for transfers between devices: 44.2 us -> 42.9 us
    ppermute x4, starting transfers between devices: 11.3 us -> 14 us  [across(): return lax.ppermute(value, ('pos', 'depth'), pairs)]
    ppermute x2, starting transfers between devices: 2.34 us -> 0.01 us  [swap_cores(): lax.ppermute(value, 'depth', [(device, device ^ 1) for device in range(de...]
  transfers between devices with their start and end apart: 20 -> 20, of which waited for: 13 -> 14; matrix products, arithmetic and copies ran while one was open for 1% -> 1% of each run, Pallas kernels for 1% -> 1%
where the time goes in v7:
time: 104 us
  starting transfers between devices  43.3 us (42%)
  waiting for transfers between devices  42.9 us (41%)
  Pallas kernels  11.8 us (11%)
  local copies, waits for them, and re-layouts  4.6 us (4%)
  between operations  1.48 us (1%)
    ppermute x6, starting transfers between devices, along_stages(): return lax.ppermute(value, 'depth', pairs)  20 us
    ppermute x6, waiting for transfers between devices, along_stages(): return lax.ppermute(value, 'depth', pairs)  19.4 us
    ppermute x4, starting transfers between devices, across(): return lax.ppermute(value, ('pos', 'depth'), pairs)  14 us
    ppermute x6, waiting for transfers between devices, along_ring(): return lax.ppermute(value, 'depth', pairs)  11.8 us
    ppermute x4, waiting for transfers between devices, across(): return lax.ppermute(value, ('pos', 'depth'), pairs)  10.3 us
    ppermute x6, starting transfers between devices, along_ring(): return lax.ppermute(value, 'depth', pairs)  7.03 us
    pallas_call x1, Pallas kernels, first_stage(): pl.pallas_call(first_kernel, out_shape=(WAVE, SAVED, STACK), in_specs=[VM...  3.87 us
    pallas_call x3, Pallas kernels, backward_stage(): pl.pallas_call(last_backward_kernel if last else functools.partial(backwa...  3.58 us
  transfers between devices with their start and end apart: 20, of which 14 were waited for; matrix products, arithmetic and copies ran while one was open for 1% of the time, Pallas kernels for 1%

profile of v7, /device:TPU:1, one launch (start us, length us, event | category | flops | bytes accessed | tf_op | source)
XLA Modules:
  0.0 104.2 jit_solution(9976356726508767092)
XLA Ops:
  0.7 2.0 %collective-permute-start = (s32[128,128]{1,0:T(8,128)S(1)}, s32[128,128]{1,0:T(8,128)S(1)}, u32[]{:S(2)}, u32[]{:S(2)}) collective-permute-start(s32[128,128]{1,0:T(8,128)S(1)} %pad.4), channel_id=1, source_target_pairs={{0,32},{32,64},{64,96},{96,0},{1,33},{33,65},{65,97},{97,1},{2,34}... | collective-permute-start | bytes 196616 | tf_op jit(solution)/shard_map/ppermute | solution.py:513
  2.7 0.9 copy-done.1
  3.6 1.2 %copy-done.3 = f32[2,2,128,512]{3,2,1,0:T(8,128)S(1)} copy-done((f32[2,2,128,512]{3,2,1,0:T(8,128)S(1)}, f32[2,2,128,512]{3,2,1,0:T(8,128)}, u32[]{:S(2)}) %copy-start.3) | copy-done | bytes 1048600
  6.4 0.9 cut_windows.1
  7.3 1.3 %collective-permute-start.1 = (f32[2,2,128,128]{3,2,1,0:T(8,128)S(1)}, f32[2,2,128,128]{3,2,1,0:T(8,128)S(1)}, u32[]{:S(2)}, u32[]{:S(2)}) collective-permute-start(f32[2,2,128,128]{3,2,1,0:T(8,128)S(1)} %get-tuple-element.35), channel_id=1, source_target_pairs={{0,96},{1,33},{2,98},{3,35},{4,100},{5,37},{6,102},{7,39},{8,104},... | collective-permute-start | bytes 786440 | tf_op jit(solution)/shard_map/ppermute | solution.py:504
  8.6 2.8 %collective-permute-start.3 = (f32[2,2,128,128]{3,2,1,0:T(8,128)S(1)}, f32[2,2,128,128]{3,2,1,0:T(8,128)S(1)}, u32[]{:S(2)}, u32[]{:S(2)}) collective-permute-start(f32[2,2,128,128]{3,2,1,0:T(8,128)S(1)} %get-tuple-element.36), channel_id=1, source_target_pairs={{0,33},{1,96},{2,35},{3,98},{4,37},{5,100},{6,39},{7,102},{8,41},{... | collective-permute-start | bytes 786440 | tf_op jit(solution)/shard_map/ppermute | solution.py:504
  13.8 0.9 collective-permute-done.1
  14.8 2.5 %collective-permute-done.3 = f32[2,2,128,128]{3,2,1,0:T(8,128)S(1)} collective-permute-done((f32[2,2,128,128]{3,2,1,0:T(8,128)S(1)}, f32[2,2,128,128]{3,2,1,0:T(8,128)S(1)}, u32[]{:S(2)}, u32[]{:S(2)}) %collective-permute-start.3) | collective-permute-done | bytes 262176 | tf_op jit(solution)/shard_map/ppermute | solution.py:504
  17.4 1.4 %collective-permute-start.6 = (f32[2,2,128,128]{3,2,1,0:T(8,128)S(1)}, f32[2,2,128,128]{3,2,1,0:T(8,128)S(1)}, u32[]{:S(2)}, u32[]{:S(2)}) collective-permute-start(f32[2,2,128,128]{3,2,1,0:T(8,128)S(1)} %pad_maximum_fusion.near0), channel_id=1, source_target_pairs={{0,2},{1,3},{2,4},{3,5},{4,6},{5,7},{6,0},{7,1},{8,10},{9,11},{10,... | collective-permute-start | bytes 786440 | tf_op jit(solution)/shard_map/ppermute | solution.py:478
  18.8 1.5 %collective-permute-start.5 = (f32[2,2,128,128]{3,2,1,0:T(8,128)S(1)}, f32[2,2,128,128]{3,2,1,0:T(8,128)S(1)}, u32[]{:S(2)}, u32[]{:S(2)}) collective-permute-start(f32[2,2,128,128]{3,2,1,0:T(8,128)S(1)} %pad_maximum_fusion.1.near1), channel_id=1, source_target_pairs={{0,6},{1,7},{2,0},{3,1},{4,2},{5,3},{6,4},{7,5},{8,14},{9,15},{10,... | collective-permute-start | bytes 786440 | tf_op jit(solution)/shard_map/ppermute | solution.py:478
  20.3 1.4 %collective-permute-start.4 = (f32[2,2,128,128]{3,2,1,0:T(8,128)S(1)}, f32[2,2,128,128]{3,2,1,0:T(8,128)S(1)}, u32[]{:S(2)}, u32[]{:S(2)}) collective-permute-start(f32[2,2,128,128]{3,2,1,0:T(8,128)S(1)} %pad_maximum_fusion.near0), channel_id=1, source_target_pairs={{0,6},{1,7},{2,0},{3,1},{4,2},{5,3},{6,4},{7,5},{8,14},{9,15},{10,... | collective-permute-start | bytes 786440 | tf_op jit(solution)/shard_map/ppermute | solution.py:478
  21.8 3.6 %collective-permute-done.6.down0 = f32[2,2,128,128]{3,2,1,0:T(8,128)S(1)} collective-permute-done((f32[2,2,128,128]{3,2,1,0:T(8,128)S(1)}, f32[2,2,128,128]{3,2,1,0:T(8,128)S(1)}, u32[]{:S(2)}, u32[]{:S(2)}) %collective-permute-start.6) | collective-permute-done | bytes 262176 | tf_op jit(solution)/shard_map/ppermute | solution.py:478
  25.3 2.7 %collective-permute-start.8 = (f32[2,2,128,128]{3,2,1,0:T(8,128)S(1)}, f32[2,2,128,128]{3,2,1,0:T(8,128)S(1)}, u32[]{:S(2)}, u32[]{:S(2)}) collective-permute-start(f32[2,2,128,128]{3,2,1,0:T(8,128)S(1)} %collective-permute-done.5.up1), channel_id=1, source_target_pairs={{0,6},{1,7},{2,0},{3,1},{4,2},{5,3},{6,4},{7,5},{8,14},{9,15},{10,... | collective-permute-start | bytes 786440 | tf_op jit(solution)/shard_map/ppermute | solution.py:478
  28.7 1.9 %collective-permute-done.4.up0 = f32[2,2,128,128]{3,2,1,0:T(8,128)S(1)} collective-permute-done((f32[2,2,128,128]{3,2,1,0:T(8,128)S(1)}, f32[2,2,128,128]{3,2,1,0:T(8,128)S(1)}, u32[]{:S(2)}, u32[]{:S(2)}) %collective-permute-start.4) | collective-permute-done | bytes 262176 | tf_op jit(solution)/shard_map/ppermute | solution.py:478
  31.3 5.6 %collective-permute-done.7.far0 = f32[2,2,128,128]{3,2,1,0:T(8,128)S(1)} collective-permute-done((f32[2,2,128,128]{3,2,1,0:T(8,128)S(1)}, f32[2,2,128,128]{3,2,1,0:T(8,128)S(1)}, u32[]{:S(2)}, u32[]{:S(2)}) %collective-permute-start.7) | collective-permute-done | bytes 262176 | tf_op jit(solution)/shard_map/ppermute | solution.py:478
  37.0 3.9 %first_stage.1 = (f32[2,128,128]{2,1,0:T(8,128)S(1)}, f32[4,2,128,128]{3,2,1,0:T(8,128)S(1)}, f32[16,2,128,128]{3,2,1,0:T(8,128)S(1)}) custom-call(f32[2,2,128,128]{3,2,1,0:T(8,128)S(1)} %pad_maximum_fusion.near0, f32[2,2,128,128]{3,2,1,0:T(8,128)S(1)} %pad_maximum_fusion.1.near1, f32[2,2,128,128]{3,2,1,0:T(8,128)S(1)} %collective-permute-done.4.up0, ...), custom_call_target="tpu_custom_call" | custom-call | tf_op jit(solution)/shard_map/first_stage/pallas_call | solution.py:430
  40.9 5.0 %collective-permute-done.10.wave = f32[2,128,128]{2,1,0:T(8,128)S(1)} collective-permute-done((f32[2,128,128]{2,1,0:T(8,128)S(1)}, f32[2,128,128]{2,1,0:T(8,128)S(1)}, u32[]{:S(2)}, u32[]{:S(2)}) %collective-permute-start.10) | collective-permute-done | bytes 131104 | tf_op jit(solution)/shard_map/ppermute | solution.py:484
  46.0 2.4 %collective-permute-start.11 = (f32[2,128,128]{2,1,0:T(8,128)S(1)}, f32[2,128,128]{2,1,0:T(8,128)S(1)}, u32[]{:S(2)}, u32[]{:S(2)}) collective-permute-start(f32[2,128,128]{2,1,0:T(8,128)S(1)} %get-tuple-element.41), channel_id=1, source_target_pairs={{0,8},{1,9},{2,10},{3,11},{4,12},{5,13},{6,14},{7,15},{8,16},{9,17... | collective-permute-start | bytes 393224 | tf_op jit(solution)/shard_map/ppermute | solution.py:484
  48.6 2.5 %collective-permute-done.11.wave = f32[2,128,128]{2,1,0:T(8,128)S(1)} collective-permute-done((f32[2,128,128]{2,1,0:T(8,128)S(1)}, f32[2,128,128]{2,1,0:T(8,128)S(1)}, u32[]{:S(2)}, u32[]{:S(2)}) %collective-permute-start.11) | collective-permute-done | bytes 131104 | tf_op jit(solution)/shard_map/ppermute | solution.py:484
  51.1 1.2 %collective-permute-start.12 = (f32[2,128,128]{2,1,0:T(8,128)S(1)}, f32[2,128,128]{2,1,0:T(8,128)S(1)}, u32[]{:S(2)}, u32[]{:S(2)}) collective-permute-start(f32[2,128,128]{2,1,0:T(8,128)S(1)} %get-tuple-element.43), channel_id=1, source_target_pairs={{0,8},{1,9},{2,10},{3,11},{4,12},{5,13},{6,14},{7,15},{8,16},{9,17... | collective-permute-start | bytes 393224 | tf_op jit(solution)/shard_map/ppermute | solution.py:484
  52.3 1.4 %collective-permute-done.13 = f32[2,128,128]{2,1,0:T(8,128)S(1)} collective-permute-done((f32[2,128,128]{2,1,0:T(8,128)S(1)}, f32[2,128,128]{2,1,0:T(8,128)S(1)}, u32[]{:S(2)}, u32[]{:S(2)}) %collective-permute-start.13) | collective-permute-done | bytes 131104 | tf_op jit(solution)/shard_map/ppermute | solution.py:547
  53.7 2.8 %collective-permute-done.12.wave = f32[2,128,128]{2,1,0:T(8,128)S(1)} collective-permute-done((f32[2,128,128]{2,1,0:T(8,128)S(1)}, f32[2,128,128]{2,1,0:T(8,128)S(1)}, u32[]{:S(2)}, u32[]{:S(2)}) %collective-permute-start.12) | collective-permute-done | bytes 131104 | tf_op jit(solution)/shard_map/ppermute | solution.py:484
  56.5 9.9 %collective-permute-start.14 = (f32[2,128,128]{2,1,0:T(8,128)S(1)}, f32[2,128,128]{2,1,0:T(8,128)S(1)}, u32[]{:S(2)}, u32[]{:S(2)}) collective-permute-start(f32[2,128,128]{2,1,0:T(8,128)S(1)} %get-tuple-element.45), channel_id=1, source_target_pairs={{0,24},{1,25},{2,26},{3,27},{4,28},{5,29},{6,30},{7,31},{8,0},{9,1... | collective-permute-start | bytes 393224 | tf_op jit(solution)/shard_map/ppermute | solution.py:484
  66.4 1.9 %collective-permute-done.14.wave = f32[2,128,128]{2,1,0:T(8,128)S(1)} collective-permute-done((f32[2,128,128]{2,1,0:T(8,128)S(1)}, f32[2,128,128]{2,1,0:T(8,128)S(1)}, u32[]{:S(2)}, u32[]{:S(2)}) %collective-permute-start.14) | collective-permute-done | bytes 131104 | tf_op jit(solution)/shard_map/ppermute | solution.py:484
  68.4 3.1 %collective-permute-start.15 = (f32[2,128,128]{2,1,0:T(8,128)S(1)}, f32[2,128,128]{2,1,0:T(8,128)S(1)}, u32[]{:S(2)}, u32[]{:S(2)}) collective-permute-start(f32[2,128,128]{2,1,0:T(8,128)S(1)} %get-tuple-element.49), channel_id=1, source_target_pairs={{0,24},{1,25},{2,26},{3,27},{4,28},{5,29},{6,30},{7,31},{8,0},{9,1... | collective-permute-start | bytes 393224 | tf_op jit(solution)/shard_map/ppermute | solution.py:484
  71.5 3.1 %collective-permute-done.15.wave = f32[2,128,128]{2,1,0:T(8,128)S(1)} collective-permute-done((f32[2,128,128]{2,1,0:T(8,128)S(1)}, f32[2,128,128]{2,1,0:T(8,128)S(1)}, u32[]{:S(2)}, u32[]{:S(2)}) %collective-permute-start.15) | collective-permute-done | bytes 131104 | tf_op jit(solution)/shard_map/ppermute | solution.py:484
  74.7 3.2 %collective-permute-start.16 = (f32[2,128,128]{2,1,0:T(8,128)S(1)}, f32[2,128,128]{2,1,0:T(8,128)S(1)}, u32[]{:S(2)}, u32[]{:S(2)}) collective-permute-start(f32[2,128,128]{2,1,0:T(8,128)S(1)} %get-tuple-element.52), channel_id=1, source_target_pairs={{0,24},{1,25},{2,26},{3,27},{4,28},{5,29},{6,30},{7,31},{8,0},{9,1... | collective-permute-start | bytes 393224 | tf_op jit(solution)/shard_map/ppermute | solution.py:484
  77.9 4.1 %collective-permute-done.16.wave = f32[2,128,128]{2,1,0:T(8,128)S(1)} collective-permute-done((f32[2,128,128]{2,1,0:T(8,128)S(1)}, f32[2,128,128]{2,1,0:T(8,128)S(1)}, u32[]{:S(2)}, u32[]{:S(2)}) %collective-permute-start.16) | collective-permute-done | bytes 131104 | tf_op jit(solution)/shard_map/ppermute | solution.py:484
  82.0 3.5 %backward_stage.5 = (f32[2,2,128,128]{3,2,1,0:T(8,128)S(1)}, f32[2,2,128,128]{3,2,1,0:T(8,128)S(1)}) custom-call(f32[16,2,128,128]{3,2,1,0:T(8,128)S(1)} %get-tuple-element.37.windows, f32[2,128,128]{2,1,0:T(8,128)S(1)} %collective-permute-done.16.wave, f32[4,2,128,128]{3,2,1,0:T(8,128)S(1)} %get-tuple-element.46.saved, f32[2,128,128]{2,1,0:T(8,128)S(1)} %copy-done, ...), custom_call_target="tpu_custom_call" | custom-call | tf_op jit(solution)/shard_map/backward_stage/pallas_call | solution.py:452
  85.9 9.6 %collective-permute-start.19 = (f32[2,2,128,128]{3,2,1,0:T(8,128)S(1)}, f32[2,2,128,128]{3,2,1,0:T(8,128)S(1)}, u32[]{:S(2)}, u32[]{:S(2)}) collective-permute-start(f32[2,2,128,128]{3,2,1,0:T(8,128)S(1)} %get-tuple-element.56), channel_id=1, source_target_pairs={{0,33},{1,96},{2,35},{3,98},{4,37},{5,100},{6,39},{7,102},{8,41},{... | collective-permute-start | bytes 786440 | tf_op jit(solution)/shard_map/ppermute | solution.py:504
  95.4 6.9 %collective-permute-done.19.moved_other = f32[2,2,128,128]{3,2,1,0:T(8,128)S(1)} collective-permute-done((f32[2,2,128,128]{3,2,1,0:T(8,128)S(1)}, f32[2,2,128,128]{3,2,1,0:T(8,128)S(1)}, u32[]{:S(2)}, u32[]{:S(2)}) %collective-permute-start.19) | collective-permute-done | bytes 262176 | tf_op jit(solution)/shard_map/ppermute | solution.py:504
  102.3 1.9 %paste_windows.1 = f32[2,2,128,512]{3,2,1,0:T(8,128)} custom-call(s32[4,2]{1,0:T(4,128)S(1)} %pad_add_fusion.corners, f32[2,2,128,128]{3,2,1,0:T(8,128)S(1)} %get-tuple-element.55.same, f32[2,2,128,128]{3,2,1,0:T(8,128)S(1)} %collective-permute-done.17.other, f32[2,2,128,128]{3,2,1,0:T(8,128)S(1)} %collective-permute-done.18.moved_same, ...), custom_call_target="tpu_custom_call" | custom-call | tf_op jit(solution)/shard_map/paste_windows/pallas_call | solution.py:250
  (44 shorter events, 5.7 us)
Async XLA Ops:
  0.7 5.0 %collective-permute-start = (s32[128,128]{1,0:T(8,128)S(1)}, s32[128,128]{1,0:T(8,128)S(1)}, u32[]{:S(2)}, u32[]{:S(2)}) collective-permute-start(s32[128,128]{1,0:T(8,128)S(1)} %pad.4), channel_id=1, source_target_pairs={{0,32},{32,64},{64,96},{96,0},{1,33},{33,65},{65,97},{97,1},{2,34}... | collective-permute-start | bytes 196616 | tf_op jit(solution)/shard_map/ppermute | solution.py:513
  2.7 0.9 copy-start.1
  3.6 1.2 %copy-start.3 = (f32[2,2,128,512]{3,2,1,0:T(8,128)S(1)}, f32[2,2,128,512]{3,2,1,0:T(8,128)}, u32[]{:S(2)}) copy-start(f32[2,2,128,512]{3,2,1,0:T(8,128)} %field.1) | copy-start | bytes 3145732
  4.9 0.7 copy-start.5
  6.4 21.6 %copy-start.2 = (f32[2,128,128]{2,1,0:T(8,128)S(1)}, f32[2,128,128]{2,1,0:T(8,128)}, u32[]{:S(2)}) copy-start(f32[2,128,128]{2,1,0:T(8,128)} %constant.33.clone.chirp) | copy-start | bytes 393220
  6.4 21.6 %copy-start.4 = (f32[2,128,128]{2,1,0:T(8,128)S(1)}, f32[2,128,128]{2,1,0:T(8,128)}, u32[]{:S(2)}) copy-start(f32[2,128,128]{2,1,0:T(8,128)} %probe.1) | copy-start | bytes 393220
  6.4 30.5 %copy-start = (f32[2,128,128]{2,1,0:T(8,128)S(1)}, f32[2,128,128]{2,1,0:T(8,128)}, u32[]{:S(2)}) copy-start(f32[2,128,128]{2,1,0:T(8,128)} %constant.32.clone.twiddle) | copy-start | bytes 393220
  7.3 7.5 %collective-permute-start.1 = (f32[2,2,128,128]{3,2,1,0:T(8,128)S(1)}, f32[2,2,128,128]{3,2,1,0:T(8,128)S(1)}, u32[]{:S(2)}, u32[]{:S(2)}) collective-permute-start(f32[2,2,128,128]{3,2,1,0:T(8,128)S(1)} %get-tuple-element.35), channel_id=1, source_target_pairs={{0,96},{1,33},{2,98},{3,35},{4,100},{5,37},{6,102},{7,39},{8,104},... | collective-permute-start | bytes 786440 | tf_op jit(solution)/shard_map/ppermute | solution.py:504
  8.6 8.7 %collective-permute-start.3 = (f32[2,2,128,128]{3,2,1,0:T(8,128)S(1)}, f32[2,2,128,128]{3,2,1,0:T(8,128)S(1)}, u32[]{:S(2)}, u32[]{:S(2)}) collective-permute-start(f32[2,2,128,128]{3,2,1,0:T(8,128)S(1)} %get-tuple-element.36), channel_id=1, source_target_pairs={{0,33},{1,96},{2,35},{3,98},{4,37},{5,100},{6,39},{7,102},{8,41},{... | collective-permute-start | bytes 786440 | tf_op jit(solution)/shard_map/ppermute | solution.py:504
  11.4 5.9 %collective-permute-start.2 = (f32[2,2,128,128]{3,2,1,0:T(8,128)S(1)}, f32[2,2,128,128]{3,2,1,0:T(8,128)S(1)}, u32[]{:S(2)}, u32[]{:S(2)}) collective-permute-start(f32[2,2,128,128]{3,2,1,0:T(8,128)S(1)} %cut_other.1), channel_id=1, source_target_pairs={{0,1},{1,0},{2,3},{3,2},{4,5},{5,4},{6,7},{7,6},{8,9},{9,8},{10,11... | collective-permute-start | bytes 786440 | tf_op jit(solution)/shard_map/ppermute | solution.py:489
  17.4 8.0 %collective-permute-start.6 = (f32[2,2,128,128]{3,2,1,0:T(8,128)S(1)}, f32[2,2,128,128]{3,2,1,0:T(8,128)S(1)}, u32[]{:S(2)}, u32[]{:S(2)}) collective-permute-start(f32[2,2,128,128]{3,2,1,0:T(8,128)S(1)} %pad_maximum_fusion.near0), channel_id=1, source_target_pairs={{0,2},{1,3},{2,4},{3,5},{4,6},{5,7},{6,0},{7,1},{8,10},{9,11},{10,... | collective-permute-start | bytes 786440 | tf_op jit(solution)/shard_map/ppermute | solution.py:478
  18.8 6.6 %collective-permute-start.5 = (f32[2,2,128,128]{3,2,1,0:T(8,128)S(1)}, f32[2,2,128,128]{3,2,1,0:T(8,128)S(1)}, u32[]{:S(2)}, u32[]{:S(2)}) collective-permute-start(f32[2,2,128,128]{3,2,1,0:T(8,128)S(1)} %pad_maximum_fusion.1.near1), channel_id=1, source_target_pairs={{0,6},{1,7},{2,0},{3,1},{4,2},{5,3},{6,4},{7,5},{8,14},{9,15},{10,... | collective-permute-start | bytes 786440 | tf_op jit(solution)/shard_map/ppermute | solution.py:478
  20.3 10.3 %collective-permute-start.4 = (f32[2,2,128,128]{3,2,1,0:T(8,128)S(1)}, f32[2,2,128,128]{3,2,1,0:T(8,128)S(1)}, u32[]{:S(2)}, u32[]{:S(2)}) collective-permute-start(f32[2,2,128,128]{3,2,1,0:T(8,128)S(1)} %pad_maximum_fusion.near0), channel_id=1, source_target_pairs={{0,6},{1,7},{2,0},{3,1},{4,2},{5,3},{6,4},{7,5},{8,14},{9,15},{10,... | collective-permute-start | bytes 786440 | tf_op jit(solution)/shard_map/ppermute | solution.py:478
  21.7 9.6 %collective-permute-start.9 = (f32[2,2,128,128]{3,2,1,0:T(8,128)S(1)}, f32[2,2,128,128]{3,2,1,0:T(8,128)S(1)}, u32[]{:S(2)}, u32[]{:S(2)}) collective-permute-start(f32[2,2,128,128]{3,2,1,0:T(8,128)S(1)} %pad_maximum_fusion.1.near1), channel_id=1, source_target_pairs={{0,2},{1,3},{2,4},{3,5},{4,6},{5,7},{6,0},{7,1},{8,10},{9,11},{10,... | collective-permute-start | bytes 786440 | tf_op jit(solution)/shard_map/ppermute | solution.py:478
  25.3 11.6 %collective-permute-start.7 = (f32[2,2,128,128]{3,2,1,0:T(8,128)S(1)}, f32[2,2,128,128]{3,2,1,0:T(8,128)S(1)}, u32[]{:S(2)}, u32[]{:S(2)}) collective-permute-start(f32[2,2,128,128]{3,2,1,0:T(8,128)S(1)} %collective-permute-done.6.down0), channel_id=1, source_target_pairs={{0,2},{1,3},{2,4},{3,5},{4,6},{5,7},{6,0},{7,1},{8,10},{9,11},{10,... | collective-permute-start | bytes 786440 | tf_op jit(solution)/shard_map/ppermute | solution.py:478
  25.3 11.6 %collective-permute-start.8 = (f32[2,2,128,128]{3,2,1,0:T(8,128)S(1)}, f32[2,2,128,128]{3,2,1,0:T(8,128)S(1)}, u32[]{:S(2)}, u32[]{:S(2)}) collective-permute-start(f32[2,2,128,128]{3,2,1,0:T(8,128)S(1)} %collective-permute-done.5.up1), channel_id=1, source_target_pairs={{0,6},{1,7},{2,0},{3,1},{4,2},{5,3},{6,4},{7,5},{8,14},{9,15},{10,... | collective-permute-start | bytes 786440 | tf_op jit(solution)/shard_map/ppermute | solution.py:478
  28.7 19.7 %copy-start.6 = (f32[2,128,128]{2,1,0:T(8,128)S(1)}, f32[2,128,128]{2,1,0:T(8,128)}, u32[]{:S(2)}) copy-start(f32[2,128,128]{2,1,0:T(8,128)} %param.9) | copy-start | bytes 393220
  40.8 5.1 %collective-permute-start.10 = (f32[2,128,128]{2,1,0:T(8,128)S(1)}, f32[2,128,128]{2,1,0:T(8,128)S(1)}, u32[]{:S(2)}, u32[]{:S(2)}) collective-permute-start(f32[2,128,128]{2,1,0:T(8,128)S(1)} %get-tuple-element.39), channel_id=1, source_target_pairs={{0,8},{1,9},{2,10},{3,11},{4,12},{5,13},{6,14},{7,15},{8,16},{9,17... | collective-permute-start | bytes 393224 | tf_op jit(solution)/shard_map/ppermute | solution.py:484
  46.0 5.1 %collective-permute-start.11 = (f32[2,128,128]{2,1,0:T(8,128)S(1)}, f32[2,128,128]{2,1,0:T(8,128)S(1)}, u32[]{:S(2)}, u32[]{:S(2)}) collective-permute-start(f32[2,128,128]{2,1,0:T(8,128)S(1)} %get-tuple-element.41), channel_id=1, source_target_pairs={{0,8},{1,9},{2,10},{3,11},{4,12},{5,13},{6,14},{7,15},{8,16},{9,17... | collective-permute-start | bytes 393224 | tf_op jit(solution)/shard_map/ppermute | solution.py:484
  48.4 5.3 %collective-permute-start.13 = (f32[2,128,128]{2,1,0:T(8,128)S(1)}, f32[2,128,128]{2,1,0:T(8,128)S(1)}, u32[]{:S(2)}, u32[]{:S(2)}) collective-permute-start(f32[2,128,128]{2,1,0:T(8,128)S(1)} %copy-done.6), channel_id=1, source_target_pairs={{0,32},{32,64},{64,96},{96,0},{1,33},{33,65},{65,97},{97,1},{2,34}... | collective-permute-start | bytes 393224 | tf_op jit(solution)/shard_map/ppermute | solution.py:547
  51.1 5.4 %collective-permute-start.12 = (f32[2,128,128]{2,1,0:T(8,128)S(1)}, f32[2,128,128]{2,1,0:T(8,128)S(1)}, u32[]{:S(2)}, u32[]{:S(2)}) collective-permute-start(f32[2,128,128]{2,1,0:T(8,128)S(1)} %get-tuple-element.43), channel_id=1, source_target_pairs={{0,8},{1,9},{2,10},{3,11},{4,12},{5,13},{6,14},{7,15},{8,16},{9,17... | collective-permute-start | bytes 393224 | tf_op jit(solution)/shard_map/ppermute | solution.py:484
  56.5 11.8 %collective-permute-start.14 = (f32[2,128,128]{2,1,0:T(8,128)S(1)}, f32[2,128,128]{2,1,0:T(8,128)S(1)}, u32[]{:S(2)}, u32[]{:S(2)}) collective-permute-start(f32[2,128,128]{2,1,0:T(8,128)S(1)} %get-tuple-element.45), channel_id=1, source_target_pairs={{0,24},{1,25},{2,26},{3,27},{4,28},{5,29},{6,30},{7,31},{8,0},{9,1... | collective-permute-start | bytes 393224 | tf_op jit(solution)/shard_map/ppermute | solution.py:484
  68.4 6.2 %collective-permute-start.15 = (f32[2,128,128]{2,1,0:T(8,128)S(1)}, f32[2,128,128]{2,1,0:T(8,128)S(1)}, u32[]{:S(2)}, u32[]{:S(2)}) collective-permute-start(f32[2,128,128]{2,1,0:T(8,128)S(1)} %get-tuple-element.49), channel_id=1, source_target_pairs={{0,24},{1,25},{2,26},{3,27},{4,28},{5,29},{6,30},{7,31},{8,0},{9,1... | collective-permute-start | bytes 393224 | tf_op jit(solution)/shard_map/ppermute | solution.py:484
  74.7 7.3 %collective-permute-start.16 = (f32[2,128,128]{2,1,0:T(8,128)S(1)}, f32[2,128,128]{2,1,0:T(8,128)S(1)}, u32[]{:S(2)}, u32[]{:S(2)}) collective-permute-start(f32[2,128,128]{2,1,0:T(8,128)S(1)} %get-tuple-element.52), channel_id=1, source_target_pairs={{0,24},{1,25},{2,26},{3,27},{4,28},{5,29},{6,30},{7,31},{8,0},{9,1... | collective-permute-start | bytes 393224 | tf_op jit(solution)/shard_map/ppermute | solution.py:484
  85.5 10.0 %collective-permute-start.18 = (f32[2,2,128,128]{3,2,1,0:T(8,128)S(1)}, f32[2,2,128,128]{3,2,1,0:T(8,128)S(1)}, u32[]{:S(2)}, u32[]{:S(2)}) collective-permute-start(f32[2,2,128,128]{3,2,1,0:T(8,128)S(1)} %get-tuple-element.55.same), channel_id=1, source_target_pairs={{0,32},{1,97},{2,34},{3,99},{4,36},{5,101},{6,38},{7,103},{8,40},{... | collective-permute-start | bytes 786440 | tf_op jit(solution)/shard_map/ppermute | solution.py:504
  85.9 16.4 %collective-permute-start.19 = (f32[2,2,128,128]{3,2,1,0:T(8,128)S(1)}, f32[2,2,128,128]{3,2,1,0:T(8,128)S(1)}, u32[]{:S(2)}, u32[]{:S(2)}) collective-permute-start(f32[2,2,128,128]{3,2,1,0:T(8,128)S(1)} %get-tuple-element.56), channel_id=1, source_target_pairs={{0,33},{1,96},{2,35},{3,98},{4,37},{5,100},{6,39},{7,102},{8,41},{... | collective-permute-start | bytes 786440 | tf_op jit(solution)/shard_map/ppermute | solution.py:504
  95.4 6.9 %collective-permute-start.17 = (f32[2,2,128,128]{3,2,1,0:T(8,128)S(1)}, f32[2,2,128,128]{3,2,1,0:T(8,128)S(1)}, u32[]{:S(2)}, u32[]{:S(2)}) collective-permute-start(f32[2,2,128,128]{3,2,1,0:T(8,128)S(1)} %get-tuple-element.56), channel_id=1, source_target_pairs={{0,1},{1,0},{2,3},{3,2},{4,5},{5,4},{6,7},{7,6},{8,9},{9,8},{10,11... | collective-permute-start | bytes 786440 | tf_op jit(solution)/shard_map/ppermute | solution.py:489

commit v8 on v7

--- a/solution.py
+++ b/solution.py
@@ -266,7 +266,7 @@
         advance(*mixed, trail.at[slot + change], twiddle, stages)
         return unused
 
-    lax.fori_loop(0, count, one, 0)
+    lax.fori_loop(0, count, one, 0, unroll=2 if count % 2 == 0 else 3)
 
 
 def keep(chip, trail, saved):

time: 104 us -> 104 us (level)
  no operation moved by 1% of the time
where the time goes in v8:
time: 104 us
  starting transfers between devices  43.3 us (42%)
  waiting for transfers between devices  42.9 us (41%)
  Pallas kernels  11.8 us (11%)
  local copies, waits for them, and re-layouts  4.6 us (4%)
  between operations  1.48 us (1%)
    ppermute x6, starting transfers between devices, along_stages(): return lax.ppermute(value, 'depth', pairs)  20 us
    ppermute x6, waiting for transfers between devices, along_stages(): return lax.ppermute(value, 'depth', pairs)  19.4 us
    ppermute x4, starting transfers between devices, across(): return lax.ppermute(value, ('pos', 'depth'), pairs)  14 us
    ppermute x6, waiting for transfers between devices, along_ring(): return lax.ppermute(value, 'depth', pairs)  11.8 us
    ppermute x4, waiting for transfers between devices, across(): return lax.ppermute(value, ('pos', 'depth'), pairs)  10.3 us
    ppermute x6, starting transfers between devices, along_ring(): return lax.ppermute(value, 'depth', pairs)  7.03 us
    pallas_call x1, Pallas kernels, first_stage(): pl.pallas_call(first_kernel, out_shape=(WAVE, SAVED, STACK), in_specs=[VM...  3.87 us
    pallas_call x3, Pallas kernels, backward_stage(): pl.pallas_call(last_backward_kernel if last else functools.partial(backwa...  3.58 us
  transfers between devices with their start and end apart: 20, of which 14 were waited for; matrix products, arithmetic and copies ran while one was open for 1% of the time, Pallas kernels for 1%

profile of v8, /device:TPU:1, one launch (start us, length us, event | category | flops | bytes accessed | tf_op | source)
XLA Modules:
  0.0 104.3 jit_solution(3700894972540248990)
XLA Ops:
  0.7 2.0 %collective-permute-start = (s32[128,128]{1,0:T(8,128)S(1)}, s32[128,128]{1,0:T(8,128)S(1)}, u32[]{:S(2)}, u32[]{:S(2)}) collective-permute-start(s32[128,128]{1,0:T(8,128)S(1)} %pad.4), channel_id=1, source_target_pairs={{0,32},{32,64},{64,96},{96,0},{1,33},{33,65},{65,97},{97,1},{2,34}... | collective-permute-start | bytes 196616 | tf_op jit(solution)/shard_map/ppermute | solution.py:513
  2.7 0.9 copy-done.1
  3.6 1.2 %copy-done.3 = f32[2,2,128,512]{3,2,1,0:T(8,128)S(1)} copy-done((f32[2,2,128,512]{3,2,1,0:T(8,128)S(1)}, f32[2,2,128,512]{3,2,1,0:T(8,128)}, u32[]{:S(2)}) %copy-start.3) | copy-done | bytes 1048600
  6.4 0.9 cut_windows.1
  7.3 1.3 %collective-permute-start.1 = (f32[2,2,128,128]{3,2,1,0:T(8,128)S(1)}, f32[2,2,128,128]{3,2,1,0:T(8,128)S(1)}, u32[]{:S(2)}, u32[]{:S(2)}) collective-permute-start(f32[2,2,128,128]{3,2,1,0:T(8,128)S(1)} %get-tuple-element.35), channel_id=1, source_target_pairs={{0,96},{1,33},{2,98},{3,35},{4,100},{5,37},{6,102},{7,39},{8,104},... | collective-permute-start | bytes 786440 | tf_op jit(solution)/shard_map/ppermute | solution.py:504
  8.6 2.8 %collective-permute-start.3 = (f32[2,2,128,128]{3,2,1,0:T(8,128)S(1)}, f32[2,2,128,128]{3,2,1,0:T(8,128)S(1)}, u32[]{:S(2)}, u32[]{:S(2)}) collective-permute-start(f32[2,2,128,128]{3,2,1,0:T(8,128)S(1)} %get-tuple-element.36), channel_id=1, source_target_pairs={{0,33},{1,96},{2,35},{3,98},{4,37},{5,100},{6,39},{7,102},{8,41},{... | collective-permute-start | bytes 786440 | tf_op jit(solution)/shard_map/ppermute | solution.py:504
  13.8 0.9 collective-permute-done.1
  14.8 2.5 %collective-permute-done.3 = f32[2,2,128,128]{3,2,1,0:T(8,128)S(1)} collective-permute-done((f32[2,2,128,128]{3,2,1,0:T(8,128)S(1)}, f32[2,2,128,128]{3,2,1,0:T(8,128)S(1)}, u32[]{:S(2)}, u32[]{:S(2)}) %collective-permute-start.3) | collective-permute-done | bytes 262176 | tf_op jit(solution)/shard_map/ppermute | solution.py:504
  17.4 1.4 %collective-permute-start.6 = (f32[2,2,128,128]{3,2,1,0:T(8,128)S(1)}, f32[2,2,128,128]{3,2,1,0:T(8,128)S(1)}, u32[]{:S(2)}, u32[]{:S(2)}) collective-permute-start(f32[2,2,128,128]{3,2,1,0:T(8,128)S(1)} %pad_maximum_fusion.near0), channel_id=1, source_target_pairs={{0,2},{1,3},{2,4},{3,5},{4,6},{5,7},{6,0},{7,1},{8,10},{9,11},{10,... | collective-permute-start | bytes 786440 | tf_op jit(solution)/shard_map/ppermute | solution.py:478
  18.8 1.5 %collective-permute-start.5 = (f32[2,2,128,128]{3,2,1,0:T(8,128)S(1)}, f32[2,2,128,128]{3,2,1,0:T(8,128)S(1)}, u32[]{:S(2)}, u32[]{:S(2)}) collective-permute-start(f32[2,2,128,128]{3,2,1,0:T(8,128)S(1)} %pad_maximum_fusion.1.near1), channel_id=1, source_target_pairs={{0,6},{1,7},{2,0},{3,1},{4,2},{5,3},{6,4},{7,5},{8,14},{9,15},{10,... | collective-permute-start | bytes 786440 | tf_op jit(solution)/shard_map/ppermute | solution.py:478
  20.3 1.4 %collective-permute-start.4 = (f32[2,2,128,128]{3,2,1,0:T(8,128)S(1)}, f32[2,2,128,128]{3,2,1,0:T(8,128)S(1)}, u32[]{:S(2)}, u32[]{:S(2)}) collective-permute-start(f32[2,2,128,128]{3,2,1,0:T(8,128)S(1)} %pad_maximum_fusion.near0), channel_id=1, source_target_pairs={{0,6},{1,7},{2,0},{3,1},{4,2},{5,3},{6,4},{7,5},{8,14},{9,15},{10,... | collective-permute-start | bytes 786440 | tf_op jit(solution)/shard_map/ppermute | solution.py:478
  21.8 3.6 %collective-permute-done.6.down0 = f32[2,2,128,128]{3,2,1,0:T(8,128)S(1)} collective-permute-done((f32[2,2,128,128]{3,2,1,0:T(8,128)S(1)}, f32[2,2,128,128]{3,2,1,0:T(8,128)S(1)}, u32[]{:S(2)}, u32[]{:S(2)}) %collective-permute-start.6) | collective-permute-done | bytes 262176 | tf_op jit(solution)/shard_map/ppermute | solution.py:478
  25.3 2.7 %collective-permute-start.8 = (f32[2,2,128,128]{3,2,1,0:T(8,128)S(1)}, f32[2,2,128,128]{3,2,1,0:T(8,128)S(1)}, u32[]{:S(2)}, u32[]{:S(2)}) collective-permute-start(f32[2,2,128,128]{3,2,1,0:T(8,128)S(1)} %collective-permute-done.5.up1), channel_id=1, source_target_pairs={{0,6},{1,7},{2,0},{3,1},{4,2},{5,3},{6,4},{7,5},{8,14},{9,15},{10,... | collective-permute-start | bytes 786440 | tf_op jit(solution)/shard_map/ppermute | solution.py:478
  28.7 1.9 %collective-permute-done.4.up0 = f32[2,2,128,128]{3,2,1,0:T(8,128)S(1)} collective-permute-done((f32[2,2,128,128]{3,2,1,0:T(8,128)S(1)}, f32[2,2,128,128]{3,2,1,0:T(8,128)S(1)}, u32[]{:S(2)}, u32[]{:S(2)}) %collective-permute-start.4) | collective-permute-done | bytes 262176 | tf_op jit(solution)/shard_map/ppermute | solution.py:478
  31.3 5.6 %collective-permute-done.7.far0 = f32[2,2,128,128]{3,2,1,0:T(8,128)S(1)} collective-permute-done((f32[2,2,128,128]{3,2,1,0:T(8,128)S(1)}, f32[2,2,128,128]{3,2,1,0:T(8,128)S(1)}, u32[]{:S(2)}, u32[]{:S(2)}) %collective-permute-start.7) | collective-permute-done | bytes 262176 | tf_op jit(solution)/shard_map/ppermute | solution.py:478
  37.0 3.9 %first_stage.1 = (f32[2,128,128]{2,1,0:T(8,128)S(1)}, f32[4,2,128,128]{3,2,1,0:T(8,128)S(1)}, f32[16,2,128,128]{3,2,1,0:T(8,128)S(1)}) custom-call(f32[2,2,128,128]{3,2,1,0:T(8,128)S(1)} %pad_maximum_fusion.near0, f32[2,2,128,128]{3,2,1,0:T(8,128)S(1)} %pad_maximum_fusion.1.near1, f32[2,2,128,128]{3,2,1,0:T(8,128)S(1)} %collective-permute-done.4.up0, ...), custom_call_target="tpu_custom_call" | custom-call | tf_op jit(solution)/shard_map/first_stage/pallas_call | solution.py:430
  40.9 5.0 %collective-permute-done.10.wave = f32[2,128,128]{2,1,0:T(8,128)S(1)} collective-permute-done((f32[2,128,128]{2,1,0:T(8,128)S(1)}, f32[2,128,128]{2,1,0:T(8,128)S(1)}, u32[]{:S(2)}, u32[]{:S(2)}) %collective-permute-start.10) | collective-permute-done | bytes 131104 | tf_op jit(solution)/shard_map/ppermute | solution.py:484
  46.0 2.4 %collective-permute-start.11 = (f32[2,128,128]{2,1,0:T(8,128)S(1)}, f32[2,128,128]{2,1,0:T(8,128)S(1)}, u32[]{:S(2)}, u32[]{:S(2)}) collective-permute-start(f32[2,128,128]{2,1,0:T(8,128)S(1)} %get-tuple-element.41), channel_id=1, source_target_pairs={{0,8},{1,9},{2,10},{3,11},{4,12},{5,13},{6,14},{7,15},{8,16},{9,17... | collective-permute-start | bytes 393224 | tf_op jit(solution)/shard_map/ppermute | solution.py:484
  48.6 2.5 %collective-permute-done.11.wave = f32[2,128,128]{2,1,0:T(8,128)S(1)} collective-permute-done((f32[2,128,128]{2,1,0:T(8,128)S(1)}, f32[2,128,128]{2,1,0:T(8,128)S(1)}, u32[]{:S(2)}, u32[]{:S(2)}) %collective-permute-start.11) | collective-permute-done | bytes 131104 | tf_op jit(solution)/shard_map/ppermute | solution.py:484
  51.1 1.2 %collective-permute-start.12 = (f32[2,128,128]{2,1,0:T(8,128)S(1)}, f32[2,128,128]{2,1,0:T(8,128)S(1)}, u32[]{:S(2)}, u32[]{:S(2)}) collective-permute-start(f32[2,128,128]{2,1,0:T(8,128)S(1)} %get-tuple-element.43), channel_id=1, source_target_pairs={{0,8},{1,9},{2,10},{3,11},{4,12},{5,13},{6,14},{7,15},{8,16},{9,17... | collective-permute-start | bytes 393224 | tf_op jit(solution)/shard_map/ppermute | solution.py:484
  52.3 1.4 %collective-permute-done.13 = f32[2,128,128]{2,1,0:T(8,128)S(1)} collective-permute-done((f32[2,128,128]{2,1,0:T(8,128)S(1)}, f32[2,128,128]{2,1,0:T(8,128)S(1)}, u32[]{:S(2)}, u32[]{:S(2)}) %collective-permute-start.13) | collective-permute-done | bytes 131104 | tf_op jit(solution)/shard_map/ppermute | solution.py:547
  53.7 2.8 %collective-permute-done.12.wave = f32[2,128,128]{2,1,0:T(8,128)S(1)} collective-permute-done((f32[2,128,128]{2,1,0:T(8,128)S(1)}, f32[2,128,128]{2,1,0:T(8,128)S(1)}, u32[]{:S(2)}, u32[]{:S(2)}) %collective-permute-start.12) | collective-permute-done | bytes 131104 | tf_op jit(solution)/shard_map/ppermute | solution.py:484
  56.5 9.9 %collective-permute-start.14 = (f32[2,128,128]{2,1,0:T(8,128)S(1)}, f32[2,128,128]{2,1,0:T(8,128)S(1)}, u32[]{:S(2)}, u32[]{:S(2)}) collective-permute-start(f32[2,128,128]{2,1,0:T(8,128)S(1)} %get-tuple-element.45), channel_id=1, source_target_pairs={{0,24},{1,25},{2,26},{3,27},{4,28},{5,29},{6,30},{7,31},{8,0},{9,1... | collective-permute-start | bytes 393224 | tf_op jit(solution)/shard_map/ppermute | solution.py:484
  66.4 1.9 %collective-permute-done.14.wave = f32[2,128,128]{2,1,0:T(8,128)S(1)} collective-permute-done((f32[2,128,128]{2,1,0:T(8,128)S(1)}, f32[2,128,128]{2,1,0:T(8,128)S(1)}, u32[]{:S(2)}, u32[]{:S(2)}) %collective-permute-start.14) | collective-permute-done | bytes 131104 | tf_op jit(solution)/shard_map/ppermute | solution.py:484
  68.4 3.1 %collective-permute-start.15 = (f32[2,128,128]{2,1,0:T(8,128)S(1)}, f32[2,128,128]{2,1,0:T(8,128)S(1)}, u32[]{:S(2)}, u32[]{:S(2)}) collective-permute-start(f32[2,128,128]{2,1,0:T(8,128)S(1)} %get-tuple-element.49), channel_id=1, source_target_pairs={{0,24},{1,25},{2,26},{3,27},{4,28},{5,29},{6,30},{7,31},{8,0},{9,1... | collective-permute-start | bytes 393224 | tf_op jit(solution)/shard_map/ppermute | solution.py:484
  71.6 3.1 %collective-permute-done.15.wave = f32[2,128,128]{2,1,0:T(8,128)S(1)} collective-permute-done((f32[2,128,128]{2,1,0:T(8,128)S(1)}, f32[2,128,128]{2,1,0:T(8,128)S(1)}, u32[]{:S(2)}, u32[]{:S(2)}) %collective-permute-start.15) | collective-permute-done | bytes 131104 | tf_op jit(solution)/shard_map/ppermute | solution.py:484
  74.7 3.2 %collective-permute-start.16 = (f32[2,128,128]{2,1,0:T(8,128)S(1)}, f32[2,128,128]{2,1,0:T(8,128)S(1)}, u32[]{:S(2)}, u32[]{:S(2)}) collective-permute-start(f32[2,128,128]{2,1,0:T(8,128)S(1)} %get-tuple-element.52), channel_id=1, source_target_pairs={{0,24},{1,25},{2,26},{3,27},{4,28},{5,29},{6,30},{7,31},{8,0},{9,1... | collective-permute-start | bytes 393224 | tf_op jit(solution)/shard_map/ppermute | solution.py:484
  77.9 4.1 %collective-permute-done.16.wave = f32[2,128,128]{2,1,0:T(8,128)S(1)} collective-permute-done((f32[2,128,128]{2,1,0:T(8,128)S(1)}, f32[2,128,128]{2,1,0:T(8,128)S(1)}, u32[]{:S(2)}, u32[]{:S(2)}) %collective-permute-start.16) | collective-permute-done | bytes 131104 | tf_op jit(solution)/shard_map/ppermute | solution.py:484
  82.0 3.5 %backward_stage.5 = (f32[2,2,128,128]{3,2,1,0:T(8,128)S(1)}, f32[2,2,128,128]{3,2,1,0:T(8,128)S(1)}) custom-call(f32[16,2,128,128]{3,2,1,0:T(8,128)S(1)} %get-tuple-element.37.windows, f32[2,128,128]{2,1,0:T(8,128)S(1)} %collective-permute-done.16.wave, f32[4,2,128,128]{3,2,1,0:T(8,128)S(1)} %get-tuple-element.46.saved, f32[2,128,128]{2,1,0:T(8,128)S(1)} %copy-done, ...), custom_call_target="tpu_custom_call" | custom-call | tf_op jit(solution)/shard_map/backward_stage/pallas_call | solution.py:452
  86.0 9.6 %collective-permute-start.19 = (f32[2,2,128,128]{3,2,1,0:T(8,128)S(1)}, f32[2,2,128,128]{3,2,1,0:T(8,128)S(1)}, u32[]{:S(2)}, u32[]{:S(2)}) collective-permute-start(f32[2,2,128,128]{3,2,1,0:T(8,128)S(1)} %get-tuple-element.56), channel_id=1, source_target_pairs={{0,33},{1,96},{2,35},{3,98},{4,37},{5,100},{6,39},{7,102},{8,41},{... | collective-permute-start | bytes 786440 | tf_op jit(solution)/shard_map/ppermute | solution.py:504
  95.5 6.9 %collective-permute-done.19.moved_other = f32[2,2,128,128]{3,2,1,0:T(8,128)S(1)} collective-permute-done((f32[2,2,128,128]{3,2,1,0:T(8,128)S(1)}, f32[2,2,128,128]{3,2,1,0:T(8,128)S(1)}, u32[]{:S(2)}, u32[]{:S(2)}) %collective-permute-start.19) | collective-permute-done | bytes 262176 | tf_op jit(solution)/shard_map/ppermute | solution.py:504
  102.4 1.9 %paste_windows.1 = f32[2,2,128,512]{3,2,1,0:T(8,128)} custom-call(s32[4,2]{1,0:T(4,128)S(1)} %pad_add_fusion.corners, f32[2,2,128,128]{3,2,1,0:T(8,128)S(1)} %get-tuple-element.55.same, f32[2,2,128,128]{3,2,1,0:T(8,128)S(1)} %collective-permute-done.17.other, f32[2,2,128,128]{3,2,1,0:T(8,128)S(1)} %collective-permute-done.18.moved_same, ...), custom_call_target="tpu_custom_call" | custom-call | tf_op jit(solution)/shard_map/paste_windows/pallas_call | solution.py:250
  (44 shorter events, 5.7 us)
Async XLA Ops:
  0.7 5.0 %collective-permute-start = (s32[128,128]{1,0:T(8,128)S(1)}, s32[128,128]{1,0:T(8,128)S(1)}, u32[]{:S(2)}, u32[]{:S(2)}) collective-permute-start(s32[128,128]{1,0:T(8,128)S(1)} %pad.4), channel_id=1, source_target_pairs={{0,32},{32,64},{64,96},{96,0},{1,33},{33,65},{65,97},{97,1},{2,34}... | collective-permute-start | bytes 196616 | tf_op jit(solution)/shard_map/ppermute | solution.py:513
  2.7 0.9 copy-start.1
  3.6 1.2 %copy-start.3 = (f32[2,2,128,512]{3,2,1,0:T(8,128)S(1)}, f32[2,2,128,512]{3,2,1,0:T(8,128)}, u32[]{:S(2)}) copy-start(f32[2,2,128,512]{3,2,1,0:T(8,128)} %field.1) | copy-start | bytes 3145732
  4.9 0.7 copy-start.5
  6.4 21.6 %copy-start.2 = (f32[2,128,128]{2,1,0:T(8,128)S(1)}, f32[2,128,128]{2,1,0:T(8,128)}, u32[]{:S(2)}) copy-start(f32[2,128,128]{2,1,0:T(8,128)} %constant.33.clone.chirp) | copy-start | bytes 393220
  6.4 21.6 %copy-start.4 = (f32[2,128,128]{2,1,0:T(8,128)S(1)}, f32[2,128,128]{2,1,0:T(8,128)}, u32[]{:S(2)}) copy-start(f32[2,128,128]{2,1,0:T(8,128)} %probe.1) | copy-start | bytes 393220
  6.4 30.5 %copy-start = (f32[2,128,128]{2,1,0:T(8,128)S(1)}, f32[2,128,128]{2,1,0:T(8,128)}, u32[]{:S(2)}) copy-start(f32[2,128,128]{2,1,0:T(8,128)} %constant.32.clone.twiddle) | copy-start | bytes 393220
  7.3 7.5 %collective-permute-start.1 = (f32[2,2,128,128]{3,2,1,0:T(8,128)S(1)}, f32[2,2,128,128]{3,2,1,0:T(8,128)S(1)}, u32[]{:S(2)}, u32[]{:S(2)}) collective-permute-start(f32[2,2,128,128]{3,2,1,0:T(8,128)S(1)} %get-tuple-element.35), channel_id=1, source_target_pairs={{0,96},{1,33},{2,98},{3,35},{4,100},{5,37},{6,102},{7,39},{8,104},... | collective-permute-start | bytes 786440 | tf_op jit(solution)/shard_map/ppermute | solution.py:504
  8.6 8.7 %collective-permute-start.3 = (f32[2,2,128,128]{3,2,1,0:T(8,128)S(1)}, f32[2,2,128,128]{3,2,1,0:T(8,128)S(1)}, u32[]{:S(2)}, u32[]{:S(2)}) collective-permute-start(f32[2,2,128,128]{3,2,1,0:T(8,128)S(1)} %get-tuple-element.36), channel_id=1, source_target_pairs={{0,33},{1,96},{2,35},{3,98},{4,37},{5,100},{6,39},{7,102},{8,41},{... | collective-permute-start | bytes 786440 | tf_op jit(solution)/shard_map/ppermute | solution.py:504
  11.4 5.9 %collective-permute-start.2 = (f32[2,2,128,128]{3,2,1,0:T(8,128)S(1)}, f32[2,2,128,128]{3,2,1,0:T(8,128)S(1)}, u32[]{:S(2)}, u32[]{:S(2)}) collective-permute-start(f32[2,2,128,128]{3,2,1,0:T(8,128)S(1)} %cut_other.1), channel_id=1, source_target_pairs={{0,1},{1,0},{2,3},{3,2},{4,5},{5,4},{6,7},{7,6},{8,9},{9,8},{10,11... | collective-permute-start | bytes 786440 | tf_op jit(solution)/shard_map/ppermute | solution.py:489
  17.4 8.0 %collective-permute-start.6 = (f32[2,2,128,128]{3,2,1,0:T(8,128)S(1)}, f32[2,2,128,128]{3,2,1,0:T(8,128)S(1)}, u32[]{:S(2)}, u32[]{:S(2)}) collective-permute-start(f32[2,2,128,128]{3,2,1,0:T(8,128)S(1)} %pad_maximum_fusion.near0), channel_id=1, source_target_pairs={{0,2},{1,3},{2,4},{3,5},{4,6},{5,7},{6,0},{7,1},{8,10},{9,11},{10,... | collective-permute-start | bytes 786440 | tf_op jit(solution)/shard_map/ppermute | solution.py:478
  18.8 6.6 %collective-permute-start.5 = (f32[2,2,128,128]{3,2,1,0:T(8,128)S(1)}, f32[2,2,128,128]{3,2,1,0:T(8,128)S(1)}, u32[]{:S(2)}, u32[]{:S(2)}) collective-permute-start(f32[2,2,128,128]{3,2,1,0:T(8,128)S(1)} %pad_maximum_fusion.1.near1), channel_id=1, source_target_pairs={{0,6},{1,7},{2,0},{3,1},{4,2},{5,3},{6,4},{7,5},{8,14},{9,15},{10,... | collective-permute-start | bytes 786440 | tf_op jit(solution)/shard_map/ppermute | solution.py:478
  20.3 10.3 %collective-permute-start.4 = (f32[2,2,128,128]{3,2,1,0:T(8,128)S(1)}, f32[2,2,128,128]{3,2,1,0:T(8,128)S(1)}, u32[]{:S(2)}, u32[]{:S(2)}) collective-permute-start(f32[2,2,128,128]{3,2,1,0:T(8,128)S(1)} %pad_maximum_fusion.near0), channel_id=1, source_target_pairs={{0,6},{1,7},{2,0},{3,1},{4,2},{5,3},{6,4},{7,5},{8,14},{9,15},{10,... | collective-permute-start | bytes 786440 | tf_op jit(solution)/shard_map/ppermute | solution.py:478
  21.7 9.6 %collective-permute-start.9 = (f32[2,2,128,128]{3,2,1,0:T(8,128)S(1)}, f32[2,2,128,128]{3,2,1,0:T(8,128)S(1)}, u32[]{:S(2)}, u32[]{:S(2)}) collective-permute-start(f32[2,2,128,128]{3,2,1,0:T(8,128)S(1)} %pad_maximum_fusion.1.near1), channel_id=1, source_target_pairs={{0,2},{1,3},{2,4},{3,5},{4,6},{5,7},{6,0},{7,1},{8,10},{9,11},{10,... | collective-permute-start | bytes 786440 | tf_op jit(solution)/shard_map/ppermute | solution.py:478
  25.3 11.6 %collective-permute-start.7 = (f32[2,2,128,128]{3,2,1,0:T(8,128)S(1)}, f32[2,2,128,128]{3,2,1,0:T(8,128)S(1)}, u32[]{:S(2)}, u32[]{:S(2)}) collective-permute-start(f32[2,2,128,128]{3,2,1,0:T(8,128)S(1)} %collective-permute-done.6.down0), channel_id=1, source_target_pairs={{0,2},{1,3},{2,4},{3,5},{4,6},{5,7},{6,0},{7,1},{8,10},{9,11},{10,... | collective-permute-start | bytes 786440 | tf_op jit(solution)/shard_map/ppermute | solution.py:478
  25.3 11.6 %collective-permute-start.8 = (f32[2,2,128,128]{3,2,1,0:T(8,128)S(1)}, f32[2,2,128,128]{3,2,1,0:T(8,128)S(1)}, u32[]{:S(2)}, u32[]{:S(2)}) collective-permute-start(f32[2,2,128,128]{3,2,1,0:T(8,128)S(1)} %collective-permute-done.5.up1), channel_id=1, source_target_pairs={{0,6},{1,7},{2,0},{3,1},{4,2},{5,3},{6,4},{7,5},{8,14},{9,15},{10,... | collective-permute-start | bytes 786440 | tf_op jit(solution)/shard_map/ppermute | solution.py:478
  28.7 19.7 %copy-start.6 = (f32[2,128,128]{2,1,0:T(8,128)S(1)}, f32[2,128,128]{2,1,0:T(8,128)}, u32[]{:S(2)}) copy-start(f32[2,128,128]{2,1,0:T(8,128)} %param.9) | copy-start | bytes 393220
  40.8 5.1 %collective-permute-start.10 = (f32[2,128,128]{2,1,0:T(8,128)S(1)}, f32[2,128,128]{2,1,0:T(8,128)S(1)}, u32[]{:S(2)}, u32[]{:S(2)}) collective-permute-start(f32[2,128,128]{2,1,0:T(8,128)S(1)} %get-tuple-element.39), channel_id=1, source_target_pairs={{0,8},{1,9},{2,10},{3,11},{4,12},{5,13},{6,14},{7,15},{8,16},{9,17... | collective-permute-start | bytes 393224 | tf_op jit(solution)/shard_map/ppermute | solution.py:484
  46.0 5.1 %collective-permute-start.11 = (f32[2,128,128]{2,1,0:T(8,128)S(1)}, f32[2,128,128]{2,1,0:T(8,128)S(1)}, u32[]{:S(2)}, u32[]{:S(2)}) collective-permute-start(f32[2,128,128]{2,1,0:T(8,128)S(1)} %get-tuple-element.41), channel_id=1, source_target_pairs={{0,8},{1,9},{2,10},{3,11},{4,12},{5,13},{6,14},{7,15},{8,16},{9,17... | collective-permute-start | bytes 393224 | tf_op jit(solution)/shard_map/ppermute | solution.py:484
  48.4 5.3 %collective-permute-start.13 = (f32[2,128,128]{2,1,0:T(8,128)S(1)}, f32[2,128,128]{2,1,0:T(8,128)S(1)}, u32[]{:S(2)}, u32[]{:S(2)}) collective-permute-start(f32[2,128,128]{2,1,0:T(8,128)S(1)} %copy-done.6), channel_id=1, source_target_pairs={{0,32},{32,64},{64,96},{96,0},{1,33},{33,65},{65,97},{97,1},{2,34}... | collective-permute-start | bytes 393224 | tf_op jit(solution)/shard_map/ppermute | solution.py:547
  51.1 5.4 %collective-permute-start.12 = (f32[2,128,128]{2,1,0:T(8,128)S(1)}, f32[2,128,128]{2,1,0:T(8,128)S(1)}, u32[]{:S(2)}, u32[]{:S(2)}) collective-permute-start(f32[2,128,128]{2,1,0:T(8,128)S(1)} %get-tuple-element.43), channel_id=1, source_target_pairs={{0,8},{1,9},{2,10},{3,11},{4,12},{5,13},{6,14},{7,15},{8,16},{9,17... | collective-permute-start | bytes 393224 | tf_op jit(solution)/shard_map/ppermute | solution.py:484
  56.5 11.9 %collective-permute-start.14 = (f32[2,128,128]{2,1,0:T(8,128)S(1)}, f32[2,128,128]{2,1,0:T(8,128)S(1)}, u32[]{:S(2)}, u32[]{:S(2)}) collective-permute-start(f32[2,128,128]{2,1,0:T(8,128)S(1)} %get-tuple-element.45), channel_id=1, source_target_pairs={{0,24},{1,25},{2,26},{3,27},{4,28},{5,29},{6,30},{7,31},{8,0},{9,1... | collective-permute-start | bytes 393224 | tf_op jit(solution)/shard_map/ppermute | solution.py:484
  68.4 6.2 %collective-permute-start.15 = (f32[2,128,128]{2,1,0:T(8,128)S(1)}, f32[2,128,128]{2,1,0:T(8,128)S(1)}, u32[]{:S(2)}, u32[]{:S(2)}) collective-permute-start(f32[2,128,128]{2,1,0:T(8,128)S(1)} %get-tuple-element.49), channel_id=1, source_target_pairs={{0,24},{1,25},{2,26},{3,27},{4,28},{5,29},{6,30},{7,31},{8,0},{9,1... | collective-permute-start | bytes 393224 | tf_op jit(solution)/shard_map/ppermute | solution.py:484
  74.7 7.4 %collective-permute-start.16 = (f32[2,128,128]{2,1,0:T(8,128)S(1)}, f32[2,128,128]{2,1,0:T(8,128)S(1)}, u32[]{:S(2)}, u32[]{:S(2)}) collective-permute-start(f32[2,128,128]{2,1,0:T(8,128)S(1)} %get-tuple-element.52), channel_id=1, source_target_pairs={{0,24},{1,25},{2,26},{3,27},{4,28},{5,29},{6,30},{7,31},{8,0},{9,1... | collective-permute-start | bytes 393224 | tf_op jit(solution)/shard_map/ppermute | solution.py:484
  85.6 10.0 %collective-permute-start.18 = (f32[2,2,128,128]{3,2,1,0:T(8,128)S(1)}, f32[2,2,128,128]{3,2,1,0:T(8,128)S(1)}, u32[]{:S(2)}, u32[]{:S(2)}) collective-permute-start(f32[2,2,128,128]{3,2,1,0:T(8,128)S(1)} %get-tuple-element.55.same), channel_id=1, source_target_pairs={{0,32},{1,97},{2,34},{3,99},{4,36},{5,101},{6,38},{7,103},{8,40},{... | collective-permute-start | bytes 786440 | tf_op jit(solution)/shard_map/ppermute | solution.py:504
  86.0 16.4 %collective-permute-start.19 = (f32[2,2,128,128]{3,2,1,0:T(8,128)S(1)}, f32[2,2,128,128]{3,2,1,0:T(8,128)S(1)}, u32[]{:S(2)}, u32[]{:S(2)}) collective-permute-start(f32[2,2,128,128]{3,2,1,0:T(8,128)S(1)} %get-tuple-element.56), channel_id=1, source_target_pairs={{0,33},{1,96},{2,35},{3,98},{4,37},{5,100},{6,39},{7,102},{8,41},{... | collective-permute-start | bytes 786440 | tf_op jit(solution)/shard_map/ppermute | solution.py:504
  95.5 6.9 %collective-permute-start.17 = (f32[2,2,128,128]{3,2,1,0:T(8,128)S(1)}, f32[2,2,128,128]{3,2,1,0:T(8,128)S(1)}, u32[]{:S(2)}, u32[]{:S(2)}) collective-permute-start(f32[2,2,128,128]{3,2,1,0:T(8,128)S(1)} %get-tuple-element.56), channel_id=1, source_target_pairs={{0,1},{1,0},{2,3},{3,2},{4,5},{5,4},{6,7},{7,6},{8,9},{9,8},{10,11... | collective-permute-start | bytes 786440 | tf_op jit(solution)/shard_map/ppermute | solution.py:489
